TPU v7x, 128 devices: a whole 4x4x4 slice. The times are simulated.
128 devices in a mesh: wide: 16 (over x_hi, z, core), narrow: 8 (over y, x_lo).
Axes of the slice: x: 4 (x_hi: 2, x_lo: 2; x = x_hi * 2 + x_lo), y: 4, z: 4, core: 2. Of those that a mesh axis runs over, the one named last changes fastest.
Arguments:
- replica_grads: bfloat16 [128, 16, 512, 512], P(('wide', 'narrow')), may hold values from -0.0625 to 0.0625
- owner_table: int32 [16], replicated, may hold values from 0 to 15, as said below
- left_stat: float32 [16, 512, 512], P('wide'), may hold values from -1 to 5, as said below
- right_stat: float32 [16, 512, 512], P('wide'), may hold values from -1 to 5, as said below
- left_root: float32 [16, 512, 512], P('wide'), may hold values from -1 to 2, as said below
- right_root: float32 [16, 512, 512], P('wide'), may hold values from -1 to 2, as said below
Outputs:
- directions: float32 [16, 512, 512], P(None, 'narrow')
- left_new: float32 [16, 512, 512], P('wide')
- right_new: float32 [16, 512, 512], P('wide')
- left_inverse: float32 [16, 512, 512], P('wide')
- right_inverse: float32 [16, 512, 512], P('wide')
Inputs may be any that keep to these rules, and one draw needn't show every extreme that they name: `owner_table`: the 16 entries are distinct, so every slot is named once. `left_stat`: each slot's matrix is symmetric positive definite. `right_stat`: each slot's matrix is symmetric positive definite. `left_root`: each slot's matrix is symmetric. `right_root`: each slot's matrix is symmetric.
All inputs are finite; a program needn't handle non-finite values.
Results may differ from a plain program's by a relative error of at most 0.0003.
Values sent between devices are 32-bit elements; how exact they have to be, the bound alone decides.
No kernel may reach another device: no remote copies, remote signals or barrier semaphores. Data moves between devices by JAX's collectives and lax.ppermute only.
A program may use at most 128 MiB of HBM per device.

v0:
```python
import jax
import jax.numpy as jnp
from jax import lax
from jax.sharding import PartitionSpec as P

decay_rate = 0.95


def matmul_high(first, second):
    return jnp.dot(
        first, second, precision=lax.Precision.HIGHEST, preferred_element_type=jnp.float32
    )


def gram_right(matrix):
    return lax.dot_general(
        matrix,
        matrix,
        (((0,), (0,)), ((), ())),
        precision=lax.Precision.HIGHEST,
        preferred_element_type=jnp.float32,
    )


def finish_newton(old_root, fourth_power, statistic):
    coupled = matmul_high(fourth_power, statistic)
    return (5.0 * old_root - matmul_high(old_root, coupled)) / 4.0


def local(replica_grads, owner_table, left_stat, right_stat, left_root, right_root):
    owners = lax.axis_size("wide")
    local_grads = replica_grads[0]
    order = local_grads.shape[1]
    selector = (owner_table[None, :] == jnp.arange(owners)[:, None]).astype(jnp.bfloat16)
    slot_grads = jnp.einsum(
        "wb,bij->wij", selector, local_grads, preferred_element_type=jnp.float32
    )
    left_prev = left_root[0]
    right_prev = right_root[0]
    left_squared = matmul_high(left_prev, left_prev)
    left_fourth = matmul_high(left_squared, left_squared)
    right_squared = matmul_high(right_prev, right_prev)
    right_fourth = matmul_high(right_squared, right_squared)
    partial_sum = lax.psum_scatter(slot_grads, "wide", scatter_dimension=0, tiled=True)[0]
    summed = lax.psum(partial_sum, "narrow")
    left_value = decay_rate * left_stat[0] + (1.0 - decay_rate) * matmul_high(summed, summed.T)
    right_value = decay_rate * right_stat[0] + (1.0 - decay_rate) * gram_right(summed)
    left_next = finish_newton(left_prev, left_fourth, left_value)
    right_next = finish_newton(right_prev, right_fourth, right_value)
    preconditioned = matmul_high(matmul_high(left_next, summed), right_next)
    piece_rows = order // lax.axis_size("narrow")
    row_start = lax.axis_index("narrow") * piece_rows
    own_rows = lax.dynamic_slice_in_dim(preconditioned, row_start, piece_rows, 0)
    gathered = lax.all_gather(own_rows[None], "wide", axis=0, tiled=True)
    directions = jnp.take(gathered, owner_table, axis=0)
    return (directions, left_value[None], right_value[None], left_next[None], right_next[None])


def solution(mesh):
    placed = (
        P(("wide", "narrow"), None, None, None),
        P(),
        P("wide", None, None),
        P("wide", None, None),
        P("wide", None, None),
        P("wide", None, None),
    )
    return jax.shard_map(
        local,
        mesh=mesh,
        in_specs=placed,
        out_specs=(
            P(None, "narrow", None),
            P("wide", None, None),
            P("wide", None, None),
            P("wide", None, None),
            P("wide", None, None),
        ),
        check_vma=False,
    )
```

profile of v0, /device:TPU:1, one launch (start us, length us, event | category | flops | bytes accessed | tf_op | source)
XLA Modules:
  0.0 346.2 jit_solution(1236870905349722525)
XLA Ops:
  7.2 0.0 reduce-scatter.2.cloned.1.call-start
  7.2 8.4 %fusion = f32[16,512,512]{2,0,1:T(8,128)S(1)} fusion(bf16[16,512,512]{2,1,0:T(8,128)(2,1)} %bitcast.68, s32[16]{0:T(128)} %param.7), kind=kOutput, calls=%fused_computation.1 | convolution fusion | flops 134217984 | bytes 25165888 | tf_op jit(solution)/shard_map/wb,bij->wij/dot_general | solution.py:35
  15.6 19.1 %copy.23 = f32[16,512,512]{2,1,0:T(8,128)} copy(f32[16,512,512]{2,0,1:T(8,128)S(1)} %fusion) | data formatting | bytes 33554432 | tf_op jit(solution)/shard_map/wb,bij->wij/dot_general | solution.py:35
  34.7 0.0 reduce-scatter.2.cloned.1.call-update
  34.8 0.0 copy-start.2
  34.8 0.0 all-reduce.2.cloned.1.call-start
  34.8 1.1 copy-done.1
  36.0 1.3 copy.21
  37.3 0.0 copy-done.2
  37.3 1.3 copy.24
  38.6 146.1 %reduce-scatter.2.cloned.1.call-done = f32[1,512,512]{2,1,0:T(8,128)} async-done(((f32[16,512,512]{2,1,0:T(8,128)}), f32[1,512,512]{2,1,0:T(8,128)}) %reduce-scatter.2.cloned.1.call-update) | async-done | bytes 1048592 | tf_op jit(solution)/shard_map/reduce_scatter | solution.py:44
  184.7 0.0 all-reduce.2.cloned.1.call-update
  184.7 0.2 all-gather.3.cloned.1.call-start
  184.9 1.8 fusion.12
  186.8 1.8 fusion.9
  188.6 1.8 fusion.17
  190.5 2.8 fusion.20
  193.3 68.5 %all-reduce.2.cloned.1.call-done = f32[512,512]{1,0:T(8,128)} async-done(((f32[512,512]{1,0:T(8,128)}), f32[512,512]{1,0:T(8,128)}) %all-reduce.2.cloned.1.call-update) | async-done | bytes 1048592 | tf_op jit(solution)/shard_map/psum | solution.py:45
  261.8 3.7 %fusion.7 = f32[512,512]{1,0:T(8,128)S(1)} fusion(f32[512,512]{1,0:T(8,128)} %all-reduce.2.cloned.1.call-done, f32[1,512,512]{2,1,0:T(8,128)} %param.8), kind=kOutput, calls=%fused_computation.12 | convolution fusion | flops 1611399168 | bytes 3145728 | tf_op jit(solution)/shard_map/dot_general | solution.py:10
  265.5 0.0 copy-start.4
  265.5 1.0 copy-done.4
  266.5 1.8 fusion.18
  268.3 0.0 copy-done.7
  268.3 0.0 copy-start
  268.4 0.0 copy-start.8
  268.4 3.7 %fusion.6 = f32[512,512]{0,1:T(8,128)S(1)} fusion(f32[512,512]{1,0:T(8,128)S(1)} %fusion.18, f32[1,512,512]{2,1,0:T(8,128)S(1)} %copy-done.1, f32[1,512,512]{1,2,0:T(8,128)S(1)} %copy-done.7), kind=kOutput, calls=%fused_computation.10 | convolution fusion | flops 1611399168 | bytes 4194304 | tf_op jit(solution)/shard_map/dot_general | solution.py:10
  272.1 0.0 copy-done
  272.1 0.0 copy-done.8
  272.1 0.0 copy-start.3
  272.1 1.9 fusion.4
  274.0 0.0 copy-done.3
  274.0 0.0 copy-start.5
  274.0 0.0 copy-start.6
  274.0 1.8 fusion.21
  275.9 0.0 copy-done.6
  275.9 3.5 %fusion.3 = f32[512,512]{0,1:T(8,128)S(1)} fusion(f32[512,512]{1,0:T(8,128)S(1)} %fusion.21, f32[1,512,512]{2,1,0:T(8,128)S(1)} %copy-done.2, f32[1,512,512]{1,2,0:T(8,128)S(1)} %copy-done.6), kind=kOutput, calls=%fused_computation.5 | convolution fusion | flops 1611399168 | bytes 4194304 | tf_op jit(solution)/shard_map/dot_general | solution.py:10
  279.4 0.0 copy-done.5
  279.4 1.8 fusion.19
  281.3 0.0 copy-start.9
  281.3 1.9 fusion.22
  283.2 0.7 constant_dynamic-slice_fusion
  283.8 0.0 all-gather.3.cloned.1.call-update
  283.8 0.0 copy-done.9
  283.9 1.3 copy.25
  285.2 1.3 copy.26
  286.5 49.1 %all-gather.3.cloned.1.call-done = f32[1024,512]{1,0:T(8,128)} async-done(((f32[64,512]{1,0:T(8,128)}), f32[1024,512]{1,0:T(8,128)}) %all-gather.3.cloned.1.call-update) | async-done | bytes 2097168 | tf_op jit(solution)/shard_map/all_gather | solution.py:54
  335.6 2.3 gather_fusion
  337.9 1.7 broadcast_select_fusion
  (5 shorter events, 0.0 us)
Async XLA Ops:
  7.2 177.5 %reduce-scatter.2.cloned.1.call-start = ((), (), s32[]{:S(2)}) async-start(), calls=%async_computation.1 | async-start | bytes 17825792 | tf_op jit(solution)/shard_map/reduce_scatter | solution.py:44
  34.7 1.2 copy-start.1
  34.8 2.5 copy-start.2
  34.8 227.0 %all-reduce.2.cloned.1.call-start = ((), (), s32[]{:S(2)}) async-start(), calls=%async_computation.2 | async-start | bytes 2097152 | tf_op jit(solution)/shard_map/psum | solution.py:45
  184.7 150.9 %all-gather.3.cloned.1.call-start = ((), (), s32[]{:S(2)}) async-start(), calls=%async_computation.3 | async-start | bytes 2228224 | tf_op jit(solution)/shard_map/all_gather | solution.py:54
  265.5 1.0 copy-start.4
  266.5 1.9 copy-start.7
  268.3 3.7 %copy-start = (f32[512,512]{1,0:T(8,128)S(1)}, f32[512,512]{1,0:T(8,128)}, u32[]{:S(2)}) copy-start(f32[512,512]{1,0:T(8,128)} %all-reduce.2.cloned.1.call-done) | copy-start | bytes 3145732
  268.4 3.7 %copy-start.8 = (f32[1,512,512]{2,1,0:T(8,128)S(1)}, f32[1,512,512]{2,1,0:T(8,128)}, u32[]{:S(2)}) copy-start(f32[1,512,512]{2,1,0:T(8,128)} %param.9) | copy-start | bytes 3145732
  272.1 1.9 copy-start.3
  274.0 5.4 %copy-start.5 = (f32[512,512]{1,0:T(8,128)}, f32[512,512]{1,0:T(8,128)S(1)}, u32[]{:S(2)}) copy-start(f32[512,512]{1,0:T(8,128)S(1)} %fusion.4) | copy-start | bytes 3145732
  274.0 1.9 copy-start.6
  281.3 2.6 copy-start.9
Sparse Core Ops, SparseCore 0:
  34.9 149.7 reduce-scatter.1
  187.2 74.5 all-reduce.1
  284.0 51.5 all-gather.2
where the time goes:
time: 346 us
  waiting for transfers between devices  264 us (76%)
  matrix products  37 us (11%)
  local copies, waits for them, and re-layouts  29.4 us (8%)
  between operations  14 us (4%)
    reduce_scatter x1, waiting for transfers between devices, local(): lax.psum_scatter(slot_grads, 'wide', scatter_dimension=0, tiled=True)[0]  146 us
    psum x1, waiting for transfers between devices, local(): summed = lax.psum(partial_sum, 'narrow')  68.5 us
    all_gather x1, waiting for transfers between devices, local(): gathered = lax.all_gather(own_rows[None], 'wide', axis=0, tiled=True)  49.1 us
    dot_general x11, matrix products, matmul_high(): jnp.dot(first, second, precision=lax.Precision.HIGHEST, preferred_element...  26.7 us
    dot_general x1, local copies, waits for them, and re-layouts, local(): jnp.einsum('wb,bij->wij', selector, local_grads, preferred_element_type=j...  19.1 us
    dot_general x1, matrix products, local(): jnp.einsum('wb,bij->wij', selector, local_grads, preferred_element_type=j...  8.42 us
    unnamed x24, local copies, waits for them, and re-layouts  7.37 us
  transfers between devices with their start and end apart: 3, of which 3 were waited for; matrix products, arithmetic and copies ran while one was open for 4% of the time, Pallas kernels for 0%

commit v1 on v0

v1 whole, which is shorter than its diff:
```python
import functools

import jax
import jax.numpy as jnp
from jax import lax
from jax.experimental import pallas as pl
from jax.experimental.pallas import tpu as pltpu
from jax.sharding import Mesh, PartitionSpec as P

AXES = ("xh", "z", "core", "y", "xl")
SIZES = (2, 4, 2, 4, 2)
DECAY = 0.95
ORDER = 512
ROWS = 64
VMEM_LIMIT = 48 * 1024 * 1024
STREAM_PAIRS = (tuple(range(0, 6)), tuple(range(6, 11)), tuple(range(11, 16)))


def index_of(x, y, z, c):
    return ((((x >> 1) * 4 + z) * 2 + c) * 4 + y) * 2 + (x & 1)


def permutation(move):
    return [
        (index_of(x, y, z, c), index_of(*move(x, y, z, c)))
        for x in range(4)
        for y in range(4)
        for z in range(4)
        for c in range(2)
    ]


def axis_move(axis, masks):
    def move(x, y, z, c):
        place = [x, y, z]
        place[axis] ^= masks[c]
        return (*place, c)

    return permutation(move)


CORE_SWAP = permutation(lambda x, y, z, c: (x, y, z, 1 - c))


def send(value, pairs):
    return lax.ppermute(value, AXES, pairs)


def place():
    xl = lax.axis_index("xl")
    x = lax.axis_index("xh") * 2 + xl
    return x, lax.axis_index("y"), lax.axis_index("z"), lax.axis_index("core")


def split(value):
    high = value.astype(jnp.bfloat16)
    low = (value - high.astype(jnp.float32)).astype(jnp.bfloat16)
    return high, low


def product(first, second, dims=((1,), (0,))):
    fh, fl = first
    sh, sl = second

    def dot(a, b):
        return lax.dot_general(a, b, (dims, ((), ())), preferred_element_type=jnp.float32)

    return dot(fh, sh) + (dot(fh, sl) + dot(fl, sh))


NT = ((1,), (1,))
TN = ((0,), (0,))


def fill_inverse(owner_ref, inverse_ref):
    for b in range(16):
        inverse_ref[owner_ref[b]] = b


def pack_kernel(own, parts, scalars_ref, owner_ref, grads_ref, *rest):
    outs = rest[: len(parts)]
    blocks, inverse, sems = rest[len(parts) :]
    x, y, z, c = (scalars_ref[i] for i in range(4))
    target = c if own else 1 - c
    fill_inverse(owner_ref, inverse)

    def fetch(g):
        return pltpu.make_async_copy(
            grads_ref.at[0, inverse[g * 2 + target]], blocks.at[g], sems.at[g]
        )

    for g in range(8):
        fetch(g).start()
    for g in range(8):
        fetch(g).wait()
    p1 = 1 + 2 * target
    p2 = 3 - 2 * target
    for (stream, half), out in zip(parts, outs):

        def body(k, carry, stream=stream, half=half, out=out):
            bits = [(k >> s) & 1 for s in (4, 3, 2, 1, 0)]
            steps = [
                (half * p1) ^ (bits[0] * p2),
                (bits[1] * p1) ^ (bits[2] * p2),
                (bits[3] * p1) ^ (bits[4] * p2),
            ]
            moved = [x, y, z]
            for i in range(3):
                moved[(stream + i) % 3] = moved[(stream + i) % 3] ^ steps[i]
            xd, yd, zd = moved
            g = (xd >> 1) * 4 + zd
            row = (yd * 2 + (xd & 1)) * ROWS
            for i, pair in enumerate(STREAM_PAIRS[stream]):
                start = pl.multiple_of(row + (pair // 4) * 16, 16)
                col = (pair % 4) * 128
                value = blocks[g, pl.ds(start, 16), col : col + 128]
                out[k, 2 * i : 2 * i + 2] = value.astype(jnp.float32).reshape(2, 8, 128)
            return carry

        lax.fori_loop(0, 32, body, 0, unroll=2)


def pack(own, parts, scalars, owner_table, grads):
    smem = pl.BlockSpec(memory_space=pltpu.SMEM)
    vmem = pl.BlockSpec(memory_space=pltpu.VMEM)
    return pl.pallas_call(
        functools.partial(pack_kernel, own, parts),
        out_shape=[
            jax.ShapeDtypeStruct((32, 2 * len(STREAM_PAIRS[s]), 8, 128), jnp.float32)
            for s, _ in parts
        ],
        in_specs=[smem, smem, pl.BlockSpec(memory_space=pl.ANY)],
        out_specs=[vmem] * len(parts),
        scratch_shapes=[
            pltpu.VMEM((8, ORDER, ORDER), jnp.bfloat16),
            pltpu.SMEM((16,), jnp.int32),
            pltpu.SemaphoreType.DMA((8,)),
        ],
        compiler_params=pltpu.CompilerParams(vmem_limit_bytes=VMEM_LIMIT),
        name="pack_own" if own else "pack_other",
    )(scalars, owner_table, grads)


def roots_kernel(ls_ref, rs_ref, lr_ref, rr_ref, lc_ref, lk_ref, rc_ref, rk_ref):
    for stat_ref, root_ref, c_ref, k_ref in (
        (ls_ref, lr_ref, lc_ref, lk_ref),
        (rs_ref, rr_ref, rc_ref, rk_ref),
    ):
        root = root_ref[0]
        parts = split(root)
        square = split(product(parts, parts))
        fourth = split(product(square, square))
        fifth = product(parts, fourth)
        k_ref[...] = fifth * ((1.0 - DECAY) / 4.0)
        c_ref[...] = 1.25 * root - (DECAY / 4.0) * product(split(fifth), split(stat_ref[0]))


def whole(count):
    return [pl.BlockSpec(memory_space=pltpu.VMEM)] * count


def roots(left_stat, right_stat, left_root, right_root):
    return pl.pallas_call(
        roots_kernel,
        out_shape=[jax.ShapeDtypeStruct((ORDER, ORDER), jnp.float32)] * 4,
        in_specs=whole(4),
        out_specs=whole(4),
        compiler_params=pltpu.CompilerParams(vmem_limit_bytes=VMEM_LIMIT),
        name="roots",
    )(left_stat, right_stat, left_root, right_root)


def join_kernel(k0, r0, k1, r1, k2, r2, out):
    at = 0
    for kept, got in ((k0, r0), (k1, r1), (k2, r2)):
        count = kept.shape[1]
        out[at : at + count] = kept[0] + got[0]
        at += count


def join(pieces):
    return pl.pallas_call(
        join_kernel,
        out_shape=jax.ShapeDtypeStruct((32, 8, 128), jnp.float32),
        in_specs=whole(6),
        out_specs=pl.BlockSpec(memory_space=pltpu.VMEM),
        name="join",
    )(*pieces)


def assemble(narrow, pieces, grad):
    for m, piece in enumerate(pieces):
        row = (narrow ^ m) * ROWS
        for pair in range(16):
            col = (pair % 4) * 128
            start = pl.multiple_of(row + (pair // 4) * 16, 16)
            grad[pl.ds(start, 16), col : col + 128] = piece[2 * pair : 2 * pair + 2].reshape(16, 128)


def rows_kernel(scalars_ref, *refs):
    pieces = refs[:8]
    lc_ref, lk_ref, rc_ref, rk_ref, out, grad = refs[8:]
    narrow = scalars_ref[4]
    assemble(narrow, pieces, grad)
    g = split(grad[...])
    start = pl.multiple_of(narrow * ROWS, ROWS)
    inner = product(split(lk_ref[pl.ds(start, ROWS), :]), g)
    left = lc_ref[pl.ds(start, ROWS), :] - product(split(inner), g, NT)
    turned = split(product(split(left), g))
    inner = product(turned, split(rk_ref[...]))
    inner = product(split(inner), g, NT)
    out[...] = product(turned, split(rc_ref[...])) - product(split(inner), g)


def precondition_rows(scalars, pieces, constants):
    return pl.pallas_call(
        rows_kernel,
        out_shape=jax.ShapeDtypeStruct((ROWS, ORDER), jnp.float32),
        in_specs=[pl.BlockSpec(memory_space=pltpu.SMEM)] + whole(12),
        out_specs=pl.BlockSpec(memory_space=pltpu.VMEM),
        scratch_shapes=[pltpu.VMEM((ORDER, ORDER), jnp.float32)],
        compiler_params=pltpu.CompilerParams(vmem_limit_bytes=VMEM_LIMIT),
        name="rows",
    )(scalars, *pieces, *constants)


def stats_kernel(scalars_ref, *refs):
    pieces = refs[:8]
    lc_ref, lk_ref, rc_ref, rk_ref, ls_ref, rs_ref = refs[8:14]
    ln_ref, rn_ref, li_ref, ri_ref, grad = refs[14:]
    assemble(scalars_ref[4], pieces, grad)
    g = split(grad[...])
    for dims, stat_ref, c_ref, k_ref, new_ref, inv_ref in (
        (NT, ls_ref, lc_ref, lk_ref, ln_ref, li_ref),
        (TN, rs_ref, rc_ref, rk_ref, rn_ref, ri_ref),
    ):
        gram = product(g, g, dims)
        new_ref[0] = DECAY * stat_ref[0] + (1.0 - DECAY) * gram
        inv_ref[0] = c_ref[...] - product(split(k_ref[...]), split(gram))


def statistics(scalars, pieces, constants, left_stat, right_stat):
    return pl.pallas_call(
        stats_kernel,
        out_shape=[jax.ShapeDtypeStruct((1, ORDER, ORDER), jnp.float32)] * 4,
        in_specs=[pl.BlockSpec(memory_space=pltpu.SMEM)] + whole(14),
        out_specs=whole(4),
        scratch_shapes=[pltpu.VMEM((ORDER, ORDER), jnp.float32)],
        compiler_params=pltpu.CompilerParams(vmem_limit_bytes=VMEM_LIMIT),
        name="stats",
    )(scalars, *pieces, *constants, left_stat, right_stat)


def spread_kernel(scalars_ref, owner_ref, pair_ref, p0, p1, p2, p3, q0, q1, q2, q3, out, inverse, sems):
    x, z, c = scalars_ref[0], scalars_ref[2], scalars_ref[3]
    xh = x >> 1
    fill_inverse(owner_ref, inverse)
    copies = []

    def put(src, xd, zd, cd):
        slot = (xd * 4 + zd) * 2 + cd
        copies.append(pltpu.make_async_copy(src, out.at[inverse[slot]], sems.at[len(copies)]))

    for i in range(2):
        put(pair_ref.at[i], xh, z, c ^ i)
    put(p0, xh ^ 1, z, c)
    put(q0, xh ^ 1, z, 1 - c)
    for holder, group in ((c, (p1, p2, p3)), (1 - c, (q1, q2, q3))):
        for j, ref in enumerate(group):
            for i in range(2):
                put(ref.at[i], xh ^ holder, z ^ (j + 1), holder ^ i)
    for copy in copies:
        copy.start()
    for copy in copies:
        copy.wait()


def spread(scalars, owner_table, pieces):
    smem = pl.BlockSpec(memory_space=pltpu.SMEM)
    anywhere = pl.BlockSpec(memory_space=pl.ANY)
    return pl.pallas_call(
        spread_kernel,
        out_shape=jax.ShapeDtypeStruct((16, ROWS, ORDER), jnp.float32),
        in_specs=[smem, smem] + [anywhere] * 9,
        out_specs=anywhere,
        scratch_shapes=[pltpu.SMEM((16,), jnp.int32), pltpu.SemaphoreType.DMA((16,))],
        name="spread",
    )(scalars, owner_table, *pieces)


def local(replica_grads, owner_table, left_stat, right_stat, left_root, right_root):
    x, y, z, c = place()
    scalars = jnp.stack([x, y, z, c, y * 2 + (x & 1)]).astype(jnp.int32)
    streams = range(3)
    sends = [(s, 1) for s in streams]
    keeps = [(s, 0) for s in streams]
    other_send = pack(False, sends, scalars, owner_table, replica_grads)
    got_send = [send(other_send[s], CORE_SWAP) for s in streams]
    own_send = pack(True, sends, scalars, owner_table, replica_grads)
    other_keep = pack(False, keeps, scalars, owner_table, replica_grads)
    got_keep = [send(other_keep[s], CORE_SWAP) for s in streams]
    own_keep = pack(True, keeps, scalars, owner_table, replica_grads)
    outgoing = [own_send[s] + got_send[s] for s in streams]
    kept = [own_keep[s] + got_keep[s] for s in streams]
    constants = roots(left_stat, right_stat, left_root, right_root)
    tails = [None] * 3
    for step in range(6):
        masks = (1, 3) if step % 2 == 0 else (3, 1)
        for s in streams:
            got = send(outgoing[s], axis_move((s + step // 2) % 3, masks))
            if step == 5:
                tails[s] = (kept[s], got)
                continue
            half = kept[s].shape[0] // 2
            outgoing[s] = kept[s][half:] + got[half:]
            kept[s] = kept[s][:half] + got[:half]
    own = join([value for pair in tails for value in pair])
    pieces = [own] + [None] * 7
    for m in (1, 5, 3, 7, 4, 2, 6):
        pieces[m] = send(
            own, permutation(lambda x, y, z, c, m=m: (x ^ (m & 1), y ^ (m >> 1), z, c))
        )
    rows = precondition_rows(scalars, pieces, constants)
    both = jnp.stack([rows, send(rows, CORE_SWAP)])
    got = [None] * 4
    for j in (2, 1, 3):
        got[j] = send(both, permutation(lambda x, y, z, c, j=j: (x ^ (2 * c), y, z ^ j, c)))
    got[0] = send(rows, axis_move(0, (2, 2)))
    swapped = [send(value, CORE_SWAP) for value in got]
    left_new, right_new, left_inverse, right_inverse = statistics(
        scalars, pieces, constants, left_stat, right_stat
    )
    directions = spread(scalars, owner_table, [both] + got + swapped)
    return directions, left_new, right_new, left_inverse, right_inverse


def solution(mesh):
    fine = Mesh(mesh.devices.reshape(SIZES), AXES)
    wide = ("xh", "z", "core")
    narrow = ("y", "xl")
    slot = P(wide, None, None)
    return jax.shard_map(
        local,
        mesh=fine,
        in_specs=(P(wide + narrow, None, None, None), P(), slot, slot, slot, slot),
        out_specs=(P(None, narrow, None), slot, slot, slot, slot),
        check_vma=False,
    )
```

time: 346 us -> 214 us (0.62)
  waiting for transfers between devices: 264 us -> 33.8 us
  Pallas kernels: 0 us -> 103 us
  starting transfers between devices: 0.3 us -> 60.9 us
  matrix products: 37 us -> 0 us
  local copies, waits for them, and re-layouts: 29.4 us -> 2.91 us
  between operations: 14 us -> 1.16 us
  other arithmetic: 1.76 us -> 12.7 us
    reduce_scatter x1 -> x0, waiting for transfers between devices: 146 us -> none  [local(): lax.psum_scatter(slot_grads, 'wide', scatter_dimension=0, tiled=True)[0]]
    pallas_call x0 -> x9, Pallas kernels: none -> 103 us  [the longest x1 65.5 us: spread(): pl.pallas_call(spread_kernel, out_shape=jax.ShapeDtypeStruct((16, ROWS, O...]
    psum x1 -> x0, waiting for transfers between devices: 68.5 us -> none  [local(): summed = lax.psum(partial_sum, 'narrow')]
    ppermute x0 -> x40, starting transfers between devices: none -> 60.9 us  [send(): return lax.ppermute(value, AXES, pairs)]
    all_gather x1 -> x0, waiting for transfers between devices: 49.1 us -> none  [local(): gathered = lax.all_gather(own_rows[None], 'wide', axis=0, tiled=True)]
    dot_general x13 -> x0, matrix products: 37 us -> none  [the longest x11 26.7 us: matmul_high(): jnp.dot(first, second, precision=lax.Precision.HIGHEST, preferred_element...]
    ppermute x0 -> x40, waiting for transfers between devices: none -> 33.8 us  [send(): return lax.ppermute(value, AXES, pairs)]
    dot_general x1 -> x0, local copies, waits for them, and re-layouts: 19.1 us -> none  [local(): jnp.einsum('wb,bij->wij', selector, local_grads, preferred_element_type=j...]
  transfers between devices with their start and end apart: 3 -> 40, of which waited for: 3 -> 14; matrix products, arithmetic and copies ran while one was open for 4% -> 6% of each run, Pallas kernels for 0% -> 13%
where the time goes in v1:
time: 214 us
  Pallas kernels  103 us (48%)
  starting transfers between devices  60.9 us (28%)
  waiting for transfers between devices  33.8 us (16%)
  other arithmetic  12.7 us (6%)
  local copies, waits for them, and re-layouts  2.91 us (1%)
    pallas_call x1, Pallas kernels, spread(): pl.pallas_call(spread_kernel, out_shape=jax.ShapeDtypeStruct((16, ROWS, O...  65.5 us
    ppermute x40, starting transfers between devices, send(): return lax.ppermute(value, AXES, pairs)  60.9 us
    ppermute x40, waiting for transfers between devices, send(): return lax.ppermute(value, AXES, pairs)  33.8 us
    pallas_call x4, Pallas kernels, pack(): pl.pallas_call(functools.partial(pack_kernel, own, parts), out_shape=[jax...  16.9 us
    pallas_call x1, Pallas kernels, roots(): pl.pallas_call(roots_kernel, out_shape=[jax.ShapeDtypeStruct((ORDER, ORDE...  8.88 us
    pallas_call x1, Pallas kernels, statistics(): pl.pallas_call(stats_kernel, out_shape=[jax.ShapeDtypeStruct((1, ORDER, O...  6.35 us
  transfers between devices with their start and end apart: 40, of which 14 were waited for; matrix products, arithmetic and copies ran while one was open for 6% of the time, Pallas kernels for 13%

profile of v1, /device:TPU:1, one launch (start us, length us, event | category | flops | bytes accessed | tf_op | source)
XLA Modules:
  0.0 214.0 jit_solution(5902573760706617339)
XLA Ops:
  1.4 4.2 %pack_other.3 = (f32[32,12,8,128]{3,2,1,0:T(8,128)S(1)}, f32[32,10,8,128]{3,2,1,0:T(8,128)S(1)}, f32[32,10,8,128]{3,2,1,0:T(8,128)S(1)}) custom-call(s32[5]{0:T(128)S(1)} %stack.32.scalars_ref, s32[16]{0:T(128)S(1)} %copy-done.3, bf16[1,16,512,512]{3,2,1,0:T(8,128)(2,1)} %grads_ref.7), custom_call_target="tpu_custom_call" | custom-call | tf_op jit(solution)/shard_map/pack_other/pallas_call | solution.py:126
  5.6 1.5 collective-permute-start.17
  7.6 4.3 %pack_other.2 = (f32[32,12,8,128]{3,2,1,0:T(8,128)S(1)}, f32[32,10,8,128]{3,2,1,0:T(8,128)S(1)}, f32[32,10,8,128]{3,2,1,0:T(8,128)S(1)}) custom-call(s32[5]{0:T(128)S(1)} %stack.32.scalars_ref, s32[16]{0:T(128)S(1)} %copy-done.3, bf16[1,16,512,512]{3,2,1,0:T(8,128)(2,1)} %grads_ref.7), custom_call_target="tpu_custom_call" | custom-call | tf_op jit(solution)/shard_map/pack_other/pallas_call | solution.py:126
  12.1 4.2 %pack_own.3 = (f32[32,12,8,128]{3,2,1,0:T(8,128)S(1)}, f32[32,10,8,128]{3,2,1,0:T(8,128)S(1)}, f32[32,10,8,128]{3,2,1,0:T(8,128)S(1)}) custom-call(s32[5]{0:T(128)S(1)} %stack.32.scalars_ref, s32[16]{0:T(128)S(1)} %copy-done.3, bf16[1,16,512,512]{3,2,1,0:T(8,128)(2,1)} %grads_ref.7), custom_call_target="tpu_custom_call" | custom-call | tf_op jit(solution)/shard_map/pack_own/pallas_call | solution.py:126
  16.3 2.5 %add.141 = f32[32,10,8,128]{3,2,1,0:T(8,128)} add(f32[32,10,8,128]{3,2,1,0:T(8,128)S(1)} %get-tuple-element.35, f32[32,10,8,128]{3,2,1,0:T(8,128)} %collective-permute-done.17) | non-fusion elementwise | flops 327680 | bytes 3932160 | tf_op jit(solution)/shard_map/add | solution.py:303
  18.8 3.8 %collective-permute-start.18 = (f32[32,10,8,128]{3,2,1,0:T(8,128)}, f32[32,10,8,128]{3,2,1,0:T(8,128)}, u32[]{:S(2)}, u32[]{:S(2)}) collective-permute-start(f32[32,10,8,128]{3,2,1,0:T(8,128)} %add.141), channel_id=1, source_target_pairs={{0,16},{8,56},{16,0},{24,40},{32,48},{40,24},{48,32},{56,8},{2,18}... | collective-permute-start | bytes 3932168 | tf_op jit(solution)/shard_map/ppermute | solution.py:46
  22.7 1.2 add.129
  23.9 2.7 %collective-permute-start.10 = (f32[32,10,8,128]{3,2,1,0:T(8,128)}, f32[32,10,8,128]{3,2,1,0:T(8,128)}, u32[]{:S(2)}, u32[]{:S(2)}) collective-permute-start(f32[32,10,8,128]{3,2,1,0:T(8,128)} %add.129), channel_id=1, source_target_pairs={{0,2},{8,14},{16,18},{24,30},{32,34},{40,46},{48,50},{56,62},{2,0}... | collective-permute-start | bytes 3932168 | tf_op jit(solution)/shard_map/ppermute | solution.py:46
  26.9 2.6 %collective-permute-start.2 = (f32[32,12,8,128]{3,2,1,0:T(8,128)S(1)}, f32[32,12,8,128]{3,2,1,0:T(8,128)S(1)}, u32[]{:S(2)}, u32[]{:S(2)}) collective-permute-start(f32[32,12,8,128]{3,2,1,0:T(8,128)S(1)} %add.117), channel_id=1, source_target_pairs={{0,1},{8,73},{16,17},{24,89},{32,33},{40,105},{48,49},{56,121},{2,... | collective-permute-start | bytes 4718600 | tf_op jit(solution)/shard_map/ppermute | solution.py:46
  29.5 4.3 %pack_own.2 = (f32[32,12,8,128]{3,2,1,0:T(8,128)S(1)}, f32[32,10,8,128]{3,2,1,0:T(8,128)S(1)}, f32[32,10,8,128]{3,2,1,0:T(8,128)S(1)}) custom-call(s32[5]{0:T(128)S(1)} %stack.32.scalars_ref, s32[16]{0:T(128)S(1)} %copy-done.3, bf16[1,16,512,512]{3,2,1,0:T(8,128)(2,1)} %grads_ref.7), custom_call_target="tpu_custom_call" | custom-call | tf_op jit(solution)/shard_map/pack_own/pallas_call | solution.py:126
  33.7 1.5 add.140
  35.2 2.8 %collective-permute-done.18 = f32[32,10,8,128]{3,2,1,0:T(8,128)} collective-permute-done((f32[32,10,8,128]{3,2,1,0:T(8,128)}, f32[32,10,8,128]{3,2,1,0:T(8,128)}, u32[]{:S(2)}, u32[]{:S(2)}) %collective-permute-start.18) | collective-permute-done | bytes 1310752 | tf_op jit(solution)/shard_map/ppermute | solution.py:46
  38.0 1.5 slice_add_fusion.3
  39.6 1.5 add.128
  41.0 0.9 collective-permute-done.10
  42.0 1.4 slice_add_fusion.5
  44.1 3.7 %collective-permute-done.2 = f32[32,12,8,128]{3,2,1,0:T(8,128)S(1)} collective-permute-done((f32[32,12,8,128]{3,2,1,0:T(8,128)S(1)}, f32[32,12,8,128]{3,2,1,0:T(8,128)S(1)}, u32[]{:S(2)}, u32[]{:S(2)}) %collective-permute-start.2) | collective-permute-done | bytes 1572896 | tf_op jit(solution)/shard_map/ppermute | solution.py:46
  48.1 1.1 collective-permute-done.19
  49.3 2.6 %collective-permute-start.20 = (f32[8,10,8,128]{3,2,1,0:T(8,128)S(1)}, f32[8,10,8,128]{3,2,1,0:T(8,128)S(1)}, u32[]{:S(2)}, u32[]{:S(2)}) collective-permute-start(f32[8,10,8,128]{3,2,1,0:T(8,128)S(1)} %get-tuple-element.54), channel_id=1, source_target_pairs={{0,1},{8,73},{16,17},{24,89},{32,33},{40,105},{48,49},{56,121},{2,... | collective-permute-start | bytes 983048 | tf_op jit(solution)/shard_map/ppermute | solution.py:46
  51.9 1.3 collective-permute-done.11
  53.3 1.8 collective-permute-start.12
  55.1 4.9 %collective-permute-done.20 = f32[8,10,8,128]{3,2,1,0:T(8,128)S(1)} collective-permute-done((f32[8,10,8,128]{3,2,1,0:T(8,128)S(1)}, f32[8,10,8,128]{3,2,1,0:T(8,128)S(1)}, u32[]{:S(2)}, u32[]{:S(2)}) %collective-permute-start.20) | collective-permute-done | bytes 327712 | tf_op jit(solution)/shard_map/ppermute | solution.py:46
  60.1 2.7 %collective-permute-done.3 = f32[16,12,8,128]{3,2,1,0:T(8,128)S(1)} collective-permute-done((f32[16,12,8,128]{3,2,1,0:T(8,128)S(1)}, f32[16,12,8,128]{3,2,1,0:T(8,128)S(1)}, u32[]{:S(2)}, u32[]{:S(2)}) %collective-permute-start.3) | collective-permute-done | bytes 786464 | tf_op jit(solution)/shard_map/ppermute | solution.py:46
  62.9 0.8 collective-permute-start.4
  64.6 3.0 %collective-permute-start.22 = (f32[2,10,8,128]{3,2,1,0:T(8,128)S(1)}, f32[2,10,8,128]{3,2,1,0:T(8,128)S(1)}, u32[]{:S(2)}, u32[]{:S(2)}) collective-permute-start(f32[2,10,8,128]{3,2,1,0:T(8,128)S(1)} %get-tuple-element.66), channel_id=1, source_target_pairs={{0,2},{8,14},{16,18},{24,30},{32,34},{40,46},{48,50},{56,62},{2,0}... | collective-permute-start | bytes 245768 | tf_op jit(solution)/shard_map/ppermute | solution.py:46
  67.6 3.5 %collective-permute-done.4 = f32[8,12,8,128]{3,2,1,0:T(8,128)S(1)} collective-permute-done((f32[8,12,8,128]{3,2,1,0:T(8,128)S(1)}, f32[8,12,8,128]{3,2,1,0:T(8,128)S(1)}, u32[]{:S(2)}, u32[]{:S(2)}) %collective-permute-start.4) | collective-permute-done | bytes 393248 | tf_op jit(solution)/shard_map/ppermute | solution.py:46
  71.3 2.6 %collective-permute-start.14 = (f32[2,10,8,128]{3,2,1,0:T(8,128)S(1)}, f32[2,10,8,128]{3,2,1,0:T(8,128)S(1)}, u32[]{:S(2)}, u32[]{:S(2)}) collective-permute-start(f32[2,10,8,128]{3,2,1,0:T(8,128)S(1)} %get-tuple-element.68), channel_id=1, source_target_pairs={{0,1},{8,73},{16,17},{24,89},{32,33},{40,105},{48,49},{56,121},{2,... | collective-permute-start | bytes 245768 | tf_op jit(solution)/shard_map/ppermute | solution.py:46
  73.8 2.1 collective-permute-done.5
  76.0 1.3 collective-permute-start.6
  77.9 2.9 %collective-permute-done.6 = f32[2,12,8,128]{3,2,1,0:T(8,128)S(1)} collective-permute-done((f32[2,12,8,128]{3,2,1,0:T(8,128)S(1)}, f32[2,12,8,128]{3,2,1,0:T(8,128)S(1)}, u32[]{:S(2)}, u32[]{:S(2)}) %collective-permute-start.6) | collective-permute-done | bytes 98336 | tf_op jit(solution)/shard_map/ppermute | solution.py:46
  82.0 3.1 %collective-permute-done.15.r1 = f32[1,10,8,128]{3,2,1,0:T(8,128)S(1)} collective-permute-done((f32[1,10,8,128]{3,2,1,0:T(8,128)S(1)}, f32[1,10,8,128]{3,2,1,0:T(8,128)S(1)}, u32[]{:S(2)}, u32[]{:S(2)}) %collective-permute-start.15) | collective-permute-done | bytes 40992 | tf_op jit(solution)/shard_map/ppermute | solution.py:46
  85.8 1.6 join.1.refs_0_
  87.6 2.4 %collective-permute-start.26 = (f32[32,8,128]{2,1,0:T(8,128)}, f32[32,8,128]{2,1,0:T(8,128)S(1)}, u32[]{:S(2)}, u32[]{:S(2)}) collective-permute-start(f32[32,8,128]{2,1,0:T(8,128)} %join.1.refs_0_), channel_id=1, source_target_pairs={{0,3},{8,11},{16,19},{24,27},{32,35},{40,43},{48,51},{56,59},{2,1}... | collective-permute-start | bytes 393224 | tf_op jit(solution)/shard_map/ppermute | solution.py:46
  90.0 2.3 %collective-permute-start.27 = (f32[32,8,128]{2,1,0:T(8,128)}, f32[32,8,128]{2,1,0:T(8,128)S(1)}, u32[]{:S(2)}, u32[]{:S(2)}) collective-permute-start(f32[32,8,128]{2,1,0:T(8,128)} %join.1.refs_0_), channel_id=1, source_target_pairs={{0,4},{8,12},{16,20},{24,28},{32,36},{40,44},{48,52},{56,60},{2,6}... | collective-permute-start | bytes 393224 | tf_op jit(solution)/shard_map/ppermute | solution.py:46
  92.7 1.6 collective-permute-start.29
  94.3 2.2 %collective-permute-start.30 = (f32[32,8,128]{2,1,0:T(8,128)}, f32[32,8,128]{2,1,0:T(8,128)S(1)}, u32[]{:S(2)}, u32[]{:S(2)}) collective-permute-start(f32[32,8,128]{2,1,0:T(8,128)} %join.1.refs_0_), channel_id=1, source_target_pairs={{0,7},{8,15},{16,23},{24,31},{32,39},{40,47},{48,55},{56,63},{2,5}... | collective-permute-start | bytes 393224 | tf_op jit(solution)/shard_map/ppermute | solution.py:46
  96.5 8.9 %roots.1 = (f32[512,512]{1,0:T(8,128)S(1)}, f32[512,512]{1,0:T(8,128)S(1)}, f32[512,512]{1,0:T(8,128)S(1)}, f32[512,512]{1,0:T(8,128)S(1)}) custom-call(f32[1,512,512]{2,1,0:T(8,128)S(1)} %copy-done, f32[1,512,512]{2,1,0:T(8,128)} %refs_13_.1, f32[1,512,512]{2,1,0:T(8,128)} %lr_ref.1, f32[1,512,512]{2,1,0:T(8,128)} %rr_ref.1), custom_call_target="tpu_custom_call" | custom-call | tf_op jit(solution)/shard_map/roots/pallas_call | solution.py:163
  105.5 3.4 %rows.1 = f32[64,512]{1,0:T(8,128)S(1)} custom-call(s32[5]{0:T(128)S(1)} %stack.32.scalars_ref, f32[32,8,128]{2,1,0:T(8,128)S(1)} %copy-done.1, f32[32,8,128]{2,1,0:T(8,128)S(1)} %collective-permute-done.24.refs_1_, f32[32,8,128]{2,1,0:T(8,128)S(1)} %collective-permute-done.25.refs_2_, f32[32,8,128]{2,1,0:T(8,128)S(1)} %collective-permute-done.26.refs_3_, ...), custom_call_target="tpu_custom_call" | custom-call | tf_op jit(solution)/shard_map/rows/pallas_call | solution.py:216
  108.9 10.9 %collective-permute-start.31 = (f32[64,512]{1,0:T(8,128)S(1)}, f32[64,512]{1,0:T(8,128)S(1)}, u32[]{:S(2)}, u32[]{:S(2)}) collective-permute-start(f32[64,512]{1,0:T(8,128)S(1)} %rows.1), channel_id=1, source_target_pairs={{0,8},{8,0},{16,24},{24,16},{32,40},{40,32},{48,56},{56,48},{2,10}... | collective-permute-start | bytes 393224 | tf_op jit(solution)/shard_map/ppermute | solution.py:46
  119.7 1.0 collective-permute-done.31
  121.5 4.3 %collective-permute-start.34 = (f32[2,64,512]{2,1,0:T(8,128)S(1)}, f32[2,64,512]{2,1,0:T(8,128)S(1)}, u32[]{:S(2)}, u32[]{:S(2)}) collective-permute-start(f32[2,64,512]{2,1,0:T(8,128)S(1)} %pad_maximum_fusion.pair_ref), channel_id=1, source_target_pairs={{0,32},{8,104},{16,48},{24,120},{32,0},{40,72},{48,16},{56,88},{2,... | collective-permute-start | bytes 786440 | tf_op jit(solution)/shard_map/ppermute | solution.py:46
  125.8 1.9 collective-permute-start.35
  127.7 2.1 %collective-permute-start.32 = (f32[64,512]{1,0:T(8,128)S(1)}, f32[64,512]{1,0:T(8,128)S(1)}, u32[]{:S(2)}, u32[]{:S(2)}) collective-permute-start(f32[64,512]{1,0:T(8,128)S(1)} %rows.1), channel_id=1, source_target_pairs={{0,64},{8,72},{16,80},{24,88},{32,96},{40,104},{48,112},{56,120},{... | collective-permute-start | bytes 393224 | tf_op jit(solution)/shard_map/ppermute | solution.py:46
  129.8 2.0 collective-permute-start.37
  131.8 3.0 %collective-permute-done.34.p2 = f32[2,64,512]{2,1,0:T(8,128)S(1)} collective-permute-done((f32[2,64,512]{2,1,0:T(8,128)S(1)}, f32[2,64,512]{2,1,0:T(8,128)S(1)}, u32[]{:S(2)}, u32[]{:S(2)}) %collective-permute-start.34) | collective-permute-done | bytes 262176 | tf_op jit(solution)/shard_map/ppermute | solution.py:46
  134.8 5.0 %collective-permute-start.38 = (f32[2,64,512]{2,1,0:T(8,128)S(1)}, f32[2,64,512]{2,1,0:T(8,128)S(1)}, u32[]{:S(2)}, u32[]{:S(2)}) collective-permute-start(f32[2,64,512]{2,1,0:T(8,128)S(1)} %collective-permute-done.34.p2), channel_id=1, source_target_pairs={{0,8},{8,0},{16,24},{24,16},{32,40},{40,32},{48,56},{56,48},{2,10}... | collective-permute-start | bytes 786440 | tf_op jit(solution)/shard_map/ppermute | solution.py:46
  140.4 6.3 %stats.1 = (f32[1,512,512]{2,1,0:T(8,128)}, f32[1,512,512]{2,1,0:T(8,128)}, f32[1,512,512]{2,1,0:T(8,128)}, f32[1,512,512]{2,1,0:T(8,128)}) custom-call(s32[5]{0:T(128)S(1)} %stack.32.scalars_ref, f32[32,8,128]{2,1,0:T(8,128)S(1)} %copy-done.1, f32[32,8,128]{2,1,0:T(8,128)S(1)} %collective-permute-done.24.refs_1_, ...), custom_call_target="tpu_custom_call" | custom-call | tf_op jit(solution)/shard_map/stats/pallas_call | solution.py:243
  148.4 65.5 %spread.1 = f32[16,64,512]{2,1,0:T(8,128)} custom-call(s32[5]{0:T(128)} %copy-done.2, s32[16]{0:T(128)} %owner_ref.9, f32[2,64,512]{2,1,0:T(8,128)} %copy-done.4, f32[64,512]{1,0:T(8,128)} %copy-done.11, f32[2,64,512]{2,1,0:T(8,128)} %copy-done.5, f32[2,64,512]{2,1,0:T(8,128)} %copy-done.6, f32[2,64,512]{2,1,0:T(8,128)} %copy-done.7, f32[64,512]{1,0:T(8,128)} %copy-done.12, ...), custom_call_target="tpu_custom_call" | custom-call | tf_op jit(solution)/shard_map/spread/pallas_call | solution.py:281
  (96 shorter events, 10.4 us)
Async XLA Ops:
  1.4 139.0 %copy-start.2 = (s32[5]{0:T(128)}, s32[5]{0:T(128)S(1)}, u32[]{:S(2)}) copy-start(s32[5]{0:T(128)S(1)} %stack.32.scalars_ref) | copy-start | bytes 64
  5.6 10.7 %collective-permute-start.17 = (f32[32,10,8,128]{3,2,1,0:T(8,128)S(1)}, f32[32,10,8,128]{3,2,1,0:T(8,128)}, u32[]{:S(2)}, u32[]{:S(2)}) collective-permute-start(f32[32,10,8,128]{3,2,1,0:T(8,128)S(1)} %get-tuple-element.36), channel_id=1, source_target_pairs={{0,8},{8,0},{16,24},{24,16},{32,40},{40,32},{48,56},{56,48},{2,10}... | collective-permute-start | bytes 3932168 | tf_op jit(solution)/shard_map/ppermute | solution.py:46
  7.1 19.5 %collective-permute-start.1 = (f32[32,12,8,128]{3,2,1,0:T(8,128)S(1)}, f32[32,12,8,128]{3,2,1,0:T(8,128)S(1)}, u32[]{:S(2)}, u32[]{:S(2)}) collective-permute-start(f32[32,12,8,128]{3,2,1,0:T(8,128)S(1)} %get-tuple-element.28), channel_id=1, source_target_pairs={{0,8},{8,0},{16,24},{24,16},{32,40},{40,32},{48,56},{56,48},{2,10}... | collective-permute-start | bytes 4718600 | tf_op jit(solution)/shard_map/ppermute | solution.py:46
  7.2 15.5 %collective-permute-start.9 = (f32[32,10,8,128]{3,2,1,0:T(8,128)S(1)}, f32[32,10,8,128]{3,2,1,0:T(8,128)S(1)}, u32[]{:S(2)}, u32[]{:S(2)}) collective-permute-start(f32[32,10,8,128]{3,2,1,0:T(8,128)S(1)} %get-tuple-element.32), channel_id=1, source_target_pairs={{0,8},{8,0},{16,24},{24,16},{32,40},{40,32},{48,56},{56,48},{2,10}... | collective-permute-start | bytes 3932168 | tf_op jit(solution)/shard_map/ppermute | solution.py:46
  11.9 15.0 %collective-permute-start.16 = (f32[32,10,8,128]{3,2,1,0:T(8,128)S(1)}, f32[32,10,8,128]{3,2,1,0:T(8,128)}, u32[]{:S(2)}, u32[]{:S(2)}) collective-permute-start(f32[32,10,8,128]{3,2,1,0:T(8,128)S(1)} %get-tuple-element.34), channel_id=1, source_target_pairs={{0,8},{8,0},{16,24},{24,16},{32,40},{40,32},{48,56},{56,48},{2,10}... | collective-permute-start | bytes 3932168 | tf_op jit(solution)/shard_map/ppermute | solution.py:46
  18.8 19.2 %collective-permute-start.18 = (f32[32,10,8,128]{3,2,1,0:T(8,128)}, f32[32,10,8,128]{3,2,1,0:T(8,128)}, u32[]{:S(2)}, u32[]{:S(2)}) collective-permute-start(f32[32,10,8,128]{3,2,1,0:T(8,128)} %add.141), channel_id=1, source_target_pairs={{0,16},{8,56},{16,0},{24,40},{32,48},{40,24},{48,32},{56,8},{2,18}... | collective-permute-start | bytes 3932168 | tf_op jit(solution)/shard_map/ppermute | solution.py:46
  22.7 16.9 %collective-permute-start.8 = (f32[32,10,8,128]{3,2,1,0:T(8,128)S(1)}, f32[32,10,8,128]{3,2,1,0:T(8,128)}, u32[]{:S(2)}, u32[]{:S(2)}) collective-permute-start(f32[32,10,8,128]{3,2,1,0:T(8,128)S(1)} %get-tuple-element.30), channel_id=1, source_target_pairs={{0,8},{8,0},{16,24},{24,16},{32,40},{40,32},{48,56},{56,48},{2,10}... | collective-permute-start | bytes 3932168 | tf_op jit(solution)/shard_map/ppermute | solution.py:46
  23.9 18.0 %collective-permute-start.10 = (f32[32,10,8,128]{3,2,1,0:T(8,128)}, f32[32,10,8,128]{3,2,1,0:T(8,128)}, u32[]{:S(2)}, u32[]{:S(2)}) collective-permute-start(f32[32,10,8,128]{3,2,1,0:T(8,128)} %add.129), channel_id=1, source_target_pairs={{0,2},{8,14},{16,18},{24,30},{32,34},{40,46},{48,50},{56,62},{2,0}... | collective-permute-start | bytes 3932168 | tf_op jit(solution)/shard_map/ppermute | solution.py:46
  26.7 17.2 %collective-permute-start = (f32[32,12,8,128]{3,2,1,0:T(8,128)S(1)}, f32[32,12,8,128]{3,2,1,0:T(8,128)S(1)}, u32[]{:S(2)}, u32[]{:S(2)}) collective-permute-start(f32[32,12,8,128]{3,2,1,0:T(8,128)S(1)} %get-tuple-element.26), channel_id=1, source_target_pairs={{0,8},{8,0},{16,24},{24,16},{32,40},{40,32},{48,56},{56,48},{2,10}... | collective-permute-start | bytes 4718600 | tf_op jit(solution)/shard_map/ppermute | solution.py:46
  26.9 20.9 %collective-permute-start.2 = (f32[32,12,8,128]{3,2,1,0:T(8,128)S(1)}, f32[32,12,8,128]{3,2,1,0:T(8,128)S(1)}, u32[]{:S(2)}, u32[]{:S(2)}) collective-permute-start(f32[32,12,8,128]{3,2,1,0:T(8,128)S(1)} %add.117), channel_id=1, source_target_pairs={{0,1},{8,73},{16,17},{24,89},{32,33},{40,105},{48,49},{56,121},{2,... | collective-permute-start | bytes 4718600 | tf_op jit(solution)/shard_map/ppermute | solution.py:46
  39.5 9.8 %collective-permute-start.19 = (f32[16,10,8,128]{3,2,1,0:T(8,128)S(1)}, f32[16,10,8,128]{3,2,1,0:T(8,128)S(1)}, u32[]{:S(2)}, u32[]{:S(2)}) collective-permute-start(f32[16,10,8,128]{3,2,1,0:T(8,128)S(1)} %get-tuple-element.48), channel_id=1, source_target_pairs={{0,48},{8,24},{16,32},{24,8},{32,16},{40,56},{48,0},{56,40},{2,50}... | collective-permute-start | bytes 1966088 | tf_op jit(solution)/shard_map/ppermute | solution.py:46
  43.4 9.8 %collective-permute-start.11 = (f32[16,10,8,128]{3,2,1,0:T(8,128)S(1)}, f32[16,10,8,128]{3,2,1,0:T(8,128)S(1)}, u32[]{:S(2)}, u32[]{:S(2)}) collective-permute-start(f32[16,10,8,128]{3,2,1,0:T(8,128)S(1)} %get-tuple-element.50), channel_id=1, source_target_pairs={{0,6},{8,10},{16,22},{24,26},{32,38},{40,42},{48,54},{56,58},{2,4}... | collective-permute-start | bytes 1966088 | tf_op jit(solution)/shard_map/ppermute | solution.py:46
  48.0 14.7 %collective-permute-start.3 = (f32[16,12,8,128]{3,2,1,0:T(8,128)S(1)}, f32[16,12,8,128]{3,2,1,0:T(8,128)S(1)}, u32[]{:S(2)}, u32[]{:S(2)}) collective-permute-start(f32[16,12,8,128]{3,2,1,0:T(8,128)S(1)} %get-tuple-element.46), channel_id=1, source_target_pairs={{0,65},{8,9},{16,81},{24,25},{32,97},{40,41},{48,113},{56,57},{2,6... | collective-permute-start | bytes 2359304 | tf_op jit(solution)/shard_map/ppermute | solution.py:46
  49.3 10.6 %collective-permute-start.20 = (f32[8,10,8,128]{3,2,1,0:T(8,128)S(1)}, f32[8,10,8,128]{3,2,1,0:T(8,128)S(1)}, u32[]{:S(2)}, u32[]{:S(2)}) collective-permute-start(f32[8,10,8,128]{3,2,1,0:T(8,128)S(1)} %get-tuple-element.54), channel_id=1, source_target_pairs={{0,1},{8,73},{16,17},{24,89},{32,33},{40,105},{48,49},{56,121},{2,... | collective-permute-start | bytes 983048 | tf_op jit(solution)/shard_map/ppermute | solution.py:46
  53.3 10.4 %collective-permute-start.12 = (f32[8,10,8,128]{3,2,1,0:T(8,128)S(1)}, f32[8,10,8,128]{3,2,1,0:T(8,128)S(1)}, u32[]{:S(2)}, u32[]{:S(2)}) collective-permute-start(f32[8,10,8,128]{3,2,1,0:T(8,128)S(1)} %get-tuple-element.56), channel_id=1, source_target_pairs={{0,16},{8,56},{16,0},{24,40},{32,48},{40,24},{48,32},{56,8},{2,18}... | collective-permute-start | bytes 983048 | tf_op jit(solution)/shard_map/ppermute | solution.py:46
  60.0 4.5 %collective-permute-start.21 = (f32[4,10,8,128]{3,2,1,0:T(8,128)S(1)}, f32[4,10,8,128]{3,2,1,0:T(8,128)S(1)}, u32[]{:S(2)}, u32[]{:S(2)}) collective-permute-start(f32[4,10,8,128]{3,2,1,0:T(8,128)S(1)} %get-tuple-element.60), channel_id=1, source_target_pairs={{0,65},{8,9},{16,81},{24,25},{32,97},{40,41},{48,113},{56,57},{2,6... | collective-permute-start | bytes 491528 | tf_op jit(solution)/shard_map/ppermute | solution.py:46
  62.9 8.2 %collective-permute-start.4 = (f32[8,12,8,128]{3,2,1,0:T(8,128)S(1)}, f32[8,12,8,128]{3,2,1,0:T(8,128)S(1)}, u32[]{:S(2)}, u32[]{:S(2)}) collective-permute-start(f32[8,12,8,128]{3,2,1,0:T(8,128)S(1)} %get-tuple-element.52), channel_id=1, source_target_pairs={{0,2},{8,14},{16,18},{24,30},{32,34},{40,46},{48,50},{56,62},{2,0}... | collective-permute-start | bytes 1179656 | tf_op jit(solution)/shard_map/ppermute | solution.py:46
  63.7 7.5 %collective-permute-start.13 = (f32[4,10,8,128]{3,2,1,0:T(8,128)S(1)}, f32[4,10,8,128]{3,2,1,0:T(8,128)S(1)}, u32[]{:S(2)}, u32[]{:S(2)}) collective-permute-start(f32[4,10,8,128]{3,2,1,0:T(8,128)S(1)} %get-tuple-element.62), channel_id=1, source_target_pairs={{0,48},{8,24},{16,32},{24,8},{32,16},{40,56},{48,0},{56,40},{2,50}... | collective-permute-start | bytes 491528 | tf_op jit(solution)/shard_map/ppermute | solution.py:46
  64.6 12.7 %collective-permute-start.22 = (f32[2,10,8,128]{3,2,1,0:T(8,128)S(1)}, f32[2,10,8,128]{3,2,1,0:T(8,128)S(1)}, u32[]{:S(2)}, u32[]{:S(2)}) collective-permute-start(f32[2,10,8,128]{3,2,1,0:T(8,128)S(1)} %get-tuple-element.66), channel_id=1, source_target_pairs={{0,2},{8,14},{16,18},{24,30},{32,34},{40,46},{48,50},{56,62},{2,0}... | collective-permute-start | bytes 245768 | tf_op jit(solution)/shard_map/ppermute | solution.py:46
  71.1 25.4 %copy-start = (f32[1,512,512]{2,1,0:T(8,128)S(1)}, f32[1,512,512]{2,1,0:T(8,128)}, u32[]{:S(2)}) copy-start(f32[1,512,512]{2,1,0:T(8,128)} %refs_12_.1) | copy-start | bytes 3145732
  71.2 4.8 %collective-permute-start.5 = (f32[4,12,8,128]{3,2,1,0:T(8,128)S(1)}, f32[4,12,8,128]{3,2,1,0:T(8,128)S(1)}, u32[]{:S(2)}, u32[]{:S(2)}) collective-permute-start(f32[4,12,8,128]{3,2,1,0:T(8,128)S(1)} %get-tuple-element.58), channel_id=1, source_target_pairs={{0,6},{8,10},{16,22},{24,26},{32,38},{40,42},{48,54},{56,58},{2,4}... | collective-permute-start | bytes 589832 | tf_op jit(solution)/shard_map/ppermute | solution.py:46
  71.3 10.1 %collective-permute-start.14 = (f32[2,10,8,128]{3,2,1,0:T(8,128)S(1)}, f32[2,10,8,128]{3,2,1,0:T(8,128)S(1)}, u32[]{:S(2)}, u32[]{:S(2)}) collective-permute-start(f32[2,10,8,128]{3,2,1,0:T(8,128)S(1)} %get-tuple-element.68), channel_id=1, source_target_pairs={{0,1},{8,73},{16,17},{24,89},{32,33},{40,105},{48,49},{56,121},{2,... | collective-permute-start | bytes 245768 | tf_op jit(solution)/shard_map/ppermute | solution.py:46
  76.0 4.8 %collective-permute-start.6 = (f32[2,12,8,128]{3,2,1,0:T(8,128)S(1)}, f32[2,12,8,128]{3,2,1,0:T(8,128)S(1)}, u32[]{:S(2)}, u32[]{:S(2)}) collective-permute-start(f32[2,12,8,128]{3,2,1,0:T(8,128)S(1)} %get-tuple-element.64), channel_id=1, source_target_pairs={{0,16},{8,56},{16,0},{24,40},{32,48},{40,24},{48,32},{56,8},{2,18}... | collective-permute-start | bytes 294920 | tf_op jit(solution)/shard_map/ppermute | solution.py:46
  77.9 4.1 %collective-permute-start.23 = (f32[1,10,8,128]{3,2,1,0:T(8,128)S(1)}, f32[1,10,8,128]{3,2,1,0:T(8,128)S(1)}, u32[]{:S(2)}, u32[]{:S(2)}) collective-permute-start(f32[1,10,8,128]{3,2,1,0:T(8,128)S(1)} %get-tuple-element.71), channel_id=1, source_target_pairs={{0,6},{8,10},{16,22},{24,26},{32,38},{40,42},{48,54},{56,58},{2,4}... | collective-permute-start | bytes 122888 | tf_op jit(solution)/shard_map/ppermute | solution.py:46
  81.4 3.8 %collective-permute-start.7 = (f32[1,12,8,128]{3,2,1,0:T(8,128)S(1)}, f32[1,12,8,128]{3,2,1,0:T(8,128)S(1)}, u32[]{:S(2)}, u32[]{:S(2)}) collective-permute-start(f32[1,12,8,128]{3,2,1,0:T(8,128)S(1)} %get-tuple-element.69), channel_id=1, source_target_pairs={{0,48},{8,24},{16,32},{24,8},{32,16},{40,56},{48,0},{56,40},{2,50}... | collective-permute-start | bytes 147464 | tf_op jit(solution)/shard_map/ppermute | solution.py:46
  82.0 3.1 %collective-permute-start.15 = (f32[1,10,8,128]{3,2,1,0:T(8,128)S(1)}, f32[1,10,8,128]{3,2,1,0:T(8,128)S(1)}, u32[]{:S(2)}, u32[]{:S(2)}) collective-permute-start(f32[1,10,8,128]{3,2,1,0:T(8,128)S(1)} %get-tuple-element.73), channel_id=1, source_target_pairs={{0,65},{8,9},{16,81},{24,25},{32,97},{40,41},{48,113},{56,57},{2,6... | collective-permute-start | bytes 122888 | tf_op jit(solution)/shard_map/ppermute | solution.py:46
  87.3 18.2 %copy-start.1 = (f32[32,8,128]{2,1,0:T(8,128)S(1)}, f32[32,8,128]{2,1,0:T(8,128)}, u32[]{:S(2)}) copy-start(f32[32,8,128]{2,1,0:T(8,128)} %join.1.refs_0_) | copy-start | bytes 393220
  87.3 5.3 %collective-permute-start.24 = (f32[32,8,128]{2,1,0:T(8,128)}, f32[32,8,128]{2,1,0:T(8,128)S(1)}, u32[]{:S(2)}, u32[]{:S(2)}) collective-permute-start(f32[32,8,128]{2,1,0:T(8,128)} %join.1.refs_0_), channel_id=1, source_target_pairs={{0,1},{8,9},{16,17},{24,25},{32,33},{40,41},{48,49},{56,57},{2,3},... | collective-permute-start | bytes 393224 | tf_op jit(solution)/shard_map/ppermute | solution.py:46
  87.3 7.0 %collective-permute-start.25 = (f32[32,8,128]{2,1,0:T(8,128)}, f32[32,8,128]{2,1,0:T(8,128)S(1)}, u32[]{:S(2)}, u32[]{:S(2)}) collective-permute-start(f32[32,8,128]{2,1,0:T(8,128)} %join.1.refs_0_), channel_id=1, source_target_pairs={{0,2},{8,10},{16,18},{24,26},{32,34},{40,42},{48,50},{56,58},{2,0}... | collective-permute-start | bytes 393224 | tf_op jit(solution)/shard_map/ppermute | solution.py:46
  87.6 17.8 %collective-permute-start.26 = (f32[32,8,128]{2,1,0:T(8,128)}, f32[32,8,128]{2,1,0:T(8,128)S(1)}, u32[]{:S(2)}, u32[]{:S(2)}) collective-permute-start(f32[32,8,128]{2,1,0:T(8,128)} %join.1.refs_0_), channel_id=1, source_target_pairs={{0,3},{8,11},{16,19},{24,27},{32,35},{40,43},{48,51},{56,59},{2,1}... | collective-permute-start | bytes 393224 | tf_op jit(solution)/shard_map/ppermute | solution.py:46
  90.0 15.5 %collective-permute-start.27 = (f32[32,8,128]{2,1,0:T(8,128)}, f32[32,8,128]{2,1,0:T(8,128)S(1)}, u32[]{:S(2)}, u32[]{:S(2)}) collective-permute-start(f32[32,8,128]{2,1,0:T(8,128)} %join.1.refs_0_), channel_id=1, source_target_pairs={{0,4},{8,12},{16,20},{24,28},{32,36},{40,44},{48,52},{56,60},{2,6}... | collective-permute-start | bytes 393224 | tf_op jit(solution)/shard_map/ppermute | solution.py:46
  92.3 13.1 %collective-permute-start.28 = (f32[32,8,128]{2,1,0:T(8,128)}, f32[32,8,128]{2,1,0:T(8,128)S(1)}, u32[]{:S(2)}, u32[]{:S(2)}) collective-permute-start(f32[32,8,128]{2,1,0:T(8,128)} %join.1.refs_0_), channel_id=1, source_target_pairs={{0,5},{8,13},{16,21},{24,29},{32,37},{40,45},{48,53},{56,61},{2,7}... | collective-permute-start | bytes 393224 | tf_op jit(solution)/shard_map/ppermute | solution.py:46
  92.7 12.8 %collective-permute-start.29 = (f32[32,8,128]{2,1,0:T(8,128)}, f32[32,8,128]{2,1,0:T(8,128)S(1)}, u32[]{:S(2)}, u32[]{:S(2)}) collective-permute-start(f32[32,8,128]{2,1,0:T(8,128)} %join.1.refs_0_), channel_id=1, source_target_pairs={{0,6},{8,14},{16,22},{24,30},{32,38},{40,46},{48,54},{56,62},{2,4}... | collective-permute-start | bytes 393224 | tf_op jit(solution)/shard_map/ppermute | solution.py:46
  94.3 11.2 %collective-permute-start.30 = (f32[32,8,128]{2,1,0:T(8,128)}, f32[32,8,128]{2,1,0:T(8,128)S(1)}, u32[]{:S(2)}, u32[]{:S(2)}) collective-permute-start(f32[32,8,128]{2,1,0:T(8,128)} %join.1.refs_0_), channel_id=1, source_target_pairs={{0,7},{8,15},{16,23},{24,31},{32,39},{40,47},{48,55},{56,63},{2,5}... | collective-permute-start | bytes 393224 | tf_op jit(solution)/shard_map/ppermute | solution.py:46
  108.9 11.9 %collective-permute-start.31 = (f32[64,512]{1,0:T(8,128)S(1)}, f32[64,512]{1,0:T(8,128)S(1)}, u32[]{:S(2)}, u32[]{:S(2)}) collective-permute-start(f32[64,512]{1,0:T(8,128)S(1)} %rows.1), channel_id=1, source_target_pairs={{0,8},{8,0},{16,24},{24,16},{32,40},{40,32},{48,56},{56,48},{2,10}... | collective-permute-start | bytes 393224 | tf_op jit(solution)/shard_map/ppermute | solution.py:46
  120.8 26.0 %copy-start.4 = (f32[2,64,512]{2,1,0:T(8,128)}, f32[2,64,512]{2,1,0:T(8,128)S(1)}, u32[]{:S(2)}) copy-start(f32[2,64,512]{2,1,0:T(8,128)S(1)} %pad_maximum_fusion.pair_ref) | copy-start | bytes 786436
  120.8 9.0 %collective-permute-start.33 = (f32[2,64,512]{2,1,0:T(8,128)S(1)}, f32[2,64,512]{2,1,0:T(8,128)S(1)}, u32[]{:S(2)}, u32[]{:S(2)}) collective-permute-start(f32[2,64,512]{2,1,0:T(8,128)S(1)} %pad_maximum_fusion.pair_ref), channel_id=1, source_target_pairs={{0,16},{8,88},{16,0},{24,72},{32,48},{40,120},{48,32},{56,104},{2,... | collective-permute-start | bytes 786440 | tf_op jit(solution)/shard_map/ppermute | solution.py:46
  121.5 13.3 %collective-permute-start.34 = (f32[2,64,512]{2,1,0:T(8,128)S(1)}, f32[2,64,512]{2,1,0:T(8,128)S(1)}, u32[]{:S(2)}, u32[]{:S(2)}) collective-permute-start(f32[2,64,512]{2,1,0:T(8,128)S(1)} %pad_maximum_fusion.pair_ref), channel_id=1, source_target_pairs={{0,32},{8,104},{16,48},{24,120},{32,0},{40,72},{48,16},{56,88},{2,... | collective-permute-start | bytes 786440 | tf_op jit(solution)/shard_map/ppermute | solution.py:46
  125.8 14.0 %collective-permute-start.35 = (f32[2,64,512]{2,1,0:T(8,128)S(1)}, f32[2,64,512]{2,1,0:T(8,128)S(1)}, u32[]{:S(2)}, u32[]{:S(2)}) collective-permute-start(f32[2,64,512]{2,1,0:T(8,128)S(1)} %pad_maximum_fusion.pair_ref), channel_id=1, source_target_pairs={{0,48},{8,120},{16,32},{24,104},{32,16},{40,88},{48,0},{56,72},{2,... | collective-permute-start | bytes 786440 | tf_op jit(solution)/shard_map/ppermute | solution.py:46
  127.7 12.7 %collective-permute-start.32 = (f32[64,512]{1,0:T(8,128)S(1)}, f32[64,512]{1,0:T(8,128)S(1)}, u32[]{:S(2)}, u32[]{:S(2)}) collective-permute-start(f32[64,512]{1,0:T(8,128)S(1)} %rows.1), channel_id=1, source_target_pairs={{0,64},{8,72},{16,80},{24,88},{32,96},{40,104},{48,112},{56,120},{... | collective-permute-start | bytes 393224 | tf_op jit(solution)/shard_map/ppermute | solution.py:46
  129.8 17.0 %copy-start.5 = (f32[2,64,512]{2,1,0:T(8,128)}, f32[2,64,512]{2,1,0:T(8,128)S(1)}, u32[]{:S(2)}) copy-start(f32[2,64,512]{2,1,0:T(8,128)S(1)} %collective-permute-done.33.p1) | copy-start | bytes 786436
  129.8 17.0 %collective-permute-start.37 = (f32[2,64,512]{2,1,0:T(8,128)S(1)}, f32[2,64,512]{2,1,0:T(8,128)S(1)}, u32[]{:S(2)}, u32[]{:S(2)}) collective-permute-start(f32[2,64,512]{2,1,0:T(8,128)S(1)} %collective-permute-done.33.p1), channel_id=1, source_target_pairs={{0,8},{8,0},{16,24},{24,16},{32,40},{40,32},{48,56},{56,48},{2,10}... | collective-permute-start | bytes 786440 | tf_op jit(solution)/shard_map/ppermute | solution.py:46
  134.8 12.0 %copy-start.6 = (f32[2,64,512]{2,1,0:T(8,128)}, f32[2,64,512]{2,1,0:T(8,128)S(1)}, u32[]{:S(2)}) copy-start(f32[2,64,512]{2,1,0:T(8,128)S(1)} %collective-permute-done.34.p2) | copy-start | bytes 786436
  134.8 12.1 %collective-permute-start.38 = (f32[2,64,512]{2,1,0:T(8,128)S(1)}, f32[2,64,512]{2,1,0:T(8,128)S(1)}, u32[]{:S(2)}, u32[]{:S(2)}) collective-permute-start(f32[2,64,512]{2,1,0:T(8,128)S(1)} %collective-permute-done.34.p2), channel_id=1, source_target_pairs={{0,8},{8,0},{16,24},{24,16},{32,40},{40,32},{48,56},{56,48},{2,10}... | collective-permute-start | bytes 786440 | tf_op jit(solution)/shard_map/ppermute | solution.py:46
  139.8 7.0 %copy-start.7 = (f32[2,64,512]{2,1,0:T(8,128)}, f32[2,64,512]{2,1,0:T(8,128)S(1)}, u32[]{:S(2)}) copy-start(f32[2,64,512]{2,1,0:T(8,128)S(1)} %collective-permute-done.35.p3) | copy-start | bytes 786436
  139.8 7.1 %collective-permute-start.39 = (f32[2,64,512]{2,1,0:T(8,128)S(1)}, f32[2,64,512]{2,1,0:T(8,128)S(1)}, u32[]{:S(2)}, u32[]{:S(2)}) collective-permute-start(f32[2,64,512]{2,1,0:T(8,128)S(1)} %collective-permute-done.35.p3), channel_id=1, source_target_pairs={{0,8},{8,0},{16,24},{24,16},{32,40},{40,32},{48,56},{56,48},{2,10}... | collective-permute-start | bytes 786440 | tf_op jit(solution)/shard_map/ppermute | solution.py:46
  140.3 6.5 %copy-start.11 = (f32[64,512]{1,0:T(8,128)}, f32[64,512]{1,0:T(8,128)S(1)}, u32[]{:S(2)}) copy-start(f32[64,512]{1,0:T(8,128)S(1)} %collective-permute-done.32.p0) | copy-start | bytes 393220
  140.3 6.5 %collective-permute-start.36 = (f32[64,512]{1,0:T(8,128)S(1)}, f32[64,512]{1,0:T(8,128)S(1)}, u32[]{:S(2)}, u32[]{:S(2)}) collective-permute-start(f32[64,512]{1,0:T(8,128)S(1)} %collective-permute-done.32.p0), channel_id=1, source_target_pairs={{0,8},{8,0},{16,24},{24,16},{32,40},{40,32},{48,56},{56,48},{2,10}... | collective-permute-start | bytes 393224 | tf_op jit(solution)/shard_map/ppermute | solution.py:46
  (8 other events, 8.0 us)

commit v2 on v1

v2 whole, which is shorter than its diff:
```python
import functools

import jax
import jax.numpy as jnp
from jax import lax
from jax.experimental import pallas as pl
from jax.experimental.pallas import tpu as pltpu
from jax.sharding import Mesh, PartitionSpec as P

AXES = ("xh", "z", "core", "y", "xl")
SIZES = (2, 4, 2, 4, 2)
DECAY = 0.95
ORDER = 512
ROWS = 64
VMEM_LIMIT = 20 * 1024 * 1024
SMALL_LIMIT = 8 * 1024 * 1024
STREAM_TILES = (range(0, 11), range(11, 22), range(22, 32))


def index_of(x, y, z, c):
    return ((((x >> 1) * 4 + z) * 2 + c) * 4 + y) * 2 + (x & 1)


def permutation(move):
    return [
        (index_of(x, y, z, c), index_of(*move(x, y, z, c)))
        for x in range(4)
        for y in range(4)
        for z in range(4)
        for c in range(2)
    ]


def axis_move(axis, masks):
    def move(x, y, z, c):
        place = [x, y, z]
        place[axis] ^= masks[c]
        return (*place, c)

    return permutation(move)


CORE_SWAP = permutation(lambda x, y, z, c: (x, y, z, 1 - c))


FLIP = (0, 0, 1)


def member(axis, core, coset, bit):
    variant = core ^ FLIP[axis]
    return (1 - variant) * ((bit << 1) | (bit ^ coset)) + variant * ((coset << 1) | bit)


def coset_of(axis, core, position):
    variant = core ^ FLIP[axis]
    return (1 - variant) * ((position ^ (position >> 1)) & 1) + variant * (position >> 1)


def first_masks(axis):
    return tuple(1 + 2 * (core ^ FLIP[axis]) for core in range(2))


BITS = (0, 1)
CUBES = [
    [
        index_of(member(0, c, qx, vx), member(1, c, qy, vy), member(2, c, qz, vz), c)
        for vx in BITS
        for vy in BITS
        for vz in BITS
    ]
    for c in BITS
    for qx in BITS
    for qy in BITS
    for qz in BITS
]


def send(value, pairs):
    return lax.ppermute(value, AXES, pairs)


def place():
    xl = lax.axis_index("xl")
    x = lax.axis_index("xh") * 2 + xl
    return x, lax.axis_index("y"), lax.axis_index("z"), lax.axis_index("core")


def split(value):
    high = value.astype(jnp.bfloat16)
    low = (value - high.astype(jnp.float32)).astype(jnp.bfloat16)
    return high, low


def product(first, second, dims=((1,), (0,))):
    fh, fl = first
    sh, sl = second

    def dot(a, b):
        return lax.dot_general(a, b, (dims, ((), ())), preferred_element_type=jnp.float32)

    return dot(fh, sh) + (dot(fh, sl) + dot(fl, sh))


NT = ((1,), (1,))
TN = ((0,), (0,))


def pack_kernel(parts, table_ref, blocks, *rest):
    extra, outs = rest[: -len(parts)], rest[-len(parts) :]
    if extra:
        roots_kernel(*extra)
    here = [table_ref[16 + i] for i in range(3)]
    c = table_ref[19]
    targets = [c if own else 1 - c for own, _, _ in parts]
    cosets = [[coset_of(i, target, here[i]) for i in range(3)] for target in targets]

    def body(k, carry):
        for (_, half, streams), target, coset, out in zip(parts, targets, cosets, outs):
            offset = STREAM_TILES[streams[0]][0]
            for stream in streams:
                flips = [0, 0, 0]
                flips[stream] = half
                flips[(stream + 1) % 3] = (k >> 4) & 1
                flips[(stream + 2) % 3] = (k >> 3) & 1
                xd, yd, zd = (
                    member(i, target, coset[i] ^ flips[i], (k >> (2 - i)) & 1) for i in range(3)
                )
                block = table_ref[((xd >> 1) * 4 + zd) * 2 + target]
                row = (yd * 2 + (xd & 1)) * ROWS
                tiles = STREAM_TILES[stream]
                for pair in range(tiles[0] // 2, tiles[-1] // 2 + 1):
                    start = pl.multiple_of(row + (pair // 4) * 16, 16)
                    col = (pair % 4) * 128
                    value = blocks[0, block, pl.ds(start, 16), col : col + 128]
                    value = value.astype(jnp.float32)
                    for i in range(2):
                        if 2 * pair + i in tiles:
                            out[k, 2 * pair + i - offset] = value[8 * i : 8 * i + 8]
        return carry

    count = sum(len(streams) for _, _, streams in parts)
    lax.fori_loop(0, 32, body, 0, unroll=4 if count == 1 else 1)


def pack(name, parts, table, grads, matrices=()):
    extra = [jax.ShapeDtypeStruct((ORDER, ORDER), kind) for kind in ROOT_KINDS] if matrices else []
    packed = [
        jax.ShapeDtypeStruct((32, sum(len(STREAM_TILES[s]) for s in streams), 8, 128), jnp.float32)
        for _, _, streams in parts
    ]
    return pl.pallas_call(
        functools.partial(pack_kernel, parts),
        out_shape=extra + packed,
        in_specs=[pl.BlockSpec(memory_space=pltpu.SMEM)] + whole(1 + len(matrices)),
        out_specs=whole(len(extra) + len(parts)),
        compiler_params=pltpu.CompilerParams(vmem_limit_bytes=VMEM_LIMIT),
        name=name,
    )(table, grads, *matrices)


def cost(products, moved):
    return pl.CostEstimate(
        flops=6 * products * ORDER**3, bytes_accessed=moved, transcendentals=0
    )


HALF, FULL = jnp.bfloat16, jnp.float32
ROOT_KINDS = (FULL, HALF, HALF, FULL, HALF, HALF, HALF, HALF)


def roots_kernel(ls_ref, rs_ref, lr_ref, rr_ref, *outs):
    for stat_ref, root_ref, refs in ((ls_ref, lr_ref, outs[:3]), (rs_ref, rr_ref, outs[3:])):
        root = root_ref[0]
        parts = split(root)
        square = split(product(parts, parts))
        fourth = split(product(square, square))
        fifth = product(parts, fourth)
        base = 1.25 * root - (DECAY / 4.0) * product(split(fifth), split(stat_ref[0]))
        refs[0][...] = base
        refs[1][...], refs[2][...] = split(fifth * ((1.0 - DECAY) / 4.0))
        if len(refs) > 3:
            refs[3][...], refs[4][...] = split(base)


def whole(count):
    return [pl.BlockSpec(memory_space=pltpu.VMEM)] * count


def join_kernel(k0, r0, k1, r1, k2, r2, out):
    for tiles, kept, got in zip(STREAM_TILES, (k0, k1, k2), (r0, r1, r2)):
        out[:, tiles[0] : tiles[-1] + 1] = kept[...] + got[...]


def join(pieces):
    return pl.pallas_call(
        join_kernel,
        out_shape=jax.ShapeDtypeStruct((8, 32, 8, 128), jnp.float32),
        in_specs=whole(6),
        out_specs=pl.BlockSpec(memory_space=pltpu.VMEM),
        compiler_params=pltpu.CompilerParams(vmem_limit_bytes=SMALL_LIMIT),
        name="join",
    )(*pieces)


def total_kernel(parts, out):
    value = parts[0]
    for i in range(1, 8):
        value = value + parts[i]
    for i in range(8):
        out[i] = value


def total(parts):
    return pl.pallas_call(
        total_kernel,
        out_shape=jax.ShapeDtypeStruct((8, 32, 8, 128), jnp.float32),
        in_specs=whole(1),
        out_specs=pl.BlockSpec(memory_space=pltpu.VMEM),
        compiler_params=pltpu.CompilerParams(vmem_limit_bytes=SMALL_LIMIT),
        name="total",
    )(parts)


def assemble(pieces, grad):
    for n in range(8):
        for pair in range(16):
            row = n * ROWS + (pair // 4) * 16
            col = (pair % 4) * 128
            grad[row : row + 16, col : col + 128] = pieces[n, 2 * pair : 2 * pair + 2].reshape(16, 128)


def rows_kernel(table_ref, pieces, lc, lkh, lkl, rkh, rkl, rch, rcl, out, grad):
    assemble(pieces, grad)
    g = split(grad[...])
    rows = pl.ds(pl.multiple_of(table_ref[20] * ROWS, ROWS), ROWS)
    inner = product((lkh[rows, :], lkl[rows, :]), g)
    left = lc[rows, :] - product(split(inner), g, NT)
    turned = split(product(split(left), g))
    inner = product(turned, (rkh[...], rkl[...]))
    inner = product(split(inner), g, NT)
    out[...] = product(turned, (rch[...], rcl[...])) - product(split(inner), g)


def precondition_rows(table, pieces, constants):
    return pl.pallas_call(
        rows_kernel,
        out_shape=jax.ShapeDtypeStruct((ROWS, ORDER), jnp.float32),
        in_specs=[pl.BlockSpec(memory_space=pltpu.SMEM)] + whole(8),
        out_specs=pl.BlockSpec(memory_space=pltpu.VMEM),
        scratch_shapes=[pltpu.VMEM((ORDER, ORDER), jnp.float32)],
        compiler_params=pltpu.CompilerParams(vmem_limit_bytes=VMEM_LIMIT),
        name="rows",
    )(table, pieces, *constants[:3], *constants[4:])


def stats_kernel(pieces, lc, lkh, lkl, rc, rkh, rkl, ls, rs, ln, rn, li, ri, grad):
    assemble(pieces, grad)
    g = split(grad[...])
    for dims, stat_ref, c_ref, kh, kl, new_ref, inv_ref in (
        (NT, ls, lc, lkh, lkl, ln, li),
        (TN, rs, rc, rkh, rkl, rn, ri),
    ):
        gram = product(g, g, dims)
        new_ref[0] = DECAY * stat_ref[0] + (1.0 - DECAY) * gram
        inv_ref[0] = c_ref[...] - product((kh[...], kl[...]), split(gram))


def statistics(pieces, constants, left_stat, right_stat):
    return pl.pallas_call(
        stats_kernel,
        out_shape=[jax.ShapeDtypeStruct((1, ORDER, ORDER), jnp.float32)] * 4,
        in_specs=whole(9),
        out_specs=whole(4),
        scratch_shapes=[pltpu.VMEM((ORDER, ORDER), jnp.float32)],
        compiler_params=pltpu.CompilerParams(vmem_limit_bytes=VMEM_LIMIT),
        cost_estimate=cost(4, 11 << 20),
        name="stats",
    )(pieces, *constants[:6], left_stat, right_stat)


def spread_kernel(table_ref, pair_ref, p0, p1, p2, p3, q0, q1, q2, q3, out, sems):
    xh, z, c = table_ref[16] >> 1, table_ref[18], table_ref[19]
    copies = []

    def put(src, xd, zd, cd):
        slot = (xd * 4 + zd) * 2 + cd
        copies.append(pltpu.make_async_copy(src, out.at[table_ref[slot]], sems.at[len(copies)]))

    for i in range(2):
        put(pair_ref.at[i], xh, z, c ^ i)
    put(p0, xh ^ 1, z, c)
    put(q0, xh ^ 1, z, 1 - c)
    for holder, group in ((c, (p1, p2, p3)), (1 - c, (q1, q2, q3))):
        for j, ref in enumerate(group):
            for i in range(2):
                put(ref.at[i], xh ^ holder, z ^ (j + 1), holder ^ i)
    for copy in copies:
        copy.start()
    for copy in copies:
        copy.wait()


def spread(table, pieces):
    return pl.pallas_call(
        spread_kernel,
        out_shape=jax.ShapeDtypeStruct((16, ROWS, ORDER), jnp.float32),
        in_specs=[pl.BlockSpec(memory_space=pltpu.SMEM)] + whole(9),
        out_specs=pl.BlockSpec(memory_space=pl.ANY),
        scratch_shapes=[pltpu.SemaphoreType.DMA((16,))],
        compiler_params=pltpu.CompilerParams(vmem_limit_bytes=SMALL_LIMIT),
        name="spread",
    )(table, *pieces)


def local(replica_grads, owner_table, left_stat, right_stat, left_root, right_root):
    x, y, z, c = place()
    slots = jnp.arange(16, dtype=jnp.int32)
    block_of_slot = jnp.sum(
        jnp.where(owner_table[None, :] == slots[:, None], slots[None, :], 0), axis=1
    )
    coords = jnp.stack([x, y, z, c, y * 2 + (x & 1)]).astype(jnp.int32)
    table = jnp.concatenate([block_of_slot, coords])
    streams = range(3)
    everything = tuple(streams)
    (first,) = pack("other0", [(False, 1, (0,))], table, replica_grads)
    table, first = lax.optimization_barrier((table, first))
    later = pack("other12", [(False, 1, (1,)), (False, 1, (2,))], table, replica_grads)
    table, later = lax.optimization_barrier((table, later))
    arrived = [send(value, CORE_SWAP) for value in (first, *later)]
    *mine, other = pack(
        "own", [(True, 1, (s,)) for s in streams] + [(False, 0, everything)], table, replica_grads
    )
    outgoing = [mine[s] + arrived[s] for s in streams]
    other, outgoing = lax.optimization_barrier((other, outgoing))
    table, other = lax.optimization_barrier((table, other))
    *constants, mine = pack(
        "keep",
        [(True, 0, everything)],
        table,
        replica_grads,
        (left_stat, right_stat, left_root, right_root),
    )
    arrived = send(other, CORE_SWAP)
    kept = [
        mine[:, tiles[0] : tiles[-1] + 1] + arrived[:, tiles[0] : tiles[-1] + 1]
        for tiles in STREAM_TILES
    ]
    tails = [None] * 3
    for step in range(3):
        for s in streams:
            axis = (s + step) % 3
            got = send(outgoing[s], axis_move(axis, first_masks(axis)))
            if step == 2:
                tails[s] = (kept[s], got)
                continue
            half = kept[s].shape[0] // 2
            outgoing[s] = kept[s][half:] + got[half:]
            kept[s] = kept[s][:half] + got[:half]
    joined = join([value for pair in tails for value in pair])
    parts = lax.all_to_all(joined, AXES, 0, 0, axis_index_groups=CUBES, tiled=True)
    pieces = lax.all_to_all(total(parts), ("y", "xl"), 0, 0, tiled=True)
    rows = precondition_rows(table, pieces, constants)
    both = jnp.stack([rows, send(rows, CORE_SWAP)])
    got = [None] * 4
    for j in (2, 1, 3):
        got[j] = send(both, permutation(lambda x, y, z, c, j=j: (x ^ (2 * c), y, z ^ j, c)))
    got[0] = send(rows, axis_move(0, (2, 2)))
    stats = statistics(pieces, constants, left_stat, right_stat)
    got, stats = lax.optimization_barrier((got, stats))
    swapped = [send(value, CORE_SWAP) for value in got]
    directions = spread(table, [both] + got + swapped)
    return (directions, *stats)


def solution(mesh):
    fine = Mesh(mesh.devices.reshape(SIZES), AXES)
    wide = ("xh", "z", "core")
    narrow = ("y", "xl")
    slot = P(wide, None, None)
    return jax.shard_map(
        local,
        mesh=fine,
        in_specs=(P(wide + narrow, None, None, None), P(), slot, slot, slot, slot),
        out_specs=(P(None, narrow, None), slot, slot, slot, slot),
        check_vma=False,
    )
```

time: 214 us -> 126 us (0.59)
  Pallas kernels: 103 us -> 26.8 us
  blocking collectives: 0 us -> 32 us
  starting transfers between devices: 60.9 us -> 39.8 us
  waiting for transfers between devices: 33.8 us -> 19.8 us
  other arithmetic: 12.7 us -> 2.48 us
    pallas_call x1, Pallas kernels: 65.5 us -> 1.99 us  [spread(): pl.pallas_call(spread_kernel, out_shape=jax.ShapeDtypeStruct((16, ROWS, O...]
    all_to_all x0 -> x2, blocking collectives: none -> 32 us  [the longest x1 16 us: local(): lax.all_to_all(joined, AXES, 0, 0, axis_index_groups=CUBES, tiled=True)]
    ppermute x40 -> x22, starting transfers between devices: 60.9 us -> 39.8 us  [send(): return lax.ppermute(value, AXES, pairs)]
    ppermute x40 -> x22, waiting for transfers between devices: 33.8 us -> 19.8 us  [send(): return lax.ppermute(value, AXES, pairs)]
    pallas_call x6, Pallas kernels: 27.4 us -> 16.8 us  [the longest x4 16.6 us: pack(): pl.pallas_call(functools.partial(pack_kernel, parts), out_shape=extra + p...]
    add x6 -> x5, other arithmetic: 7.19 us -> 0.97 us  [the longest x2 0.54 us: local(): mine[:, tiles[0]:tiles[-1] + 1] + arrived[:, tiles[0]:tiles[-1] + 1]]
    add x12 -> x3, other arithmetic: 3.59 us -> 0.47 us  [local(): kept[s] = kept[s][:half] + got[:half]]
  transfers between devices with their start and end apart: 40 -> 22, of which waited for: 14 -> 8; matrix products, arithmetic and copies ran while one was open for 6% -> 1% of each run, Pallas kernels for 13% -> 15%
where the time goes in v2:
time: 126 us; the launch traced here: 125 us
  starting transfers between devices  39.8 us (32%)
  blocking collectives  32 us (25%)
  Pallas kernels  26.8 us (21%)
  waiting for transfers between devices  19.8 us (16%)
  local copies, waits for them, and re-layouts  3.5 us (3%)
  other arithmetic  2.48 us (2%)
    ppermute x22, starting transfers between devices, send(): return lax.ppermute(value, AXES, pairs)  39.8 us
    ppermute x22, waiting for transfers between devices, send(): return lax.ppermute(value, AXES, pairs)  19.8 us
    pallas_call x4, Pallas kernels, pack(): pl.pallas_call(functools.partial(pack_kernel, parts), out_shape=extra + p...  16.6 us
    all_to_all x1, blocking collectives, local(): lax.all_to_all(joined, AXES, 0, 0, axis_index_groups=CUBES, tiled=True)  16 us
    all_to_all x1, blocking collectives, local(): pieces = lax.all_to_all(total(parts), ('y', 'xl'), 0, 0, tiled=True)  16 us
    pallas_call x1, Pallas kernels, statistics(): pl.pallas_call(stats_kernel, out_shape=[jax.ShapeDtypeStruct((1, ORDER, O...  4.77 us
    unnamed x10, local copies, waits for them, and re-layouts  3.41 us
    pallas_call x1, Pallas kernels, precondition_rows(): pl.pallas_call(rows_kernel, out_shape=jax.ShapeDtypeStruct((ROWS, ORDER),...  3.25 us
  transfers between devices with their start and end apart: 22, of which 8 were waited for; matrix products, arithmetic and copies ran while one was open for 1% of the time, Pallas kernels for 15%

profile of v2, /device:TPU:1, one launch (start us, length us, event | category | flops | bytes accessed | tf_op | source)
XLA Modules:
  0.0 125.4 jit_solution(3010347386884624291)
XLA Ops:
  0.6 0.8 select_reduce_fusion
  1.5 3.4 %copy-done = bf16[1,16,512,512]{3,2,1,0:T(8,128)(2,1)S(1)} copy-done((bf16[1,16,512,512]{3,2,1,0:T(8,128)(2,1)S(1)}, bf16[1,16,512,512]{3,2,1,0:T(8,128)(2,1)}, u32[]{:S(2)}) %copy-start) | copy-done | bytes 8388632
  4.9 1.1 other0.1
  6.0 1.8 %other12.1 = (f32[32,11,8,128]{3,2,1,0:T(8,128)S(1)}, f32[32,10,8,128]{3,2,1,0:T(8,128)S(1)}) custom-call(s32[21]{0:T(128)S(1)} %concatenate.3.table_ref, bf16[1,16,512,512]{3,2,1,0:T(8,128)(2,1)S(1)} %copy-done), custom_call_target="tpu_custom_call" | custom-call | tf_op jit(solution)/shard_map/other12/pallas_call | solution.py:151
  7.9 1.5 %collective-permute-start.1 = (f32[32,11,8,128]{3,2,1,0:T(8,128)S(1)}, f32[32,11,8,128]{3,2,1,0:T(8,128)S(1)}, u32[]{:S(2)}, u32[]{:S(2)}) collective-permute-start(f32[32,11,8,128]{3,2,1,0:T(8,128)S(1)} %get-tuple-element.51), channel_id=1, source_target_pairs={{0,8},{8,0},{16,24},{24,16},{32,40},{40,32},{48,56},{56,48},{2,10}... | collective-permute-start | bytes 4325384 | tf_op jit(solution)/shard_map/ppermute | solution.py:79
  9.5 0.4 collective-permute-start.2
  9.9 3.8 %own.1 = (f32[32,11,8,128]{3,2,1,0:T(8,128)S(1)}, f32[32,11,8,128]{3,2,1,0:T(8,128)S(1)}, f32[32,10,8,128]{3,2,1,0:T(8,128)S(1)}, f32[32,32,8,128]{3,2,1,0:T(8,128)S(1)}) custom-call(s32[21]{0:T(128)S(1)} %concatenate.3.table_ref, bf16[1,16,512,512]{3,2,1,0:T(8,128)(2,1)S(1)} %copy-done), custom_call_target="tpu_custom_call" | custom-call | tf_op jit(solution)/shard_map/own/pallas_call | solution.py:151
  13.7 2.4 %collective-permute-done.2 = f32[32,10,8,128]{3,2,1,0:T(8,128)S(1)} collective-permute-done((f32[32,10,8,128]{3,2,1,0:T(8,128)S(1)}, f32[32,10,8,128]{3,2,1,0:T(8,128)S(1)}, u32[]{:S(2)}, u32[]{:S(2)}) %collective-permute-start.2) | collective-permute-done | bytes 1310752 | tf_op jit(solution)/shard_map/ppermute | solution.py:79
  16.2 0.1 add.64
  16.3 0.1 add.63
  16.5 0.1 add.62
  16.7 0.5 collective-permute-start.3
  17.1 2.6 %collective-permute-start.4 = (f32[32,11,8,128]{3,2,1,0:T(8,128)S(1)}, f32[32,11,8,128]{3,2,1,0:T(8,128)S(1)}, u32[]{:S(2)}, u32[]{:S(2)}) collective-permute-start(f32[32,11,8,128]{3,2,1,0:T(8,128)S(1)} %add.62), channel_id=1, source_target_pairs={{0,1},{8,73},{16,17},{24,89},{32,33},{40,105},{48,49},{56,121},{2,... | collective-permute-start | bytes 4325384 | tf_op jit(solution)/shard_map/ppermute | solution.py:79
  19.7 2.7 %collective-permute-start.7 = (f32[32,11,8,128]{3,2,1,0:T(8,128)S(1)}, f32[32,11,8,128]{3,2,1,0:T(8,128)S(1)}, u32[]{:S(2)}, u32[]{:S(2)}) collective-permute-start(f32[32,11,8,128]{3,2,1,0:T(8,128)S(1)} %add.63), channel_id=1, source_target_pairs={{0,2},{8,14},{16,18},{24,30},{32,34},{40,46},{48,50},{56,62},{2,0}... | collective-permute-start | bytes 4325384 | tf_op jit(solution)/shard_map/ppermute | solution.py:79
  22.4 1.6 %collective-permute-start.10 = (f32[32,10,8,128]{3,2,1,0:T(8,128)S(1)}, f32[32,10,8,128]{3,2,1,0:T(8,128)S(1)}, u32[]{:S(2)}, u32[]{:S(2)}) collective-permute-start(f32[32,10,8,128]{3,2,1,0:T(8,128)S(1)} %add.64), channel_id=1, source_target_pairs={{0,48},{8,24},{16,32},{24,8},{32,16},{40,56},{48,0},{56,40},{2,50}... | collective-permute-start | bytes 3932168 | tf_op jit(solution)/shard_map/ppermute | solution.py:79
  24.1 9.8 %keep.1 = (f32[512,512]{1,0:T(8,128)S(1)}, bf16[512,512]{1,0:T(8,128)(2,1)S(1)}, bf16[512,512]{1,0:T(8,128)(2,1)S(1)}, f32[512,512]{1,0:T(8,128)S(1)}, bf16[512,...) custom-call(s32[21]{0:T(128)S(1)} %concatenate.3.table_ref, ...), custom_call_target="tpu_custom_call" | custom-call | tf_op jit(solution)/shard_map/keep/pallas_call | solution.py:151
  33.9 0.4 slice_add_fusion
  34.3 2.2 %collective-permute-done.4 = f32[32,11,8,128]{3,2,1,0:T(8,128)S(1)} collective-permute-done((f32[32,11,8,128]{3,2,1,0:T(8,128)S(1)}, f32[32,11,8,128]{3,2,1,0:T(8,128)S(1)}, u32[]{:S(2)}, u32[]{:S(2)}) %collective-permute-start.4) | collective-permute-done | bytes 1441824 | tf_op jit(solution)/shard_map/ppermute | solution.py:79
  36.5 0.1 slice_add_fusion.6
  36.6 2.9 %collective-permute-start.5 = (f32[16,11,8,128]{3,2,1,0:T(8,128)S(1)}, f32[16,11,8,128]{3,2,1,0:T(8,128)S(1)}, u32[]{:S(2)}, u32[]{:S(2)}) collective-permute-start(f32[16,11,8,128]{3,2,1,0:T(8,128)S(1)} %get-tuple-element.86), channel_id=1, source_target_pairs={{0,2},{8,14},{16,18},{24,30},{32,34},{40,46},{48,50},{56,62},{2,0}... | collective-permute-start | bytes 2162696 | tf_op jit(solution)/shard_map/ppermute | solution.py:79
  39.5 0.2 slice_add_fusion.4
  39.7 1.4 %collective-permute-start.8 = (f32[16,11,8,128]{3,2,1,0:T(8,128)S(1)}, f32[16,11,8,128]{3,2,1,0:T(8,128)S(1)}, u32[]{:S(2)}, u32[]{:S(2)}) collective-permute-start(f32[16,11,8,128]{3,2,1,0:T(8,128)S(1)} %get-tuple-element.84), channel_id=1, source_target_pairs={{0,48},{8,24},{16,32},{24,8},{32,16},{40,56},{48,0},{56,40},{2,50}... | collective-permute-start | bytes 2162696 | tf_op jit(solution)/shard_map/ppermute | solution.py:79
  41.1 0.2 slice_add_fusion.2
  41.3 0.1 slice_add_fusion.8
  41.5 2.6 %collective-permute-start.11 = (f32[16,10,8,128]{3,2,1,0:T(8,128)S(1)}, f32[16,10,8,128]{3,2,1,0:T(8,128)S(1)}, u32[]{:S(2)}, u32[]{:S(2)}) collective-permute-start(f32[16,10,8,128]{3,2,1,0:T(8,128)S(1)} %get-tuple-element.88), channel_id=1, source_target_pairs={{0,1},{8,73},{16,17},{24,89},{32,33},{40,105},{48,49},{56,121},{2,... | collective-permute-start | bytes 1966088 | tf_op jit(solution)/shard_map/ppermute | solution.py:79
  44.0 4.5 %collective-permute-done.5 = f32[16,11,8,128]{3,2,1,0:T(8,128)S(1)} collective-permute-done((f32[16,11,8,128]{3,2,1,0:T(8,128)S(1)}, f32[16,11,8,128]{3,2,1,0:T(8,128)S(1)}, u32[]{:S(2)}, u32[]{:S(2)}) %collective-permute-start.5) | collective-permute-done | bytes 720928 | tf_op jit(solution)/shard_map/ppermute | solution.py:79
  48.5 0.1 slice_add_fusion.11
  48.6 1.1 collective-permute-start.6
  49.7 0.5 collective-permute-done.8
  50.3 2.6 %collective-permute-start.9 = (f32[8,11,8,128]{3,2,1,0:T(8,128)S(1)}, f32[8,11,8,128]{3,2,1,0:T(8,128)S(1)}, u32[]{:S(2)}, u32[]{:S(2)}) collective-permute-start(f32[8,11,8,128]{3,2,1,0:T(8,128)S(1)} %get-tuple-element.89), channel_id=1, source_target_pairs={{0,1},{8,73},{16,17},{24,89},{32,33},{40,105},{48,49},{56,121},{2,... | collective-permute-start | bytes 1081352 | tf_op jit(solution)/shard_map/ppermute | solution.py:79
  53.0 2.3 %collective-permute-start.12 = (f32[8,10,8,128]{3,2,1,0:T(8,128)S(1)}, f32[8,10,8,128]{3,2,1,0:T(8,128)S(1)}, u32[]{:S(2)}, u32[]{:S(2)}) collective-permute-start(f32[8,10,8,128]{3,2,1,0:T(8,128)S(1)} %get-tuple-element.93), channel_id=1, source_target_pairs={{0,2},{8,14},{16,18},{24,30},{32,34},{40,46},{48,50},{56,62},{2,0}... | collective-permute-start | bytes 983048 | tf_op jit(solution)/shard_map/ppermute | solution.py:79
  55.2 5.0 %collective-permute-done.12.r2 = f32[8,10,8,128]{3,2,1,0:T(8,128)S(1)} collective-permute-done((f32[8,10,8,128]{3,2,1,0:T(8,128)S(1)}, f32[8,10,8,128]{3,2,1,0:T(8,128)S(1)}, u32[]{:S(2)}, u32[]{:S(2)}) %collective-permute-start.12) | collective-permute-done | bytes 327712 | tf_op jit(solution)/shard_map/ppermute | solution.py:79
  60.2 0.2 join.1
  60.3 16.0 %all_to_all.10.parts = f32[8,32,8,128]{3,2,1,0:T(8,128)S(1)} all-to-all(f32[8,32,8,128]{3,2,1,0:T(8,128)S(1)} %join.1), channel_id=1, replica_groups={{0,16,6,22,65,81,71,87},{32,48,38,54,97,113,103,119},{2,18,4,20,67,83,6..., dimensions={0} | all-to-all | bytes 2097152 | tf_op jit(solution)/shard_map/all_to_all | solution.py:360
  76.4 16.0 %all_to_all.11.pieces = f32[8,32,8,128]{3,2,1,0:T(8,128)S(1)} all-to-all(f32[8,32,8,128]{3,2,1,0:T(8,128)S(1)} %total.1), channel_id=1, replica_groups=mesh['xh'=2,'z'=4,'core'=2,'y'=4,'xl'=2] {'y','xl'}, dimensions={0} | all-to-all | bytes 2097152 | tf_op jit(solution)/shard_map/all_to_all | solution.py:361
  92.4 3.3 %rows.1 = f32[64,512]{1,0:T(8,128)S(1)} custom-call(s32[21]{0:T(128)S(1)} %concatenate.3.table_ref, f32[8,32,8,128]{3,2,1,0:T(8,128)S(1)} %all_to_all.11.pieces, f32[512,512]{1,0:T(8,128)S(1)} %get-tuple-element.61.lc, bf16[512,512]{1,0:T(8,128)(2,1)S(1)} %get-tuple-element.62.lkh, bf16[512,512]{1,0:T(8,128)(2,1)S(1)} %get-tuple-element.63.lkl, ...), custom_call_target="tpu_custom_call" | custom-call | tf_op jit(solution)/shard_map/rows/pallas_call | solution.py:245
  95.7 3.9 %collective-permute-start.13 = (f32[64,512]{1,0:T(8,128)S(1)}, f32[64,512]{1,0:T(8,128)S(1)}, u32[]{:S(2)}, u32[]{:S(2)}) collective-permute-start(f32[64,512]{1,0:T(8,128)S(1)} %rows.1), channel_id=1, source_target_pairs={{0,8},{8,0},{16,24},{24,16},{32,40},{40,32},{48,56},{56,48},{2,10}... | collective-permute-start | bytes 393224 | tf_op jit(solution)/shard_map/ppermute | solution.py:79
  99.6 1.9 %collective-permute-start.14 = (f32[64,512]{1,0:T(8,128)S(1)}, f32[64,512]{1,0:T(8,128)S(1)}, u32[]{:S(2)}, u32[]{:S(2)}) collective-permute-start(f32[64,512]{1,0:T(8,128)S(1)} %rows.1), channel_id=1, source_target_pairs={{0,64},{8,72},{16,80},{24,88},{32,96},{40,104},{48,112},{56,120},{... | collective-permute-start | bytes 393224 | tf_op jit(solution)/shard_map/ppermute | solution.py:79
  101.5 1.0 collective-permute-start.17
  102.6 2.4 %collective-permute-start.16 = (f32[2,64,512]{2,1,0:T(8,128)S(1)}, f32[2,64,512]{2,1,0:T(8,128)S(1)}, u32[]{:S(2)}, u32[]{:S(2)}) collective-permute-start(f32[2,64,512]{2,1,0:T(8,128)S(1)} %pad_maximum_fusion.pair_ref), channel_id=1, source_target_pairs={{0,32},{8,104},{16,48},{24,120},{32,0},{40,72},{48,16},{56,88},{2,... | collective-permute-start | bytes 786440 | tf_op jit(solution)/shard_map/ppermute | solution.py:79
  104.9 3.1 %collective-permute-start.15 = (f32[2,64,512]{2,1,0:T(8,128)S(1)}, f32[2,64,512]{2,1,0:T(8,128)S(1)}, u32[]{:S(2)}, u32[]{:S(2)}) collective-permute-start(f32[2,64,512]{2,1,0:T(8,128)S(1)} %pad_maximum_fusion.pair_ref), channel_id=1, source_target_pairs={{0,16},{8,88},{16,0},{24,72},{32,48},{40,120},{48,32},{56,104},{2,... | collective-permute-start | bytes 786440 | tf_op jit(solution)/shard_map/ppermute | solution.py:79
  108.1 4.8 %stats.1 = (f32[1,512,512]{2,1,0:T(8,128)}, f32[1,512,512]{2,1,0:T(8,128)}, f32[1,512,512]{2,1,0:T(8,128)}, f32[1,512,512]{2,1,0:T(8,128)}) custom-call(f32[8,32,8,128]{3,2,1,0:T(8,128)S(1)} %all_to_all.11.pieces, f32[512,512]{1,0:T(8,128)S(1)} %get-tuple-element.61.lc, bf16[512,512]{1,0:T(8,128)(2,1)S(1)} %get-tuple-element.62.lkh, ...), custom_call_target="tpu_custom_call" | custom-call | flops 3221225472 | bytes 11534336 | tf_op jit(solution)/shard_map/stats/pallas_call | solution.py:269
  112.9 2.1 %collective-permute-done.16.p2 = f32[2,64,512]{2,1,0:T(8,128)S(1)} collective-permute-done((f32[2,64,512]{2,1,0:T(8,128)S(1)}, f32[2,64,512]{2,1,0:T(8,128)S(1)}, u32[]{:S(2)}, u32[]{:S(2)}) %collective-permute-start.16) | collective-permute-done | bytes 262176 | tf_op jit(solution)/shard_map/ppermute | solution.py:79
  115.0 1.5 %collective-permute-done.15.p1 = f32[2,64,512]{2,1,0:T(8,128)S(1)} collective-permute-done((f32[2,64,512]{2,1,0:T(8,128)S(1)}, f32[2,64,512]{2,1,0:T(8,128)S(1)}, u32[]{:S(2)}, u32[]{:S(2)}) %collective-permute-start.15) | collective-permute-done | bytes 262176 | tf_op jit(solution)/shard_map/ppermute | solution.py:79
  116.4 4.7 %collective-permute-start.19 = (f32[2,64,512]{2,1,0:T(8,128)S(1)}, f32[2,64,512]{2,1,0:T(8,128)S(1)}, u32[]{:S(2)}, u32[]{:S(2)}) collective-permute-start(f32[2,64,512]{2,1,0:T(8,128)S(1)} %collective-permute-done.15.p1), channel_id=1, source_target_pairs={{0,8},{8,0},{16,24},{24,16},{32,40},{40,32},{48,56},{56,48},{2,10}... | collective-permute-start | bytes 786440 | tf_op jit(solution)/shard_map/ppermute | solution.py:79
  121.1 0.5 collective-permute-start.21
  121.6 1.6 %collective-permute-done.18.q0 = f32[64,512]{1,0:T(8,128)S(1)} collective-permute-done((f32[64,512]{1,0:T(8,128)S(1)}, f32[64,512]{1,0:T(8,128)S(1)}, u32[]{:S(2)}, u32[]{:S(2)}) %collective-permute-start.18) | collective-permute-done | bytes 131104 | tf_op jit(solution)/shard_map/ppermute | solution.py:79
  123.2 2.0 %spread.1 = f32[16,64,512]{2,1,0:T(8,128)} custom-call(s32[21]{0:T(128)S(1)} %concatenate.3.table_ref, f32[2,64,512]{2,1,0:T(8,128)S(1)} %pad_maximum_fusion.pair_ref, f32[64,512]{1,0:T(8,128)S(1)} %collective-permute-done.14.p0, f32[2,64,512]{2,1,0:T(8,128)S(1)} %collective-permute-done.15.p1, f32[2,64,512]{2,1,0:T(8,128)S(1)} %collective-permute-done.16.p2, ...), custom_call_target="tpu_custom_call" | custom-call | tf_op jit(solution)/shard_map/spread/pallas_call | solution.py:304
  (31 shorter events, 0.5 us)
Async XLA Ops:
  1.5 3.4 %copy-start = (bf16[1,16,512,512]{3,2,1,0:T(8,128)(2,1)S(1)}, bf16[1,16,512,512]{3,2,1,0:T(8,128)(2,1)}, u32[]{:S(2)}) copy-start(bf16[1,16,512,512]{3,2,1,0:T(8,128)(2,1)} %blocks.7) | copy-start | bytes 25165828
  7.9 8.4 %collective-permute-start.1 = (f32[32,11,8,128]{3,2,1,0:T(8,128)S(1)}, f32[32,11,8,128]{3,2,1,0:T(8,128)S(1)}, u32[]{:S(2)}, u32[]{:S(2)}) collective-permute-start(f32[32,11,8,128]{3,2,1,0:T(8,128)S(1)} %get-tuple-element.51), channel_id=1, source_target_pairs={{0,8},{8,0},{16,24},{24,16},{32,40},{40,32},{48,56},{56,48},{2,10}... | collective-permute-start | bytes 4325384 | tf_op jit(solution)/shard_map/ppermute | solution.py:79
  9.4 7.1 %collective-permute-start = (f32[32,11,8,128]{3,2,1,0:T(8,128)S(1)}, f32[32,11,8,128]{3,2,1,0:T(8,128)S(1)}, u32[]{:S(2)}, u32[]{:S(2)}) collective-permute-start(f32[32,11,8,128]{3,2,1,0:T(8,128)S(1)} %other0.1), channel_id=1, source_target_pairs={{0,8},{8,0},{16,24},{24,16},{32,40},{40,32},{48,56},{56,48},{2,10}... | collective-permute-start | bytes 4325384 | tf_op jit(solution)/shard_map/ppermute | solution.py:79
  9.5 6.7 %collective-permute-start.2 = (f32[32,10,8,128]{3,2,1,0:T(8,128)S(1)}, f32[32,10,8,128]{3,2,1,0:T(8,128)S(1)}, u32[]{:S(2)}, u32[]{:S(2)}) collective-permute-start(f32[32,10,8,128]{3,2,1,0:T(8,128)S(1)} %get-tuple-element.53), channel_id=1, source_target_pairs={{0,8},{8,0},{16,24},{24,16},{32,40},{40,32},{48,56},{56,48},{2,10}... | collective-permute-start | bytes 3932168 | tf_op jit(solution)/shard_map/ppermute | solution.py:79
  16.5 7.6 %copy-start.1 = (f32[1,512,512]{2,1,0:T(8,128)S(1)}, f32[1,512,512]{2,1,0:T(8,128)}, u32[]{:S(2)}) copy-start(f32[1,512,512]{2,1,0:T(8,128)} %rest_2_.1) | copy-start | bytes 3145732
  16.5 7.6 %copy-start.2 = (f32[1,512,512]{2,1,0:T(8,128)S(1)}, f32[1,512,512]{2,1,0:T(8,128)}, u32[]{:S(2)}) copy-start(f32[1,512,512]{2,1,0:T(8,128)} %rest_3_.1) | copy-start | bytes 3145732
  16.5 7.6 %copy-start.3 = (f32[1,512,512]{2,1,0:T(8,128)S(1)}, f32[1,512,512]{2,1,0:T(8,128)}, u32[]{:S(2)}) copy-start(f32[1,512,512]{2,1,0:T(8,128)} %ls.1) | copy-start | bytes 3145732
  16.5 7.6 %copy-start.4 = (f32[1,512,512]{2,1,0:T(8,128)S(1)}, f32[1,512,512]{2,1,0:T(8,128)}, u32[]{:S(2)}) copy-start(f32[1,512,512]{2,1,0:T(8,128)} %rs.1) | copy-start | bytes 3145732
  16.7 17.2 %collective-permute-start.3 = (f32[32,32,8,128]{3,2,1,0:T(8,128)S(1)}, f32[32,32,8,128]{3,2,1,0:T(8,128)S(1)}, u32[]{:S(2)}, u32[]{:S(2)}) collective-permute-start(f32[32,32,8,128]{3,2,1,0:T(8,128)S(1)} %get-tuple-element.57), channel_id=1, source_target_pairs={{0,8},{8,0},{16,24},{24,16},{32,40},{40,32},{48,56},{56,48},{2,10}... | collective-permute-start | bytes 12582920 | tf_op jit(solution)/shard_map/ppermute | solution.py:79
  17.1 19.4 %collective-permute-start.4 = (f32[32,11,8,128]{3,2,1,0:T(8,128)S(1)}, f32[32,11,8,128]{3,2,1,0:T(8,128)S(1)}, u32[]{:S(2)}, u32[]{:S(2)}) collective-permute-start(f32[32,11,8,128]{3,2,1,0:T(8,128)S(1)} %add.62), channel_id=1, source_target_pairs={{0,1},{8,73},{16,17},{24,89},{32,33},{40,105},{48,49},{56,121},{2,... | collective-permute-start | bytes 4325384 | tf_op jit(solution)/shard_map/ppermute | solution.py:79
  19.7 19.9 %collective-permute-start.7 = (f32[32,11,8,128]{3,2,1,0:T(8,128)S(1)}, f32[32,11,8,128]{3,2,1,0:T(8,128)S(1)}, u32[]{:S(2)}, u32[]{:S(2)}) collective-permute-start(f32[32,11,8,128]{3,2,1,0:T(8,128)S(1)} %add.63), channel_id=1, source_target_pairs={{0,2},{8,14},{16,18},{24,30},{32,34},{40,46},{48,50},{56,62},{2,0}... | collective-permute-start | bytes 4325384 | tf_op jit(solution)/shard_map/ppermute | solution.py:79
  22.4 18.9 %collective-permute-start.10 = (f32[32,10,8,128]{3,2,1,0:T(8,128)S(1)}, f32[32,10,8,128]{3,2,1,0:T(8,128)S(1)}, u32[]{:S(2)}, u32[]{:S(2)}) collective-permute-start(f32[32,10,8,128]{3,2,1,0:T(8,128)S(1)} %add.64), channel_id=1, source_target_pairs={{0,48},{8,24},{16,32},{24,8},{32,16},{40,56},{48,0},{56,40},{2,50}... | collective-permute-start | bytes 3932168 | tf_op jit(solution)/shard_map/ppermute | solution.py:79
  36.6 11.9 %collective-permute-start.5 = (f32[16,11,8,128]{3,2,1,0:T(8,128)S(1)}, f32[16,11,8,128]{3,2,1,0:T(8,128)S(1)}, u32[]{:S(2)}, u32[]{:S(2)}) collective-permute-start(f32[16,11,8,128]{3,2,1,0:T(8,128)S(1)} %get-tuple-element.86), channel_id=1, source_target_pairs={{0,2},{8,14},{16,18},{24,30},{32,34},{40,46},{48,50},{56,62},{2,0}... | collective-permute-start | bytes 2162696 | tf_op jit(solution)/shard_map/ppermute | solution.py:79
  39.7 10.5 %collective-permute-start.8 = (f32[16,11,8,128]{3,2,1,0:T(8,128)S(1)}, f32[16,11,8,128]{3,2,1,0:T(8,128)S(1)}, u32[]{:S(2)}, u32[]{:S(2)}) collective-permute-start(f32[16,11,8,128]{3,2,1,0:T(8,128)S(1)} %get-tuple-element.84), channel_id=1, source_target_pairs={{0,48},{8,24},{16,32},{24,8},{32,16},{40,56},{48,0},{56,40},{2,50}... | collective-permute-start | bytes 2162696 | tf_op jit(solution)/shard_map/ppermute | solution.py:79
  41.5 11.4 %collective-permute-start.11 = (f32[16,10,8,128]{3,2,1,0:T(8,128)S(1)}, f32[16,10,8,128]{3,2,1,0:T(8,128)S(1)}, u32[]{:S(2)}, u32[]{:S(2)}) collective-permute-start(f32[16,10,8,128]{3,2,1,0:T(8,128)S(1)} %get-tuple-element.88), channel_id=1, source_target_pairs={{0,1},{8,73},{16,17},{24,89},{32,33},{40,105},{48,49},{56,121},{2,... | collective-permute-start | bytes 1966088 | tf_op jit(solution)/shard_map/ppermute | solution.py:79
  48.6 11.6 %collective-permute-start.6 = (f32[8,11,8,128]{3,2,1,0:T(8,128)S(1)}, f32[8,11,8,128]{3,2,1,0:T(8,128)S(1)}, u32[]{:S(2)}, u32[]{:S(2)}) collective-permute-start(f32[8,11,8,128]{3,2,1,0:T(8,128)S(1)} %get-tuple-element.91), channel_id=1, source_target_pairs={{0,48},{8,24},{16,32},{24,8},{32,16},{40,56},{48,0},{56,40},{2,50}... | collective-permute-start | bytes 1081352 | tf_op jit(solution)/shard_map/ppermute | solution.py:79
  50.3 9.9 %collective-permute-start.9 = (f32[8,11,8,128]{3,2,1,0:T(8,128)S(1)}, f32[8,11,8,128]{3,2,1,0:T(8,128)S(1)}, u32[]{:S(2)}, u32[]{:S(2)}) collective-permute-start(f32[8,11,8,128]{3,2,1,0:T(8,128)S(1)} %get-tuple-element.89), channel_id=1, source_target_pairs={{0,1},{8,73},{16,17},{24,89},{32,33},{40,105},{48,49},{56,121},{2,... | collective-permute-start | bytes 1081352 | tf_op jit(solution)/shard_map/ppermute | solution.py:79
  53.0 7.2 %collective-permute-start.12 = (f32[8,10,8,128]{3,2,1,0:T(8,128)S(1)}, f32[8,10,8,128]{3,2,1,0:T(8,128)S(1)}, u32[]{:S(2)}, u32[]{:S(2)}) collective-permute-start(f32[8,10,8,128]{3,2,1,0:T(8,128)S(1)} %get-tuple-element.93), channel_id=1, source_target_pairs={{0,2},{8,14},{16,18},{24,30},{32,34},{40,46},{48,50},{56,62},{2,0}... | collective-permute-start | bytes 983048 | tf_op jit(solution)/shard_map/ppermute | solution.py:79
  95.7 5.8 %collective-permute-start.13 = (f32[64,512]{1,0:T(8,128)S(1)}, f32[64,512]{1,0:T(8,128)S(1)}, u32[]{:S(2)}, u32[]{:S(2)}) collective-permute-start(f32[64,512]{1,0:T(8,128)S(1)} %rows.1), channel_id=1, source_target_pairs={{0,8},{8,0},{16,24},{24,16},{32,40},{40,32},{48,56},{56,48},{2,10}... | collective-permute-start | bytes 393224 | tf_op jit(solution)/shard_map/ppermute | solution.py:79
  99.6 13.2 %collective-permute-start.14 = (f32[64,512]{1,0:T(8,128)S(1)}, f32[64,512]{1,0:T(8,128)S(1)}, u32[]{:S(2)}, u32[]{:S(2)}) collective-permute-start(f32[64,512]{1,0:T(8,128)S(1)} %rows.1), channel_id=1, source_target_pairs={{0,64},{8,72},{16,80},{24,88},{32,96},{40,104},{48,112},{56,120},{... | collective-permute-start | bytes 393224 | tf_op jit(solution)/shard_map/ppermute | solution.py:79
  101.5 11.3 %collective-permute-start.17 = (f32[2,64,512]{2,1,0:T(8,128)S(1)}, f32[2,64,512]{2,1,0:T(8,128)S(1)}, u32[]{:S(2)}, u32[]{:S(2)}) collective-permute-start(f32[2,64,512]{2,1,0:T(8,128)S(1)} %pad_maximum_fusion.pair_ref), channel_id=1, source_target_pairs={{0,48},{8,120},{16,32},{24,104},{32,16},{40,88},{48,0},{56,72},{2,... | collective-permute-start | bytes 786440 | tf_op jit(solution)/shard_map/ppermute | solution.py:79
  102.6 12.4 %collective-permute-start.16 = (f32[2,64,512]{2,1,0:T(8,128)S(1)}, f32[2,64,512]{2,1,0:T(8,128)S(1)}, u32[]{:S(2)}, u32[]{:S(2)}) collective-permute-start(f32[2,64,512]{2,1,0:T(8,128)S(1)} %pad_maximum_fusion.pair_ref), channel_id=1, source_target_pairs={{0,32},{8,104},{16,48},{24,120},{32,0},{40,72},{48,16},{56,88},{2,... | collective-permute-start | bytes 786440 | tf_op jit(solution)/shard_map/ppermute | solution.py:79
  104.9 11.5 %collective-permute-start.15 = (f32[2,64,512]{2,1,0:T(8,128)S(1)}, f32[2,64,512]{2,1,0:T(8,128)S(1)}, u32[]{:S(2)}, u32[]{:S(2)}) collective-permute-start(f32[2,64,512]{2,1,0:T(8,128)S(1)} %pad_maximum_fusion.pair_ref), channel_id=1, source_target_pairs={{0,16},{8,88},{16,0},{24,72},{32,48},{40,120},{48,32},{56,104},{2,... | collective-permute-start | bytes 786440 | tf_op jit(solution)/shard_map/ppermute | solution.py:79
  116.4 6.8 %collective-permute-start.19 = (f32[2,64,512]{2,1,0:T(8,128)S(1)}, f32[2,64,512]{2,1,0:T(8,128)S(1)}, u32[]{:S(2)}, u32[]{:S(2)}) collective-permute-start(f32[2,64,512]{2,1,0:T(8,128)S(1)} %collective-permute-done.15.p1), channel_id=1, source_target_pairs={{0,8},{8,0},{16,24},{24,16},{32,40},{40,32},{48,56},{56,48},{2,10}... | collective-permute-start | bytes 786440 | tf_op jit(solution)/shard_map/ppermute | solution.py:79
  121.1 2.1 %collective-permute-start.20 = (f32[2,64,512]{2,1,0:T(8,128)S(1)}, f32[2,64,512]{2,1,0:T(8,128)S(1)}, u32[]{:S(2)}, u32[]{:S(2)}) collective-permute-start(f32[2,64,512]{2,1,0:T(8,128)S(1)} %collective-permute-done.16.p2), channel_id=1, source_target_pairs={{0,8},{8,0},{16,24},{24,16},{32,40},{40,32},{48,56},{56,48},{2,10}... | collective-permute-start | bytes 786440 | tf_op jit(solution)/shard_map/ppermute | solution.py:79
  121.1 2.1 %collective-permute-start.21 = (f32[2,64,512]{2,1,0:T(8,128)S(1)}, f32[2,64,512]{2,1,0:T(8,128)S(1)}, u32[]{:S(2)}, u32[]{:S(2)}) collective-permute-start(f32[2,64,512]{2,1,0:T(8,128)S(1)} %collective-permute-done.17.p3), channel_id=1, source_target_pairs={{0,8},{8,0},{16,24},{24,16},{32,40},{40,32},{48,56},{56,48},{2,10}... | collective-permute-start | bytes 786440 | tf_op jit(solution)/shard_map/ppermute | solution.py:79
  121.6 1.6 %collective-permute-start.18 = (f32[64,512]{1,0:T(8,128)S(1)}, f32[64,512]{1,0:T(8,128)S(1)}, u32[]{:S(2)}, u32[]{:S(2)}) collective-permute-start(f32[64,512]{1,0:T(8,128)S(1)} %collective-permute-done.14.p0), channel_id=1, source_target_pairs={{0,8},{8,0},{16,24},{24,16},{32,40},{40,32},{48,56},{56,48},{2,10}... | collective-permute-start | bytes 393224 | tf_op jit(solution)/shard_map/ppermute | solution.py:79

commit v3 on v2

--- a/solution.py
+++ b/solution.py
@@ -99,6 +99,18 @@
         return lax.dot_general(a, b, (dims, ((), ())), preferred_element_type=jnp.float32)
 
     return dot(fh, sh) + (dot(fh, sl) + dot(fl, sh))
+
+
+def thin_product(first, second, dims=((1,), (0,))):
+    fh, fl = first
+    sh, sl = second
+    count = fh.shape[0]
+
+    def dot(a, b):
+        return lax.dot_general(a, b, (dims, ((), ())), preferred_element_type=jnp.float32)
+
+    stacked = dot(jnp.concatenate([fh, fl], axis=0), sh)
+    return stacked[:count] + (stacked[count:] + dot(fh, sl))
 
 
 NT = ((1,), (1,))
@@ -233,18 +245,20 @@
     assemble(pieces, grad)
     g = split(grad[...])
     rows = pl.ds(pl.multiple_of(table_ref[20] * ROWS, ROWS), ROWS)
-    inner = product((lkh[rows, :], lkl[rows, :]), g)
-    left = lc[rows, :] - product(split(inner), g, NT)
-    turned = split(product(split(left), g))
-    inner = product(turned, (rkh[...], rkl[...]))
-    inner = product(split(inner), g, NT)
-    out[...] = product(turned, (rch[...], rcl[...])) - product(split(inner), g)
+    inner = thin_product((lkh[rows, :], lkl[rows, :]), g)
+    left = lc[rows, :] - thin_product(split(inner), g, NT)
+    turned = split(thin_product(split(left), g))
+    inner = thin_product(turned, (rkh[...], rkl[...]))
+    inner = thin_product(split(inner), g, NT)
+    value = thin_product(turned, (rch[...], rcl[...])) - thin_product(split(inner), g)
+    for i in range(8):
+        out[i] = value
 
 
 def precondition_rows(table, pieces, constants):
     return pl.pallas_call(
         rows_kernel,
-        out_shape=jax.ShapeDtypeStruct((ROWS, ORDER), jnp.float32),
+        out_shape=jax.ShapeDtypeStruct((8, ROWS, ORDER), jnp.float32),
         in_specs=[pl.BlockSpec(memory_space=pltpu.SMEM)] + whole(8),
         out_specs=pl.BlockSpec(memory_space=pltpu.VMEM),
         scratch_shapes=[pltpu.VMEM((ORDER, ORDER), jnp.float32)],
@@ -278,38 +292,32 @@
     )(pieces, *constants[:6], left_stat, right_stat)
 
 
-def spread_kernel(table_ref, pair_ref, p0, p1, p2, p3, q0, q1, q2, q3, out, sems):
-    xh, z, c = table_ref[16] >> 1, table_ref[18], table_ref[19]
-    copies = []
-
-    def put(src, xd, zd, cd):
-        slot = (xd * 4 + zd) * 2 + cd
-        copies.append(pltpu.make_async_copy(src, out.at[table_ref[slot]], sems.at[len(copies)]))
-
-    for i in range(2):
-        put(pair_ref.at[i], xh, z, c ^ i)
-    put(p0, xh ^ 1, z, c)
-    put(q0, xh ^ 1, z, 1 - c)
-    for holder, group in ((c, (p1, p2, p3)), (1 - c, (q1, q2, q3))):
-        for j, ref in enumerate(group):
-            for i in range(2):
-                put(ref.at[i], xh ^ holder, z ^ (j + 1), holder ^ i)
+def spread_kernel(late, table_ref, *refs):
+    source, (out, sems) = refs[0], refs[-2:]
+    core = 1 - table_ref[19] if late else table_ref[19]
+    copies = [
+        pltpu.make_async_copy(source.at[i], out.at[table_ref[2 * i + core]], sems.at[i])
+        for i in range(8)
+    ]
     for copy in copies:
         copy.start()
     for copy in copies:
         copy.wait()
 
 
-def spread(table, pieces):
-    return pl.pallas_call(
-        spread_kernel,
+def spread(table, source, before=None):
+    late = before is not None
+    anywhere = pl.BlockSpec(memory_space=pl.ANY)
+    return pl.pallas_call(
+        functools.partial(spread_kernel, late),
         out_shape=jax.ShapeDtypeStruct((16, ROWS, ORDER), jnp.float32),
-        in_specs=[pl.BlockSpec(memory_space=pltpu.SMEM)] + whole(9),
-        out_specs=pl.BlockSpec(memory_space=pl.ANY),
-        scratch_shapes=[pltpu.SemaphoreType.DMA((16,))],
+        in_specs=[pl.BlockSpec(memory_space=pltpu.SMEM)] + whole(1) + [anywhere] * late,
+        out_specs=anywhere,
+        scratch_shapes=[pltpu.SemaphoreType.DMA((8,))],
+        input_output_aliases={2: 0} if late else {},
         compiler_params=pltpu.CompilerParams(vmem_limit_bytes=SMALL_LIMIT),
-        name="spread",
-    )(table, *pieces)
+        name="spread_late" if late else "spread",
+    )(table, source, *([before] if late else []))
 
 
 def local(replica_grads, owner_table, left_stat, right_stat, left_root, right_root):
@@ -322,17 +330,16 @@
     table = jnp.concatenate([block_of_slot, coords])
     streams = range(3)
     everything = tuple(streams)
-    (first,) = pack("other0", [(False, 1, (0,))], table, replica_grads)
-    table, first = lax.optimization_barrier((table, first))
-    later = pack("other12", [(False, 1, (1,)), (False, 1, (2,))], table, replica_grads)
-    table, later = lax.optimization_barrier((table, later))
-    arrived = [send(value, CORE_SWAP) for value in (first, *later)]
-    *mine, other = pack(
-        "own", [(True, 1, (s,)) for s in streams] + [(False, 0, everything)], table, replica_grads
-    )
+    arrived = []
+    for s in streams:
+        (value,) = pack(f"other{s}", [(False, 1, (s,))], table, replica_grads)
+        table, value = lax.optimization_barrier((table, value))
+        arrived.append(send(value, CORE_SWAP))
+    mine = pack("own", [(True, 1, (s,)) for s in streams], table, replica_grads)
+    table, mine = lax.optimization_barrier((table, mine))
+    (other,) = pack("otherkeep", [(False, 0, everything)], table, replica_grads)
     outgoing = [mine[s] + arrived[s] for s in streams]
-    other, outgoing = lax.optimization_barrier((other, outgoing))
-    table, other = lax.optimization_barrier((table, other))
+    table, other, _ = lax.optimization_barrier((table, other, outgoing))
     *constants, mine = pack(
         "keep",
         [(True, 0, everything)],
@@ -360,15 +367,11 @@
     parts = lax.all_to_all(joined, AXES, 0, 0, axis_index_groups=CUBES, tiled=True)
     pieces = lax.all_to_all(total(parts), ("y", "xl"), 0, 0, tiled=True)
     rows = precondition_rows(table, pieces, constants)
-    both = jnp.stack([rows, send(rows, CORE_SWAP)])
-    got = [None] * 4
-    for j in (2, 1, 3):
-        got[j] = send(both, permutation(lambda x, y, z, c, j=j: (x ^ (2 * c), y, z ^ j, c)))
-    got[0] = send(rows, axis_move(0, (2, 2)))
+    got = lax.all_to_all(rows, ("xh", "z"), 0, 0, tiled=True)
     stats = statistics(pieces, constants, left_stat, right_stat)
     got, stats = lax.optimization_barrier((got, stats))
-    swapped = [send(value, CORE_SWAP) for value in got]
-    directions = spread(table, [both] + got + swapped)
+    swapped = send(got, CORE_SWAP)
+    directions = spread(table, swapped, spread(table, got))
     return (directions, *stats)
 
 

time: 126 us -> 121 us (0.960)
  starting transfers between devices: 39.8 us -> 31.1 us
  local copies, waits for them, and re-layouts: 3.5 us -> 11.9 us
  waiting for transfers between devices: 19.8 us -> 12.3 us
  Pallas kernels: 26.8 us -> 29.4 us
    ppermute x22 -> x14, starting transfers between devices: 39.8 us -> 26.6 us  [send(): return lax.ppermute(value, AXES, pairs)]
    unnamed x10 -> x36, local copies, waits for them, and re-layouts: 3.41 us -> 11.8 us
    ppermute x22 -> x14, waiting for transfers between devices: 19.8 us -> 12.3 us  [send(): return lax.ppermute(value, AXES, pairs)]
    all_to_all x0 -> x1, starting transfers between devices: none -> 4.44 us  [local(): got = lax.all_to_all(rows, ('xh', 'z'), 0, 0, tiled=True)]
    pallas_call x2 -> x3, Pallas kernels: 5.25 us -> 6.6 us  [the longest x1 3.46 us: precondition_rows(): pl.pallas_call(rows_kernel, out_shape=jax.ShapeDtypeStruct((8, ROWS, ORDE...]
    pallas_call x4 -> x6, Pallas kernels: 16.6 us -> 17.9 us  [pack(): pl.pallas_call(functools.partial(pack_kernel, parts), out_shape=extra + p...]
  transfers between devices with their start and end apart: 22 -> 15, of which waited for: 8 -> 5; matrix products, arithmetic and copies ran while one was open for 1% -> 1% of each run, Pallas kernels for 15% -> 19%
where the time goes in v3:
time: 121 us; the launch traced here: 120 us
  blocking collectives  31.8 us (26%)
  starting transfers between devices  31.1 us (26%)
  Pallas kernels  29.4 us (24%)
  waiting for transfers between devices  12.3 us (10%)
  local copies, waits for them, and re-layouts  11.9 us (10%)
  other arithmetic  2.39 us (2%)
    ppermute x14, starting transfers between devices, send(): return lax.ppermute(value, AXES, pairs)  26.6 us
    pallas_call x6, Pallas kernels, pack(): pl.pallas_call(functools.partial(pack_kernel, parts), out_shape=extra + p...  17.9 us
    all_to_all x1, blocking collectives, local(): pieces = lax.all_to_all(total(parts), ('y', 'xl'), 0, 0, tiled=True)  16 us
    all_to_all x1, blocking collectives, local(): lax.all_to_all(joined, AXES, 0, 0, axis_index_groups=CUBES, tiled=True)  15.7 us
    ppermute x14, waiting for transfers between devices, send(): return lax.ppermute(value, AXES, pairs)  12.3 us
    unnamed x36, local copies, waits for them, and re-layouts  11.8 us
    pallas_call x1, Pallas kernels, statistics(): pl.pallas_call(stats_kernel, out_shape=[jax.ShapeDtypeStruct((1, ORDER, O...  4.7 us
    all_to_all x1, starting transfers between devices, local(): got = lax.all_to_all(rows, ('xh', 'z'), 0, 0, tiled=True)  4.44 us
  transfers between devices with their start and end apart: 15, of which 5 were waited for; matrix products, arithmetic and copies ran while one was open for 1% of the time, Pallas kernels for 19%

profile of v3, /device:TPU:1, one launch (start us, length us, event | category | flops | bytes accessed | tf_op | source)
XLA Modules:
  0.0 120.0 jit_solution(4667685427302297535)
XLA Ops:
  0.6 0.8 select_reduce_fusion
  1.5 3.4 %copy-done = bf16[1,16,512,512]{3,2,1,0:T(8,128)(2,1)S(1)} copy-done((bf16[1,16,512,512]{3,2,1,0:T(8,128)(2,1)S(1)}, bf16[1,16,512,512]{3,2,1,0:T(8,128)(2,1)}, u32[]{:S(2)}) %copy-start) | copy-done | bytes 8388632
  4.9 1.1 other0.1
  6.0 1.5 %collective-permute-start = (f32[32,11,8,128]{3,2,1,0:T(8,128)S(1)}, f32[32,11,8,128]{3,2,1,0:T(8,128)S(1)}, u32[]{:S(2)}, u32[]{:S(2)}) collective-permute-start(f32[32,11,8,128]{3,2,1,0:T(8,128)S(1)} %other0.1), channel_id=1, source_target_pairs={{0,8},{8,0},{16,24},{24,16},{32,40},{40,32},{48,56},{56,48},{2,10}... | collective-permute-start | bytes 4325384 | tf_op jit(solution)/shard_map/ppermute | solution.py:79
  7.5 1.1 other1.1
  8.8 1.2 other2.1
  10.0 0.6 collective-permute-start.2
  10.5 2.4 %own.1 = (f32[32,11,8,128]{3,2,1,0:T(8,128)S(1)}, f32[32,11,8,128]{3,2,1,0:T(8,128)S(1)}, f32[32,10,8,128]{3,2,1,0:T(8,128)S(1)}) custom-call(s32[21]{0:T(128)S(1)} %concatenate.3.table_ref, bf16[1,16,512,512]{3,2,1,0:T(8,128)(2,1)S(1)} %copy-done), custom_call_target="tpu_custom_call" | custom-call | tf_op jit(solution)/shard_map/own/pallas_call | solution.py:163
  12.9 2.3 %otherkeep.1 = f32[32,32,8,128]{3,2,1,0:T(8,128)S(1)} custom-call(s32[21]{0:T(128)S(1)} %concatenate.3.table_ref, bf16[1,16,512,512]{3,2,1,0:T(8,128)(2,1)S(1)} %copy-done), custom_call_target="tpu_custom_call" | custom-call | tf_op jit(solution)/shard_map/otherkeep/pallas_call | solution.py:163
  15.4 0.1 add.62
  15.6 0.1 add.63
  15.9 2.6 %collective-permute-start.4 = (f32[32,11,8,128]{3,2,1,0:T(8,128)S(1)}, f32[32,11,8,128]{3,2,1,0:T(8,128)S(1)}, u32[]{:S(2)}, u32[]{:S(2)}) collective-permute-start(f32[32,11,8,128]{3,2,1,0:T(8,128)S(1)} %add.62), channel_id=1, source_target_pairs={{0,1},{8,73},{16,17},{24,89},{32,33},{40,105},{48,49},{56,121},{2,... | collective-permute-start | bytes 4325384 | tf_op jit(solution)/shard_map/ppermute | solution.py:79
  18.5 2.7 %collective-permute-start.7 = (f32[32,11,8,128]{3,2,1,0:T(8,128)S(1)}, f32[32,11,8,128]{3,2,1,0:T(8,128)S(1)}, u32[]{:S(2)}, u32[]{:S(2)}) collective-permute-start(f32[32,11,8,128]{3,2,1,0:T(8,128)S(1)} %add.63), channel_id=1, source_target_pairs={{0,2},{8,14},{16,18},{24,30},{32,34},{40,46},{48,50},{56,62},{2,0}... | collective-permute-start | bytes 4325384 | tf_op jit(solution)/shard_map/ppermute | solution.py:79
  21.2 1.6 %collective-permute-start.10 = (f32[32,10,8,128]{3,2,1,0:T(8,128)S(1)}, f32[32,10,8,128]{3,2,1,0:T(8,128)S(1)}, u32[]{:S(2)}, u32[]{:S(2)}) collective-permute-start(f32[32,10,8,128]{3,2,1,0:T(8,128)S(1)} %add.64), channel_id=1, source_target_pairs={{0,48},{8,24},{16,32},{24,8},{32,16},{40,56},{48,0},{56,40},{2,50}... | collective-permute-start | bytes 3932168 | tf_op jit(solution)/shard_map/ppermute | solution.py:79
  22.9 9.7 %keep.1 = (f32[512,512]{1,0:T(8,128)S(1)}, bf16[512,512]{1,0:T(8,128)(2,1)S(1)}, bf16[512,512]{1,0:T(8,128)(2,1)S(1)}, f32[512,512]{1,0:T(8,128)S(1)}, bf16[512,...) custom-call(s32[21]{0:T(128)S(1)} %concatenate.3.table_ref, ...), custom_call_target="tpu_custom_call" | custom-call | tf_op jit(solution)/shard_map/keep/pallas_call | solution.py:163
  32.7 0.4 slice_add_fusion
  33.1 0.6 copy-done.16
  33.6 1.7 %collective-permute-done.4 = f32[32,11,8,128]{3,2,1,0:T(8,128)S(1)} collective-permute-done((f32[32,11,8,128]{3,2,1,0:T(8,128)S(1)}, f32[32,11,8,128]{3,2,1,0:T(8,128)S(1)}, u32[]{:S(2)}, u32[]{:S(2)}) %collective-permute-start.4) | collective-permute-done | bytes 1441824 | tf_op jit(solution)/shard_map/ppermute | solution.py:79
  35.3 0.1 slice_add_fusion.6
  35.4 2.9 %collective-permute-start.5 = (f32[16,11,8,128]{3,2,1,0:T(8,128)S(1)}, f32[16,11,8,128]{3,2,1,0:T(8,128)S(1)}, u32[]{:S(2)}, u32[]{:S(2)}) collective-permute-start(f32[16,11,8,128]{3,2,1,0:T(8,128)S(1)} %get-tuple-element.76), channel_id=1, source_target_pairs={{0,2},{8,14},{16,18},{24,30},{32,34},{40,46},{48,50},{56,62},{2,0}... | collective-permute-start | bytes 2162696 | tf_op jit(solution)/shard_map/ppermute | solution.py:79
  38.3 0.1 slice_add_fusion.4
  38.5 1.4 %collective-permute-start.8 = (f32[16,11,8,128]{3,2,1,0:T(8,128)S(1)}, f32[16,11,8,128]{3,2,1,0:T(8,128)S(1)}, u32[]{:S(2)}, u32[]{:S(2)}) collective-permute-start(f32[16,11,8,128]{3,2,1,0:T(8,128)S(1)} %get-tuple-element.74), channel_id=1, source_target_pairs={{0,48},{8,24},{16,32},{24,8},{32,16},{40,56},{48,0},{56,40},{2,50}... | collective-permute-start | bytes 2162696 | tf_op jit(solution)/shard_map/ppermute | solution.py:79
  39.9 0.2 slice_add_fusion.2
  40.1 0.1 slice_add_fusion.8
  40.3 2.6 %collective-permute-start.11 = (f32[16,10,8,128]{3,2,1,0:T(8,128)S(1)}, f32[16,10,8,128]{3,2,1,0:T(8,128)S(1)}, u32[]{:S(2)}, u32[]{:S(2)}) collective-permute-start(f32[16,10,8,128]{3,2,1,0:T(8,128)S(1)} %get-tuple-element.78), channel_id=1, source_target_pairs={{0,1},{8,73},{16,17},{24,89},{32,33},{40,105},{48,49},{56,121},{2,... | collective-permute-start | bytes 1966088 | tf_op jit(solution)/shard_map/ppermute | solution.py:79
  42.8 4.5 %collective-permute-done.5 = f32[16,11,8,128]{3,2,1,0:T(8,128)S(1)} collective-permute-done((f32[16,11,8,128]{3,2,1,0:T(8,128)S(1)}, f32[16,11,8,128]{3,2,1,0:T(8,128)S(1)}, u32[]{:S(2)}, u32[]{:S(2)}) %collective-permute-start.5) | collective-permute-done | bytes 720928 | tf_op jit(solution)/shard_map/ppermute | solution.py:79
  47.4 1.1 collective-permute-start.6
  48.5 0.5 collective-permute-done.8
  49.1 2.6 %collective-permute-start.9 = (f32[8,11,8,128]{3,2,1,0:T(8,128)S(1)}, f32[8,11,8,128]{3,2,1,0:T(8,128)S(1)}, u32[]{:S(2)}, u32[]{:S(2)}) collective-permute-start(f32[8,11,8,128]{3,2,1,0:T(8,128)S(1)} %get-tuple-element.79), channel_id=1, source_target_pairs={{0,1},{8,73},{16,17},{24,89},{32,33},{40,105},{48,49},{56,121},{2,... | collective-permute-start | bytes 1081352 | tf_op jit(solution)/shard_map/ppermute | solution.py:79
  51.7 2.3 %collective-permute-start.12 = (f32[8,10,8,128]{3,2,1,0:T(8,128)S(1)}, f32[8,10,8,128]{3,2,1,0:T(8,128)S(1)}, u32[]{:S(2)}, u32[]{:S(2)}) collective-permute-start(f32[8,10,8,128]{3,2,1,0:T(8,128)S(1)} %get-tuple-element.83), channel_id=1, source_target_pairs={{0,2},{8,14},{16,18},{24,30},{32,34},{40,46},{48,50},{56,62},{2,0}... | collective-permute-start | bytes 983048 | tf_op jit(solution)/shard_map/ppermute | solution.py:79
  54.0 5.0 %collective-permute-done.12.r2 = f32[8,10,8,128]{3,2,1,0:T(8,128)S(1)} collective-permute-done((f32[8,10,8,128]{3,2,1,0:T(8,128)S(1)}, f32[8,10,8,128]{3,2,1,0:T(8,128)S(1)}, u32[]{:S(2)}, u32[]{:S(2)}) %collective-permute-start.12) | collective-permute-done | bytes 327712 | tf_op jit(solution)/shard_map/ppermute | solution.py:79
  58.9 0.1 join.1
  59.1 15.7 %all_to_all.15.parts = f32[8,32,8,128]{3,2,1,0:T(8,128)S(1)} all-to-all(f32[8,32,8,128]{3,2,1,0:T(8,128)S(1)} %join.1), channel_id=1, replica_groups={{0,16,6,22,65,81,71,87},{32,48,38,54,97,113,103,119},{2,18,4,20,67,83,6..., dimensions={0} | all-to-all | bytes 2097152 | tf_op jit(solution)/shard_map/all_to_all | solution.py:367
  74.9 16.0 %all_to_all.16.pieces = f32[8,32,8,128]{3,2,1,0:T(8,128)S(1)} all-to-all(f32[8,32,8,128]{3,2,1,0:T(8,128)S(1)} %total.1), channel_id=1, replica_groups=mesh['xh'=2,'z'=4,'core'=2,'y'=4,'xl'=2] {'y','xl'}, dimensions={0} | all-to-all | bytes 2097152 | tf_op jit(solution)/shard_map/all_to_all | solution.py:368
  91.0 3.5 %rows.1 = f32[8,64,512]{2,1,0:T(8,128)} custom-call(s32[21]{0:T(128)S(1)} %concatenate.3.table_ref, f32[8,32,8,128]{3,2,1,0:T(8,128)S(1)} %all_to_all.16.pieces, f32[512,512]{1,0:T(8,128)S(1)} %get-tuple-element.54.lc, bf16[512,512]{1,0:T(8,128)(2,1)S(1)} %get-tuple-element.55.lkh, bf16[512,512]{1,0:T(8,128)(2,1)S(1)} %get-tuple-element.56.lkl, ...), custom_call_target="tpu_custom_call" | custom-call | tf_op jit(solution)/shard_map/rows/pallas_call | solution.py:259
  94.4 4.4 %all-to-all-start.2 = ((f32[8,64,512]{2,1,0:T(8,128)}), f32[8,64,512]{2,1,0:T(8,128)S(1)}, u32[]{:S(2)}, u32[]{:S(2)}) async-start(f32[8,64,512]{2,1,0:T(8,128)} %rows.1), calls=%async_computation.2 | async-start | bytes 2097152 | tf_op jit(solution)/shard_map/all_to_all | solution.py:370
  98.9 1.2 %copy-done.5 = f32[1,512,512]{2,1,0:T(8,128)S(1)} copy-done((f32[1,512,512]{2,1,0:T(8,128)S(1)}, f32[1,512,512]{2,1,0:T(8,128)}, u32[]{:S(2)}) %copy-start.5) | copy-done | bytes 1048600
  100.1 1.2 %copy-done.7 = f32[512,512]{1,0:T(8,128)S(1)} copy-done((f32[512,512]{1,0:T(8,128)S(1)}, f32[512,512]{1,0:T(8,128)}, u32[]{:S(2)}) %copy-start.7) | copy-done | bytes 1048600
  101.3 1.0 copy-done.9
  102.3 1.0 copy-done.11
  103.4 1.0 copy-done.13
  104.4 1.0 copy-done.15
  105.5 1.2 %copy-done.17 = f32[512,512]{1,0:T(8,128)S(1)} copy-done((f32[512,512]{1,0:T(8,128)S(1)}, f32[512,512]{1,0:T(8,128)}, u32[]{:S(2)}) %copy-start.17) | copy-done | bytes 1048600
  106.7 4.7 %stats.1 = (f32[1,512,512]{2,1,0:T(8,128)}, f32[1,512,512]{2,1,0:T(8,128)}, f32[1,512,512]{2,1,0:T(8,128)}, f32[1,512,512]{2,1,0:T(8,128)}) custom-call(f32[8,32,8,128]{3,2,1,0:T(8,128)S(1)} %all_to_all.16.pieces, f32[512,512]{1,0:T(8,128)S(1)} %copy-done.7, bf16[512,512]{1,0:T(8,128)(2,1)S(1)} %copy-done.9, bf16[512,512]{1,0:T(8,128)(2,1)S(1)} %copy-done.11, ...), custom_call_target="tpu_custom_call" | custom-call | flops 3221225472 | bytes 11534336 | tf_op jit(solution)/shard_map/stats/pallas_call | solution.py:283
  111.4 4.5 %collective-permute-start.13 = (f32[8,64,512]{2,1,0:T(8,128)S(1)}, f32[8,64,512]{2,1,0:T(8,128)S(1)}, u32[]{:S(2)}, u32[]{:S(2)}) collective-permute-start(f32[8,64,512]{2,1,0:T(8,128)S(1)} %all-to-all-done.2.refs_0_), channel_id=1, source_target_pairs={{0,8},{8,0},{16,24},{24,16},{32,40},{40,32},{48,56},{56,48},{2,10}... | collective-permute-start | bytes 3145736 | tf_op jit(solution)/shard_map/ppermute | solution.py:79
  115.9 1.6 %spread.1.refs_1_ = f32[16,64,512]{2,1,0:T(8,128)} custom-call(s32[21]{0:T(128)S(1)} %concatenate.3.table_ref, f32[8,64,512]{2,1,0:T(8,128)S(1)} %all-to-all-done.2.refs_0_), custom_call_target="tpu_custom_call" | custom-call | tf_op jit(solution)/shard_map/spread/pallas_call | solution.py:311
  117.5 0.7 collective-permute-done.13.refs_0_
  118.2 1.6 %spread_late.1 = f32[16,64,512]{2,1,0:T(8,128)} custom-call(s32[21]{0:T(128)S(1)} %concatenate.3.table_ref, f32[8,64,512]{2,1,0:T(8,128)S(1)} %collective-permute-done.13.refs_0_, f32[16,64,512]{2,1,0:T(8,128)} %spread.1.refs_1_), custom_call_target="tpu_custom_call", output_to_operand_aliasing={{}: (2, {})} | custom-call | tf_op jit(solution)/shard_map/spread_late/pallas_call | solution.py:311
  (45 shorter events, 0.8 us)
Async XLA Ops:
  1.5 3.4 %copy-start = (bf16[1,16,512,512]{3,2,1,0:T(8,128)(2,1)S(1)}, bf16[1,16,512,512]{3,2,1,0:T(8,128)(2,1)}, u32[]{:S(2)}) copy-start(bf16[1,16,512,512]{3,2,1,0:T(8,128)(2,1)} %blocks.11) | copy-start | bytes 25165828
  6.0 9.3 %collective-permute-start = (f32[32,11,8,128]{3,2,1,0:T(8,128)S(1)}, f32[32,11,8,128]{3,2,1,0:T(8,128)S(1)}, u32[]{:S(2)}, u32[]{:S(2)}) collective-permute-start(f32[32,11,8,128]{3,2,1,0:T(8,128)S(1)} %other0.1), channel_id=1, source_target_pairs={{0,8},{8,0},{16,24},{24,16},{32,40},{40,32},{48,56},{56,48},{2,10}... | collective-permute-start | bytes 4325384 | tf_op jit(solution)/shard_map/ppermute | solution.py:79
  8.7 6.9 %collective-permute-start.1 = (f32[32,11,8,128]{3,2,1,0:T(8,128)S(1)}, f32[32,11,8,128]{3,2,1,0:T(8,128)S(1)}, u32[]{:S(2)}, u32[]{:S(2)}) collective-permute-start(f32[32,11,8,128]{3,2,1,0:T(8,128)S(1)} %other1.1), channel_id=1, source_target_pairs={{0,8},{8,0},{16,24},{24,16},{32,40},{40,32},{48,56},{56,48},{2,10}... | collective-permute-start | bytes 4325384 | tf_op jit(solution)/shard_map/ppermute | solution.py:79
  10.0 5.3 %collective-permute-start.2 = (f32[32,10,8,128]{3,2,1,0:T(8,128)S(1)}, f32[32,10,8,128]{3,2,1,0:T(8,128)S(1)}, u32[]{:S(2)}, u32[]{:S(2)}) collective-permute-start(f32[32,10,8,128]{3,2,1,0:T(8,128)S(1)} %other2.1), channel_id=1, source_target_pairs={{0,8},{8,0},{16,24},{24,16},{32,40},{40,32},{48,56},{56,48},{2,10}... | collective-permute-start | bytes 3932168 | tf_op jit(solution)/shard_map/ppermute | solution.py:79
  15.5 7.3 %copy-start.1 = (f32[1,512,512]{2,1,0:T(8,128)S(1)}, f32[1,512,512]{2,1,0:T(8,128)}, u32[]{:S(2)}) copy-start(f32[1,512,512]{2,1,0:T(8,128)} %rest_2_.1) | copy-start | bytes 3145732
  15.6 7.3 %copy-start.2 = (f32[1,512,512]{2,1,0:T(8,128)S(1)}, f32[1,512,512]{2,1,0:T(8,128)}, u32[]{:S(2)}) copy-start(f32[1,512,512]{2,1,0:T(8,128)} %rest_3_.1) | copy-start | bytes 3145732
  15.6 7.3 %copy-start.3 = (f32[1,512,512]{2,1,0:T(8,128)S(1)}, f32[1,512,512]{2,1,0:T(8,128)}, u32[]{:S(2)}) copy-start(f32[1,512,512]{2,1,0:T(8,128)} %ls.1) | copy-start | bytes 3145732
  15.6 7.3 %copy-start.4 = (f32[1,512,512]{2,1,0:T(8,128)S(1)}, f32[1,512,512]{2,1,0:T(8,128)}, u32[]{:S(2)}) copy-start(f32[1,512,512]{2,1,0:T(8,128)} %rs.1) | copy-start | bytes 3145732
  15.8 16.9 %collective-permute-start.3 = (f32[32,32,8,128]{3,2,1,0:T(8,128)S(1)}, f32[32,32,8,128]{3,2,1,0:T(8,128)S(1)}, u32[]{:S(2)}, u32[]{:S(2)}) collective-permute-start(f32[32,32,8,128]{3,2,1,0:T(8,128)S(1)} %otherkeep.1), channel_id=1, source_target_pairs={{0,8},{8,0},{16,24},{24,16},{32,40},{40,32},{48,56},{56,48},{2,10}... | collective-permute-start | bytes 12582920 | tf_op jit(solution)/shard_map/ppermute | solution.py:79
  15.9 19.4 %collective-permute-start.4 = (f32[32,11,8,128]{3,2,1,0:T(8,128)S(1)}, f32[32,11,8,128]{3,2,1,0:T(8,128)S(1)}, u32[]{:S(2)}, u32[]{:S(2)}) collective-permute-start(f32[32,11,8,128]{3,2,1,0:T(8,128)S(1)} %add.62), channel_id=1, source_target_pairs={{0,1},{8,73},{16,17},{24,89},{32,33},{40,105},{48,49},{56,121},{2,... | collective-permute-start | bytes 4325384 | tf_op jit(solution)/shard_map/ppermute | solution.py:79
  18.5 19.9 %collective-permute-start.7 = (f32[32,11,8,128]{3,2,1,0:T(8,128)S(1)}, f32[32,11,8,128]{3,2,1,0:T(8,128)S(1)}, u32[]{:S(2)}, u32[]{:S(2)}) collective-permute-start(f32[32,11,8,128]{3,2,1,0:T(8,128)S(1)} %add.63), channel_id=1, source_target_pairs={{0,2},{8,14},{16,18},{24,30},{32,34},{40,46},{48,50},{56,62},{2,0}... | collective-permute-start | bytes 4325384 | tf_op jit(solution)/shard_map/ppermute | solution.py:79
  21.2 18.9 %collective-permute-start.10 = (f32[32,10,8,128]{3,2,1,0:T(8,128)S(1)}, f32[32,10,8,128]{3,2,1,0:T(8,128)S(1)}, u32[]{:S(2)}, u32[]{:S(2)}) collective-permute-start(f32[32,10,8,128]{3,2,1,0:T(8,128)S(1)} %add.64), channel_id=1, source_target_pairs={{0,48},{8,24},{16,32},{24,8},{32,16},{40,56},{48,0},{56,40},{2,50}... | collective-permute-start | bytes 3932168 | tf_op jit(solution)/shard_map/ppermute | solution.py:79
  32.6 1.0 copy-start.16
  32.6 58.3 %copy-start.6 = (f32[512,512]{1,0:T(8,128)}, f32[512,512]{1,0:T(8,128)S(1)}, u32[]{:S(2)}) copy-start(f32[512,512]{1,0:T(8,128)S(1)} %get-tuple-element.54.lc) | copy-start | bytes 3145732
  32.6 58.3 %copy-start.8 = (bf16[512,512]{1,0:T(8,128)(2,1)}, bf16[512,512]{1,0:T(8,128)(2,1)S(1)}, u32[]{:S(2)}) copy-start(bf16[512,512]{1,0:T(8,128)(2,1)S(1)} %get-tuple-element.55.lkh) | copy-start | bytes 1572868
  32.7 58.3 %copy-start.10 = (bf16[512,512]{1,0:T(8,128)(2,1)}, bf16[512,512]{1,0:T(8,128)(2,1)S(1)}, u32[]{:S(2)}) copy-start(bf16[512,512]{1,0:T(8,128)(2,1)S(1)} %get-tuple-element.56.lkl) | copy-start | bytes 1572868
  32.7 58.3 %copy-start.12 = (bf16[512,512]{1,0:T(8,128)(2,1)}, bf16[512,512]{1,0:T(8,128)(2,1)S(1)}, u32[]{:S(2)}) copy-start(bf16[512,512]{1,0:T(8,128)(2,1)S(1)} %get-tuple-element.57.rkh) | copy-start | bytes 1572868
  32.7 58.3 %copy-start.14 = (bf16[512,512]{1,0:T(8,128)(2,1)}, bf16[512,512]{1,0:T(8,128)(2,1)S(1)}, u32[]{:S(2)}) copy-start(bf16[512,512]{1,0:T(8,128)(2,1)S(1)} %get-tuple-element.58.rkl) | copy-start | bytes 1572868
  35.4 11.9 %collective-permute-start.5 = (f32[16,11,8,128]{3,2,1,0:T(8,128)S(1)}, f32[16,11,8,128]{3,2,1,0:T(8,128)S(1)}, u32[]{:S(2)}, u32[]{:S(2)}) collective-permute-start(f32[16,11,8,128]{3,2,1,0:T(8,128)S(1)} %get-tuple-element.76), channel_id=1, source_target_pairs={{0,2},{8,14},{16,18},{24,30},{32,34},{40,46},{48,50},{56,62},{2,0}... | collective-permute-start | bytes 2162696 | tf_op jit(solution)/shard_map/ppermute | solution.py:79
  38.5 10.5 %collective-permute-start.8 = (f32[16,11,8,128]{3,2,1,0:T(8,128)S(1)}, f32[16,11,8,128]{3,2,1,0:T(8,128)S(1)}, u32[]{:S(2)}, u32[]{:S(2)}) collective-permute-start(f32[16,11,8,128]{3,2,1,0:T(8,128)S(1)} %get-tuple-element.74), channel_id=1, source_target_pairs={{0,48},{8,24},{16,32},{24,8},{32,16},{40,56},{48,0},{56,40},{2,50}... | collective-permute-start | bytes 2162696 | tf_op jit(solution)/shard_map/ppermute | solution.py:79
  40.3 11.4 %collective-permute-start.11 = (f32[16,10,8,128]{3,2,1,0:T(8,128)S(1)}, f32[16,10,8,128]{3,2,1,0:T(8,128)S(1)}, u32[]{:S(2)}, u32[]{:S(2)}) collective-permute-start(f32[16,10,8,128]{3,2,1,0:T(8,128)S(1)} %get-tuple-element.78), channel_id=1, source_target_pairs={{0,1},{8,73},{16,17},{24,89},{32,33},{40,105},{48,49},{56,121},{2,... | collective-permute-start | bytes 1966088 | tf_op jit(solution)/shard_map/ppermute | solution.py:79
  47.4 11.5 %collective-permute-start.6 = (f32[8,11,8,128]{3,2,1,0:T(8,128)S(1)}, f32[8,11,8,128]{3,2,1,0:T(8,128)S(1)}, u32[]{:S(2)}, u32[]{:S(2)}) collective-permute-start(f32[8,11,8,128]{3,2,1,0:T(8,128)S(1)} %get-tuple-element.81), channel_id=1, source_target_pairs={{0,48},{8,24},{16,32},{24,8},{32,16},{40,56},{48,0},{56,40},{2,50}... | collective-permute-start | bytes 1081352 | tf_op jit(solution)/shard_map/ppermute | solution.py:79
  49.1 9.9 %collective-permute-start.9 = (f32[8,11,8,128]{3,2,1,0:T(8,128)S(1)}, f32[8,11,8,128]{3,2,1,0:T(8,128)S(1)}, u32[]{:S(2)}, u32[]{:S(2)}) collective-permute-start(f32[8,11,8,128]{3,2,1,0:T(8,128)S(1)} %get-tuple-element.79), channel_id=1, source_target_pairs={{0,1},{8,73},{16,17},{24,89},{32,33},{40,105},{48,49},{56,121},{2,... | collective-permute-start | bytes 1081352 | tf_op jit(solution)/shard_map/ppermute | solution.py:79
  51.7 7.2 %collective-permute-start.12 = (f32[8,10,8,128]{3,2,1,0:T(8,128)S(1)}, f32[8,10,8,128]{3,2,1,0:T(8,128)S(1)}, u32[]{:S(2)}, u32[]{:S(2)}) collective-permute-start(f32[8,10,8,128]{3,2,1,0:T(8,128)S(1)} %get-tuple-element.83), channel_id=1, source_target_pairs={{0,2},{8,14},{16,18},{24,30},{32,34},{40,46},{48,50},{56,62},{2,0}... | collective-permute-start | bytes 983048 | tf_op jit(solution)/shard_map/ppermute | solution.py:79
  94.4 17.0 %all-to-all-start.2 = ((f32[8,64,512]{2,1,0:T(8,128)}), f32[8,64,512]{2,1,0:T(8,128)S(1)}, u32[]{:S(2)}, u32[]{:S(2)}) async-start(f32[8,64,512]{2,1,0:T(8,128)} %rows.1), calls=%async_computation.2 | async-start | bytes 2097152 | tf_op jit(solution)/shard_map/all_to_all | solution.py:370
  98.9 1.2 %copy-start.5 = (f32[1,512,512]{2,1,0:T(8,128)S(1)}, f32[1,512,512]{2,1,0:T(8,128)}, u32[]{:S(2)}) copy-start(f32[1,512,512]{2,1,0:T(8,128)} %rs.1) | copy-start | bytes 3145732
  100.1 1.2 %copy-start.7 = (f32[512,512]{1,0:T(8,128)S(1)}, f32[512,512]{1,0:T(8,128)}, u32[]{:S(2)}) copy-start(f32[512,512]{1,0:T(8,128)} %copy-done.6) | copy-start | bytes 3145732
  101.3 1.0 copy-start.9
  102.3 1.0 copy-start.11
  103.4 1.0 copy-start.13
  104.4 1.0 copy-start.15
  105.5 1.2 %copy-start.17 = (f32[512,512]{1,0:T(8,128)S(1)}, f32[512,512]{1,0:T(8,128)}, u32[]{:S(2)}) copy-start(f32[512,512]{1,0:T(8,128)} %copy-done.16) | copy-start | bytes 3145732
  111.4 6.8 %collective-permute-start.13 = (f32[8,64,512]{2,1,0:T(8,128)S(1)}, f32[8,64,512]{2,1,0:T(8,128)S(1)}, u32[]{:S(2)}, u32[]{:S(2)}) collective-permute-start(f32[8,64,512]{2,1,0:T(8,128)S(1)} %all-to-all-done.2.refs_0_), channel_id=1, source_target_pairs={{0,8},{8,0},{16,24},{24,16},{32,40},{40,32},{48,56},{56,48},{2,10}... | collective-permute-start | bytes 3145736 | tf_op jit(solution)/shard_map/ppermute | solution.py:79

commit v4 on v3

--- a/solution.py
+++ b/solution.py
@@ -64,9 +64,9 @@
 CUBES = [
     [
         index_of(member(0, c, qx, vx), member(1, c, qy, vy), member(2, c, qz, vz), c)
-        for vx in BITS
-        for vy in BITS
-        for vz in BITS
+        for vx in BITS[::-1]
+        for vy in BITS[::-1]
+        for vz in BITS[::-1]
     ]
     for c in BITS
     for qx in BITS
@@ -135,7 +135,7 @@
                 flips[(stream + 1) % 3] = (k >> 4) & 1
                 flips[(stream + 2) % 3] = (k >> 3) & 1
                 xd, yd, zd = (
-                    member(i, target, coset[i] ^ flips[i], (k >> (2 - i)) & 1) for i in range(3)
+                    member(i, target, coset[i] ^ flips[i], 1 - ((k >> (2 - i)) & 1)) for i in range(3)
                 )
                 block = table_ref[((xd >> 1) * 4 + zd) * 2 + target]
                 row = (yd * 2 + (xd & 1)) * ROWS
@@ -151,7 +151,7 @@
         return carry
 
     count = sum(len(streams) for _, _, streams in parts)
-    lax.fori_loop(0, 32, body, 0, unroll=4 if count == 1 else 1)
+    lax.fori_loop(0, 32, body, 0, unroll=8 if count == 1 else 2)
 
 
 def pack(name, parts, table, grads, matrices=()):
@@ -215,17 +215,19 @@
 
 
 def total_kernel(parts, out):
-    value = parts[0]
-    for i in range(1, 8):
-        value = value + parts[i]
-    for i in range(8):
-        out[i] = value
+    for tile in range(32):
+        value = parts[0, tile]
+        for i in range(1, 8):
+            value = value + parts[i, tile]
+        row, col = tile // 8 * 16 + tile % 2 * 8, tile // 2 % 4 * 128
+        for i in range(8):
+            out[i, row : row + 8, col : col + 128] = value
 
 
 def total(parts):
     return pl.pallas_call(
         total_kernel,
-        out_shape=jax.ShapeDtypeStruct((8, 32, 8, 128), jnp.float32),
+        out_shape=jax.ShapeDtypeStruct((8, ROWS, ORDER), jnp.float32),
         in_specs=whole(1),
         out_specs=pl.BlockSpec(memory_space=pltpu.VMEM),
         compiler_params=pltpu.CompilerParams(vmem_limit_bytes=SMALL_LIMIT),
@@ -233,16 +235,7 @@
     )(parts)
 
 
-def assemble(pieces, grad):
-    for n in range(8):
-        for pair in range(16):
-            row = n * ROWS + (pair // 4) * 16
-            col = (pair % 4) * 128
-            grad[row : row + 16, col : col + 128] = pieces[n, 2 * pair : 2 * pair + 2].reshape(16, 128)
-
-
-def rows_kernel(table_ref, pieces, lc, lkh, lkl, rkh, rkl, rch, rcl, out, grad):
-    assemble(pieces, grad)
+def rows_kernel(table_ref, grad, lc, lkh, lkl, rkh, rkl, rch, rcl, out):
     g = split(grad[...])
     rows = pl.ds(pl.multiple_of(table_ref[20] * ROWS, ROWS), ROWS)
     inner = thin_product((lkh[rows, :], lkl[rows, :]), g)
@@ -255,20 +248,18 @@
         out[i] = value
 
 
-def precondition_rows(table, pieces, constants):
+def precondition_rows(table, grad, constants):
     return pl.pallas_call(
         rows_kernel,
         out_shape=jax.ShapeDtypeStruct((8, ROWS, ORDER), jnp.float32),
         in_specs=[pl.BlockSpec(memory_space=pltpu.SMEM)] + whole(8),
         out_specs=pl.BlockSpec(memory_space=pltpu.VMEM),
-        scratch_shapes=[pltpu.VMEM((ORDER, ORDER), jnp.float32)],
         compiler_params=pltpu.CompilerParams(vmem_limit_bytes=VMEM_LIMIT),
         name="rows",
-    )(table, pieces, *constants[:3], *constants[4:])
-
-
-def stats_kernel(pieces, lc, lkh, lkl, rc, rkh, rkl, ls, rs, ln, rn, li, ri, grad):
-    assemble(pieces, grad)
+    )(table, grad, *constants[:3], *constants[4:])
+
+
+def stats_kernel(grad, lc, lkh, lkl, rc, rkh, rkl, ls, rs, ln, rn, li, ri):
     g = split(grad[...])
     for dims, stat_ref, c_ref, kh, kl, new_ref, inv_ref in (
         (NT, ls, lc, lkh, lkl, ln, li),
@@ -279,17 +270,16 @@
         inv_ref[0] = c_ref[...] - product((kh[...], kl[...]), split(gram))
 
 
-def statistics(pieces, constants, left_stat, right_stat):
+def statistics(grad, constants, left_stat, right_stat):
     return pl.pallas_call(
         stats_kernel,
         out_shape=[jax.ShapeDtypeStruct((1, ORDER, ORDER), jnp.float32)] * 4,
         in_specs=whole(9),
         out_specs=whole(4),
-        scratch_shapes=[pltpu.VMEM((ORDER, ORDER), jnp.float32)],
         compiler_params=pltpu.CompilerParams(vmem_limit_bytes=VMEM_LIMIT),
         cost_estimate=cost(4, 11 << 20),
         name="stats",
-    )(pieces, *constants[:6], left_stat, right_stat)
+    )(grad, *constants[:6], left_stat, right_stat)
 
 
 def spread_kernel(late, table_ref, *refs):
@@ -365,10 +355,10 @@
             kept[s] = kept[s][:half] + got[:half]
     joined = join([value for pair in tails for value in pair])
     parts = lax.all_to_all(joined, AXES, 0, 0, axis_index_groups=CUBES, tiled=True)
-    pieces = lax.all_to_all(total(parts), ("y", "xl"), 0, 0, tiled=True)
-    rows = precondition_rows(table, pieces, constants)
+    grad = lax.all_to_all(total(parts), ("y", "xl"), 0, 0, tiled=True).reshape(ORDER, ORDER)
+    rows = precondition_rows(table, grad, constants)
     got = lax.all_to_all(rows, ("xh", "z"), 0, 0, tiled=True)
-    stats = statistics(pieces, constants, left_stat, right_stat)
+    stats = statistics(grad, constants, left_stat, right_stat)
     got, stats = lax.optimization_barrier((got, stats))
     swapped = send(got, CORE_SWAP)
     directions = spread(table, swapped, spread(table, got))

time: 121 us -> 119 us (0.983)
  blocking collectives: 31.8 us -> 30.4 us
    all_to_all x1, blocking collectives: 15.7 us -> 14.3 us  [local(): lax.all_to_all(joined, AXES, 0, 0, axis_index_groups=CUBES, tiled=True)]
where the time goes in v4:
time: 119 us; the launch traced here: 118 us
  starting transfers between devices  30.9 us (26%)
  blocking collectives  30.4 us (26%)
  Pallas kernels  29 us (24%)
  waiting for transfers between devices  12.4 us (10%)
  local copies, waits for them, and re-layouts  11.9 us (10%)
  other arithmetic  2.39 us (2%)
    ppermute x14, starting transfers between devices, send(): return lax.ppermute(value, AXES, pairs)  27.4 us
    pallas_call x6, Pallas kernels, pack(): pl.pallas_call(functools.partial(pack_kernel, parts), out_shape=extra + p...  17.5 us
    all_to_all x1, blocking collectives, local(): lax.all_to_all(total(parts), ('y', 'xl'), 0, 0, tiled=True)  16.2 us
    all_to_all x1, blocking collectives, local(): lax.all_to_all(joined, AXES, 0, 0, axis_index_groups=CUBES, tiled=True)  14.3 us
    ppermute x14, waiting for transfers between devices, send(): return lax.ppermute(value, AXES, pairs)  12.4 us
    unnamed x36, local copies, waits for them, and re-layouts  11.8 us
    pallas_call x1, Pallas kernels, statistics(): pl.pallas_call(stats_kernel, out_shape=[jax.ShapeDtypeStruct((1, ORDER, O...  4.69 us
    all_to_all x1, starting transfers between devices, local(): got = lax.all_to_all(rows, ('xh', 'z'), 0, 0, tiled=True)  3.56 us
  transfers between devices with their start and end apart: 15, of which 5 were waited for; matrix products, arithmetic and copies ran while one was open for 1% of the time, Pallas kernels for 19%

profile of v4, /device:TPU:1, one launch (start us, length us, event | category | flops | bytes accessed | tf_op | source)
XLA Modules:
  0.0 118.3 jit_solution(15502043023939243397)
XLA Ops:
  0.6 0.8 select_reduce_fusion
  1.5 3.4 %copy-done = bf16[1,16,512,512]{3,2,1,0:T(8,128)(2,1)S(1)} copy-done((bf16[1,16,512,512]{3,2,1,0:T(8,128)(2,1)S(1)}, bf16[1,16,512,512]{3,2,1,0:T(8,128)(2,1)}, u32[]{:S(2)}) %copy-start) | copy-done | bytes 8388632
  4.9 1.1 other0.1
  6.0 1.5 %collective-permute-start = (f32[32,11,8,128]{3,2,1,0:T(8,128)S(1)}, f32[32,11,8,128]{3,2,1,0:T(8,128)S(1)}, u32[]{:S(2)}, u32[]{:S(2)}) collective-permute-start(f32[32,11,8,128]{3,2,1,0:T(8,128)S(1)} %other0.1), channel_id=1, source_target_pairs={{0,8},{8,0},{16,24},{24,16},{32,40},{40,32},{48,56},{56,48},{2,10}... | collective-permute-start | bytes 4325384 | tf_op jit(solution)/shard_map/ppermute | solution.py:79
  7.5 1.1 other1.1
  8.8 1.1 other2.1
  9.9 0.6 collective-permute-start.2
  10.5 2.3 %own.1 = (f32[32,11,8,128]{3,2,1,0:T(8,128)S(1)}, f32[32,11,8,128]{3,2,1,0:T(8,128)S(1)}, f32[32,10,8,128]{3,2,1,0:T(8,128)S(1)}) custom-call(s32[21]{0:T(128)S(1)} %concatenate.3.table_ref, bf16[1,16,512,512]{3,2,1,0:T(8,128)(2,1)S(1)} %copy-done), custom_call_target="tpu_custom_call" | custom-call | tf_op jit(solution)/shard_map/own/pallas_call | solution.py:163
  12.8 2.2 %otherkeep.1 = f32[32,32,8,128]{3,2,1,0:T(8,128)S(1)} custom-call(s32[21]{0:T(128)S(1)} %concatenate.3.table_ref, bf16[1,16,512,512]{3,2,1,0:T(8,128)(2,1)S(1)} %copy-done), custom_call_target="tpu_custom_call" | custom-call | tf_op jit(solution)/shard_map/otherkeep/pallas_call | solution.py:163
  15.1 0.1 add.62
  15.4 0.1 add.63
  15.6 2.6 %collective-permute-start.4 = (f32[32,11,8,128]{3,2,1,0:T(8,128)S(1)}, f32[32,11,8,128]{3,2,1,0:T(8,128)S(1)}, u32[]{:S(2)}, u32[]{:S(2)}) collective-permute-start(f32[32,11,8,128]{3,2,1,0:T(8,128)S(1)} %add.62), channel_id=1, source_target_pairs={{0,1},{8,73},{16,17},{24,89},{32,33},{40,105},{48,49},{56,121},{2,... | collective-permute-start | bytes 4325384 | tf_op jit(solution)/shard_map/ppermute | solution.py:79
  18.2 2.7 %collective-permute-start.7 = (f32[32,11,8,128]{3,2,1,0:T(8,128)S(1)}, f32[32,11,8,128]{3,2,1,0:T(8,128)S(1)}, u32[]{:S(2)}, u32[]{:S(2)}) collective-permute-start(f32[32,11,8,128]{3,2,1,0:T(8,128)S(1)} %add.63), channel_id=1, source_target_pairs={{0,2},{8,14},{16,18},{24,30},{32,34},{40,46},{48,50},{56,62},{2,0}... | collective-permute-start | bytes 4325384 | tf_op jit(solution)/shard_map/ppermute | solution.py:79
  21.0 1.6 %collective-permute-start.10 = (f32[32,10,8,128]{3,2,1,0:T(8,128)S(1)}, f32[32,10,8,128]{3,2,1,0:T(8,128)S(1)}, u32[]{:S(2)}, u32[]{:S(2)}) collective-permute-start(f32[32,10,8,128]{3,2,1,0:T(8,128)S(1)} %add.64), channel_id=1, source_target_pairs={{0,48},{8,24},{16,32},{24,8},{32,16},{40,56},{48,0},{56,40},{2,50}... | collective-permute-start | bytes 3932168 | tf_op jit(solution)/shard_map/ppermute | solution.py:79
  22.6 9.6 %keep.1 = (f32[512,512]{1,0:T(8,128)S(1)}, bf16[512,512]{1,0:T(8,128)(2,1)S(1)}, bf16[512,512]{1,0:T(8,128)(2,1)S(1)}, f32[512,512]{1,0:T(8,128)S(1)}, bf16[512,...) custom-call(s32[21]{0:T(128)S(1)} %concatenate.3.table_ref, ...), custom_call_target="tpu_custom_call" | custom-call | tf_op jit(solution)/shard_map/keep/pallas_call | solution.py:163
  32.3 0.4 slice_add_fusion
  32.7 0.6 copy-done.16
  33.3 1.8 %collective-permute-done.4 = f32[32,11,8,128]{3,2,1,0:T(8,128)S(1)} collective-permute-done((f32[32,11,8,128]{3,2,1,0:T(8,128)S(1)}, f32[32,11,8,128]{3,2,1,0:T(8,128)S(1)}, u32[]{:S(2)}, u32[]{:S(2)}) %collective-permute-start.4) | collective-permute-done | bytes 1441824 | tf_op jit(solution)/shard_map/ppermute | solution.py:79
  35.0 0.1 slice_add_fusion.6
  35.2 2.9 %collective-permute-start.5 = (f32[16,11,8,128]{3,2,1,0:T(8,128)S(1)}, f32[16,11,8,128]{3,2,1,0:T(8,128)S(1)}, u32[]{:S(2)}, u32[]{:S(2)}) collective-permute-start(f32[16,11,8,128]{3,2,1,0:T(8,128)S(1)} %get-tuple-element.76), channel_id=1, source_target_pairs={{0,2},{8,14},{16,18},{24,30},{32,34},{40,46},{48,50},{56,62},{2,0}... | collective-permute-start | bytes 2162696 | tf_op jit(solution)/shard_map/ppermute | solution.py:79
  38.1 0.1 slice_add_fusion.4
  38.2 1.4 %collective-permute-start.8 = (f32[16,11,8,128]{3,2,1,0:T(8,128)S(1)}, f32[16,11,8,128]{3,2,1,0:T(8,128)S(1)}, u32[]{:S(2)}, u32[]{:S(2)}) collective-permute-start(f32[16,11,8,128]{3,2,1,0:T(8,128)S(1)} %get-tuple-element.74), channel_id=1, source_target_pairs={{0,48},{8,24},{16,32},{24,8},{32,16},{40,56},{48,0},{56,40},{2,50}... | collective-permute-start | bytes 2162696 | tf_op jit(solution)/shard_map/ppermute | solution.py:79
  39.7 0.2 slice_add_fusion.2
  39.9 0.1 slice_add_fusion.8
  40.0 2.6 %collective-permute-start.11 = (f32[16,10,8,128]{3,2,1,0:T(8,128)S(1)}, f32[16,10,8,128]{3,2,1,0:T(8,128)S(1)}, u32[]{:S(2)}, u32[]{:S(2)}) collective-permute-start(f32[16,10,8,128]{3,2,1,0:T(8,128)S(1)} %get-tuple-element.78), channel_id=1, source_target_pairs={{0,1},{8,73},{16,17},{24,89},{32,33},{40,105},{48,49},{56,121},{2,... | collective-permute-start | bytes 1966088 | tf_op jit(solution)/shard_map/ppermute | solution.py:79
  42.6 4.5 %collective-permute-done.5 = f32[16,11,8,128]{3,2,1,0:T(8,128)S(1)} collective-permute-done((f32[16,11,8,128]{3,2,1,0:T(8,128)S(1)}, f32[16,11,8,128]{3,2,1,0:T(8,128)S(1)}, u32[]{:S(2)}, u32[]{:S(2)}) %collective-permute-start.5) | collective-permute-done | bytes 720928 | tf_op jit(solution)/shard_map/ppermute | solution.py:79
  47.1 1.1 collective-permute-start.6
  48.3 0.5 collective-permute-done.8
  48.8 2.6 %collective-permute-start.9 = (f32[8,11,8,128]{3,2,1,0:T(8,128)S(1)}, f32[8,11,8,128]{3,2,1,0:T(8,128)S(1)}, u32[]{:S(2)}, u32[]{:S(2)}) collective-permute-start(f32[8,11,8,128]{3,2,1,0:T(8,128)S(1)} %get-tuple-element.79), channel_id=1, source_target_pairs={{0,1},{8,73},{16,17},{24,89},{32,33},{40,105},{48,49},{56,121},{2,... | collective-permute-start | bytes 1081352 | tf_op jit(solution)/shard_map/ppermute | solution.py:79
  51.5 2.3 %collective-permute-start.12 = (f32[8,10,8,128]{3,2,1,0:T(8,128)S(1)}, f32[8,10,8,128]{3,2,1,0:T(8,128)S(1)}, u32[]{:S(2)}, u32[]{:S(2)}) collective-permute-start(f32[8,10,8,128]{3,2,1,0:T(8,128)S(1)} %get-tuple-element.83), channel_id=1, source_target_pairs={{0,2},{8,14},{16,18},{24,30},{32,34},{40,46},{48,50},{56,62},{2,0}... | collective-permute-start | bytes 983048 | tf_op jit(solution)/shard_map/ppermute | solution.py:79
  53.7 5.0 %collective-permute-done.12.r2 = f32[8,10,8,128]{3,2,1,0:T(8,128)S(1)} collective-permute-done((f32[8,10,8,128]{3,2,1,0:T(8,128)S(1)}, f32[8,10,8,128]{3,2,1,0:T(8,128)S(1)}, u32[]{:S(2)}, u32[]{:S(2)}) %collective-permute-start.12) | collective-permute-done | bytes 327712 | tf_op jit(solution)/shard_map/ppermute | solution.py:79
  58.7 0.1 join.1
  58.8 14.3 %all_to_all.15.parts = f32[8,32,8,128]{3,2,1,0:T(8,128)S(1)} all-to-all(f32[8,32,8,128]{3,2,1,0:T(8,128)S(1)} %join.1), channel_id=1, replica_groups={{87,71,81,65,22,6,16,0},{119,103,113,97,54,38,48,32},{85,69,83,67,20,4,..., dimensions={0} | all-to-all | bytes 2097152 | tf_op jit(solution)/shard_map/all_to_all | solution.py:357
  73.2 16.2 %all_to_all.16 = f32[8,64,512]{2,1,0:T(8,128)S(1)} all-to-all(f32[8,64,512]{2,1,0:T(8,128)S(1)} %total.1), channel_id=1, replica_groups=mesh['xh'=2,'z'=4,'core'=2,'y'=4,'xl'=2] {'y','xl'}, dimensions={0} | all-to-all | bytes 2097152 | tf_op jit(solution)/shard_map/all_to_all | solution.py:358
  89.4 3.5 %rows.1 = f32[8,64,512]{2,1,0:T(8,128)} custom-call(s32[21]{0:T(128)S(1)} %concatenate.3.table_ref, f32[512,512]{1,0:T(8,128)S(1)} %bitcast.6, f32[512,512]{1,0:T(8,128)S(1)} %get-tuple-element.54.lc, bf16[512,512]{1,0:T(8,128)(2,1)S(1)} %get-tuple-element.55.lkh, bf16[512,512]{1,0:T(8,128)(2,1)S(1)} %get-tuple-element.56.lkl, ...), custom_call_target="tpu_custom_call" | custom-call | tf_op jit(solution)/shard_map/rows/pallas_call | solution.py:252
  92.9 3.6 %all-to-all-start.2 = ((f32[8,64,512]{2,1,0:T(8,128)}), f32[8,64,512]{2,1,0:T(8,128)S(1)}, u32[]{:S(2)}, u32[]{:S(2)}) async-start(f32[8,64,512]{2,1,0:T(8,128)} %rows.1), calls=%async_computation.2 | async-start | bytes 2097152 | tf_op jit(solution)/shard_map/all_to_all | solution.py:360
  96.5 1.2 %copy-done.5 = f32[1,512,512]{2,1,0:T(8,128)S(1)} copy-done((f32[1,512,512]{2,1,0:T(8,128)S(1)}, f32[1,512,512]{2,1,0:T(8,128)}, u32[]{:S(2)}) %copy-start.5) | copy-done | bytes 1048600
  97.7 1.2 %copy-done.7 = f32[512,512]{1,0:T(8,128)S(1)} copy-done((f32[512,512]{1,0:T(8,128)S(1)}, f32[512,512]{1,0:T(8,128)}, u32[]{:S(2)}) %copy-start.7) | copy-done | bytes 1048600
  98.9 1.0 copy-done.9
  99.9 1.0 copy-done.11
  101.0 1.0 copy-done.13
  102.0 1.0 copy-done.15
  103.1 1.2 %copy-done.17 = f32[512,512]{1,0:T(8,128)S(1)} copy-done((f32[512,512]{1,0:T(8,128)S(1)}, f32[512,512]{1,0:T(8,128)}, u32[]{:S(2)}) %copy-start.17) | copy-done | bytes 1048600
  104.3 4.7 %stats.1 = (f32[1,512,512]{2,1,0:T(8,128)}, f32[1,512,512]{2,1,0:T(8,128)}, f32[1,512,512]{2,1,0:T(8,128)}, f32[1,512,512]{2,1,0:T(8,128)}) custom-call(f32[512,512]{1,0:T(8,128)S(1)} %bitcast.7, f32[512,512]{1,0:T(8,128)S(1)} %copy-done.7, bf16[512,512]{1,0:T(8,128)(2,1)S(1)} %copy-done.9, bf16[512,512]{1,0:T(8,128)(2,1)S(1)} %copy-done.11, ...), custom_call_target="tpu_custom_call" | custom-call | flops 3221225472 | bytes 11534336 | tf_op jit(solution)/shard_map/stats/pallas_call | solution.py:274
  109.0 5.3 %collective-permute-start.13 = (f32[8,64,512]{2,1,0:T(8,128)S(1)}, f32[8,64,512]{2,1,0:T(8,128)S(1)}, u32[]{:S(2)}, u32[]{:S(2)}) collective-permute-start(f32[8,64,512]{2,1,0:T(8,128)S(1)} %all-to-all-done.2.refs_0_), channel_id=1, source_target_pairs={{0,8},{8,0},{16,24},{24,16},{32,40},{40,32},{48,56},{56,48},{2,10}... | collective-permute-start | bytes 3145736 | tf_op jit(solution)/shard_map/ppermute | solution.py:79
  114.3 1.6 %spread.1.refs_1_ = f32[16,64,512]{2,1,0:T(8,128)} custom-call(s32[21]{0:T(128)S(1)} %concatenate.3.table_ref, f32[8,64,512]{2,1,0:T(8,128)S(1)} %all-to-all-done.2.refs_0_), custom_call_target="tpu_custom_call" | custom-call | tf_op jit(solution)/shard_map/spread/pallas_call | solution.py:301
  115.9 0.7 collective-permute-done.13.refs_0_
  116.6 1.6 %spread_late.1 = f32[16,64,512]{2,1,0:T(8,128)} custom-call(s32[21]{0:T(128)S(1)} %concatenate.3.table_ref, f32[8,64,512]{2,1,0:T(8,128)S(1)} %collective-permute-done.13.refs_0_, f32[16,64,512]{2,1,0:T(8,128)} %spread.1.refs_1_), custom_call_target="tpu_custom_call", output_to_operand_aliasing={{}: (2, {})} | custom-call | tf_op jit(solution)/shard_map/spread_late/pallas_call | solution.py:301
  (45 shorter events, 0.8 us)
Async XLA Ops:
  1.5 3.4 %copy-start = (bf16[1,16,512,512]{3,2,1,0:T(8,128)(2,1)S(1)}, bf16[1,16,512,512]{3,2,1,0:T(8,128)(2,1)}, u32[]{:S(2)}) copy-start(bf16[1,16,512,512]{3,2,1,0:T(8,128)(2,1)} %blocks.11) | copy-start | bytes 25165828
  6.0 9.1 %collective-permute-start = (f32[32,11,8,128]{3,2,1,0:T(8,128)S(1)}, f32[32,11,8,128]{3,2,1,0:T(8,128)S(1)}, u32[]{:S(2)}, u32[]{:S(2)}) collective-permute-start(f32[32,11,8,128]{3,2,1,0:T(8,128)S(1)} %other0.1), channel_id=1, source_target_pairs={{0,8},{8,0},{16,24},{24,16},{32,40},{40,32},{48,56},{56,48},{2,10}... | collective-permute-start | bytes 4325384 | tf_op jit(solution)/shard_map/ppermute | solution.py:79
  8.7 6.7 %collective-permute-start.1 = (f32[32,11,8,128]{3,2,1,0:T(8,128)S(1)}, f32[32,11,8,128]{3,2,1,0:T(8,128)S(1)}, u32[]{:S(2)}, u32[]{:S(2)}) collective-permute-start(f32[32,11,8,128]{3,2,1,0:T(8,128)S(1)} %other1.1), channel_id=1, source_target_pairs={{0,8},{8,0},{16,24},{24,16},{32,40},{40,32},{48,56},{56,48},{2,10}... | collective-permute-start | bytes 4325384 | tf_op jit(solution)/shard_map/ppermute | solution.py:79
  9.9 5.0 %collective-permute-start.2 = (f32[32,10,8,128]{3,2,1,0:T(8,128)S(1)}, f32[32,10,8,128]{3,2,1,0:T(8,128)S(1)}, u32[]{:S(2)}, u32[]{:S(2)}) collective-permute-start(f32[32,10,8,128]{3,2,1,0:T(8,128)S(1)} %other2.1), channel_id=1, source_target_pairs={{0,8},{8,0},{16,24},{24,16},{32,40},{40,32},{48,56},{56,48},{2,10}... | collective-permute-start | bytes 3932168 | tf_op jit(solution)/shard_map/ppermute | solution.py:79
  15.3 7.3 %copy-start.1 = (f32[1,512,512]{2,1,0:T(8,128)S(1)}, f32[1,512,512]{2,1,0:T(8,128)}, u32[]{:S(2)}) copy-start(f32[1,512,512]{2,1,0:T(8,128)} %rest_2_.1) | copy-start | bytes 3145732
  15.3 7.3 %copy-start.2 = (f32[1,512,512]{2,1,0:T(8,128)S(1)}, f32[1,512,512]{2,1,0:T(8,128)}, u32[]{:S(2)}) copy-start(f32[1,512,512]{2,1,0:T(8,128)} %rest_3_.1) | copy-start | bytes 3145732
  15.3 7.3 %copy-start.3 = (f32[1,512,512]{2,1,0:T(8,128)S(1)}, f32[1,512,512]{2,1,0:T(8,128)}, u32[]{:S(2)}) copy-start(f32[1,512,512]{2,1,0:T(8,128)} %ls.1) | copy-start | bytes 3145732
  15.3 7.3 %copy-start.4 = (f32[1,512,512]{2,1,0:T(8,128)S(1)}, f32[1,512,512]{2,1,0:T(8,128)}, u32[]{:S(2)}) copy-start(f32[1,512,512]{2,1,0:T(8,128)} %rs.1) | copy-start | bytes 3145732
  15.5 16.8 %collective-permute-start.3 = (f32[32,32,8,128]{3,2,1,0:T(8,128)S(1)}, f32[32,32,8,128]{3,2,1,0:T(8,128)S(1)}, u32[]{:S(2)}, u32[]{:S(2)}) collective-permute-start(f32[32,32,8,128]{3,2,1,0:T(8,128)S(1)} %otherkeep.1), channel_id=1, source_target_pairs={{0,8},{8,0},{16,24},{24,16},{32,40},{40,32},{48,56},{56,48},{2,10}... | collective-permute-start | bytes 12582920 | tf_op jit(solution)/shard_map/ppermute | solution.py:79
  15.6 19.4 %collective-permute-start.4 = (f32[32,11,8,128]{3,2,1,0:T(8,128)S(1)}, f32[32,11,8,128]{3,2,1,0:T(8,128)S(1)}, u32[]{:S(2)}, u32[]{:S(2)}) collective-permute-start(f32[32,11,8,128]{3,2,1,0:T(8,128)S(1)} %add.62), channel_id=1, source_target_pairs={{0,1},{8,73},{16,17},{24,89},{32,33},{40,105},{48,49},{56,121},{2,... | collective-permute-start | bytes 4325384 | tf_op jit(solution)/shard_map/ppermute | solution.py:79
  18.2 19.9 %collective-permute-start.7 = (f32[32,11,8,128]{3,2,1,0:T(8,128)S(1)}, f32[32,11,8,128]{3,2,1,0:T(8,128)S(1)}, u32[]{:S(2)}, u32[]{:S(2)}) collective-permute-start(f32[32,11,8,128]{3,2,1,0:T(8,128)S(1)} %add.63), channel_id=1, source_target_pairs={{0,2},{8,14},{16,18},{24,30},{32,34},{40,46},{48,50},{56,62},{2,0}... | collective-permute-start | bytes 4325384 | tf_op jit(solution)/shard_map/ppermute | solution.py:79
  21.0 18.9 %collective-permute-start.10 = (f32[32,10,8,128]{3,2,1,0:T(8,128)S(1)}, f32[32,10,8,128]{3,2,1,0:T(8,128)S(1)}, u32[]{:S(2)}, u32[]{:S(2)}) collective-permute-start(f32[32,10,8,128]{3,2,1,0:T(8,128)S(1)} %add.64), channel_id=1, source_target_pairs={{0,48},{8,24},{16,32},{24,8},{32,16},{40,56},{48,0},{56,40},{2,50}... | collective-permute-start | bytes 3932168 | tf_op jit(solution)/shard_map/ppermute | solution.py:79
  32.3 1.0 copy-start.16
  32.3 57.1 %copy-start.6 = (f32[512,512]{1,0:T(8,128)}, f32[512,512]{1,0:T(8,128)S(1)}, u32[]{:S(2)}) copy-start(f32[512,512]{1,0:T(8,128)S(1)} %get-tuple-element.54.lc) | copy-start | bytes 3145732
  32.3 57.1 %copy-start.8 = (bf16[512,512]{1,0:T(8,128)(2,1)}, bf16[512,512]{1,0:T(8,128)(2,1)S(1)}, u32[]{:S(2)}) copy-start(bf16[512,512]{1,0:T(8,128)(2,1)S(1)} %get-tuple-element.55.lkh) | copy-start | bytes 1572868
  32.3 57.1 %copy-start.10 = (bf16[512,512]{1,0:T(8,128)(2,1)}, bf16[512,512]{1,0:T(8,128)(2,1)S(1)}, u32[]{:S(2)}) copy-start(bf16[512,512]{1,0:T(8,128)(2,1)S(1)} %get-tuple-element.56.lkl) | copy-start | bytes 1572868
  32.3 57.1 %copy-start.12 = (bf16[512,512]{1,0:T(8,128)(2,1)}, bf16[512,512]{1,0:T(8,128)(2,1)S(1)}, u32[]{:S(2)}) copy-start(bf16[512,512]{1,0:T(8,128)(2,1)S(1)} %get-tuple-element.57.rkh) | copy-start | bytes 1572868
  32.3 57.1 %copy-start.14 = (bf16[512,512]{1,0:T(8,128)(2,1)}, bf16[512,512]{1,0:T(8,128)(2,1)S(1)}, u32[]{:S(2)}) copy-start(bf16[512,512]{1,0:T(8,128)(2,1)S(1)} %get-tuple-element.58.rkl) | copy-start | bytes 1572868
  35.2 11.9 %collective-permute-start.5 = (f32[16,11,8,128]{3,2,1,0:T(8,128)S(1)}, f32[16,11,8,128]{3,2,1,0:T(8,128)S(1)}, u32[]{:S(2)}, u32[]{:S(2)}) collective-permute-start(f32[16,11,8,128]{3,2,1,0:T(8,128)S(1)} %get-tuple-element.76), channel_id=1, source_target_pairs={{0,2},{8,14},{16,18},{24,30},{32,34},{40,46},{48,50},{56,62},{2,0}... | collective-permute-start | bytes 2162696 | tf_op jit(solution)/shard_map/ppermute | solution.py:79
  38.2 10.5 %collective-permute-start.8 = (f32[16,11,8,128]{3,2,1,0:T(8,128)S(1)}, f32[16,11,8,128]{3,2,1,0:T(8,128)S(1)}, u32[]{:S(2)}, u32[]{:S(2)}) collective-permute-start(f32[16,11,8,128]{3,2,1,0:T(8,128)S(1)} %get-tuple-element.74), channel_id=1, source_target_pairs={{0,48},{8,24},{16,32},{24,8},{32,16},{40,56},{48,0},{56,40},{2,50}... | collective-permute-start | bytes 2162696 | tf_op jit(solution)/shard_map/ppermute | solution.py:79
  40.0 11.4 %collective-permute-start.11 = (f32[16,10,8,128]{3,2,1,0:T(8,128)S(1)}, f32[16,10,8,128]{3,2,1,0:T(8,128)S(1)}, u32[]{:S(2)}, u32[]{:S(2)}) collective-permute-start(f32[16,10,8,128]{3,2,1,0:T(8,128)S(1)} %get-tuple-element.78), channel_id=1, source_target_pairs={{0,1},{8,73},{16,17},{24,89},{32,33},{40,105},{48,49},{56,121},{2,... | collective-permute-start | bytes 1966088 | tf_op jit(solution)/shard_map/ppermute | solution.py:79
  47.1 11.5 %collective-permute-start.6 = (f32[8,11,8,128]{3,2,1,0:T(8,128)S(1)}, f32[8,11,8,128]{3,2,1,0:T(8,128)S(1)}, u32[]{:S(2)}, u32[]{:S(2)}) collective-permute-start(f32[8,11,8,128]{3,2,1,0:T(8,128)S(1)} %get-tuple-element.81), channel_id=1, source_target_pairs={{0,48},{8,24},{16,32},{24,8},{32,16},{40,56},{48,0},{56,40},{2,50}... | collective-permute-start | bytes 1081352 | tf_op jit(solution)/shard_map/ppermute | solution.py:79
  48.8 9.9 %collective-permute-start.9 = (f32[8,11,8,128]{3,2,1,0:T(8,128)S(1)}, f32[8,11,8,128]{3,2,1,0:T(8,128)S(1)}, u32[]{:S(2)}, u32[]{:S(2)}) collective-permute-start(f32[8,11,8,128]{3,2,1,0:T(8,128)S(1)} %get-tuple-element.79), channel_id=1, source_target_pairs={{0,1},{8,73},{16,17},{24,89},{32,33},{40,105},{48,49},{56,121},{2,... | collective-permute-start | bytes 1081352 | tf_op jit(solution)/shard_map/ppermute | solution.py:79
  51.5 7.2 %collective-permute-start.12 = (f32[8,10,8,128]{3,2,1,0:T(8,128)S(1)}, f32[8,10,8,128]{3,2,1,0:T(8,128)S(1)}, u32[]{:S(2)}, u32[]{:S(2)}) collective-permute-start(f32[8,10,8,128]{3,2,1,0:T(8,128)S(1)} %get-tuple-element.83), channel_id=1, source_target_pairs={{0,2},{8,14},{16,18},{24,30},{32,34},{40,46},{48,50},{56,62},{2,0}... | collective-permute-start | bytes 983048 | tf_op jit(solution)/shard_map/ppermute | solution.py:79
  92.9 16.1 %all-to-all-start.2 = ((f32[8,64,512]{2,1,0:T(8,128)}), f32[8,64,512]{2,1,0:T(8,128)S(1)}, u32[]{:S(2)}, u32[]{:S(2)}) async-start(f32[8,64,512]{2,1,0:T(8,128)} %rows.1), calls=%async_computation.2 | async-start | bytes 2097152 | tf_op jit(solution)/shard_map/all_to_all | solution.py:360
  96.5 1.2 %copy-start.5 = (f32[1,512,512]{2,1,0:T(8,128)S(1)}, f32[1,512,512]{2,1,0:T(8,128)}, u32[]{:S(2)}) copy-start(f32[1,512,512]{2,1,0:T(8,128)} %rs.1) | copy-start | bytes 3145732
  97.7 1.2 %copy-start.7 = (f32[512,512]{1,0:T(8,128)S(1)}, f32[512,512]{1,0:T(8,128)}, u32[]{:S(2)}) copy-start(f32[512,512]{1,0:T(8,128)} %copy-done.6) | copy-start | bytes 3145732
  98.9 1.0 copy-start.9
  99.9 1.0 copy-start.11
  101.0 1.0 copy-start.13
  102.0 1.0 copy-start.15
  103.1 1.2 %copy-start.17 = (f32[512,512]{1,0:T(8,128)S(1)}, f32[512,512]{1,0:T(8,128)}, u32[]{:S(2)}) copy-start(f32[512,512]{1,0:T(8,128)} %copy-done.16) | copy-start | bytes 3145732
  109.0 7.6 %collective-permute-start.13 = (f32[8,64,512]{2,1,0:T(8,128)S(1)}, f32[8,64,512]{2,1,0:T(8,128)S(1)}, u32[]{:S(2)}, u32[]{:S(2)}) collective-permute-start(f32[8,64,512]{2,1,0:T(8,128)S(1)} %all-to-all-done.2.refs_0_), channel_id=1, source_target_pairs={{0,8},{8,0},{16,24},{24,16},{32,40},{40,32},{48,56},{56,48},{2,10}... | collective-permute-start | bytes 3145736 | tf_op jit(solution)/shard_map/ppermute | solution.py:79

commit v5 on v4

--- a/solution.py
+++ b/solution.py
@@ -235,7 +235,7 @@
     )(parts)
 
 
-def rows_kernel(table_ref, grad, lc, lkh, lkl, rkh, rkl, rch, rcl, out):
+def rows_kernel(table_ref, grad, lc, lkh, lkl, rkh, rkl, rch, rcl, out, value, sems):
     g = split(grad[...])
     rows = pl.ds(pl.multiple_of(table_ref[20] * ROWS, ROWS), ROWS)
     inner = thin_product((lkh[rows, :], lkl[rows, :]), g)
@@ -243,9 +243,22 @@
     turned = split(thin_product(split(left), g))
     inner = thin_product(turned, (rkh[...], rkl[...]))
     inner = thin_product(split(inner), g, NT)
-    value = thin_product(turned, (rch[...], rcl[...])) - thin_product(split(inner), g)
-    for i in range(8):
-        out[i] = value
+    inner = split(inner)
+    copies = []
+    for half in range(2):
+        cols = slice(half * 256, half * 256 + 256)
+        value[:, cols] = thin_product(turned, (rch[:, cols], rcl[:, cols])) - thin_product(
+            inner, tuple(term[:, cols] for term in g)
+        )
+        for i in range(8):
+            copies.append(
+                pltpu.make_async_copy(
+                    value.at[:, cols], out.at[i, :, cols], sems.at[8 * half + i]
+                )
+            )
+            copies[-1].start()
+    for copy in copies:
+        copy.wait()
 
 
 def precondition_rows(table, grad, constants):
@@ -253,7 +266,8 @@
         rows_kernel,
         out_shape=jax.ShapeDtypeStruct((8, ROWS, ORDER), jnp.float32),
         in_specs=[pl.BlockSpec(memory_space=pltpu.SMEM)] + whole(8),
-        out_specs=pl.BlockSpec(memory_space=pltpu.VMEM),
+        out_specs=pl.BlockSpec(memory_space=pl.ANY),
+        scratch_shapes=[pltpu.VMEM((ROWS, ORDER), jnp.float32), pltpu.SemaphoreType.DMA((16,))],
         compiler_params=pltpu.CompilerParams(vmem_limit_bytes=VMEM_LIMIT),
         name="rows",
     )(table, grad, *constants[:3], *constants[4:])

time: 119 us -> 119 us (level)
  no operation moved by 1% of the time
where the time goes in v5:
time: 119 us; the launch traced here: 118 us
  starting transfers between devices  30.9 us (26%)
  blocking collectives  30.4 us (26%)
  Pallas kernels  29 us (24%)
  waiting for transfers between devices  12.4 us (10%)
  local copies, waits for them, and re-layouts  11.9 us (10%)
  other arithmetic  2.39 us (2%)
    ppermute x14, starting transfers between devices, send(): return lax.ppermute(value, AXES, pairs)  27.4 us
    pallas_call x6, Pallas kernels, pack(): pl.pallas_call(functools.partial(pack_kernel, parts), out_shape=extra + p...  17.5 us
    all_to_all x1, blocking collectives, local(): lax.all_to_all(total(parts), ('y', 'xl'), 0, 0, tiled=True)  16.2 us
    all_to_all x1, blocking collectives, local(): lax.all_to_all(joined, AXES, 0, 0, axis_index_groups=CUBES, tiled=True)  14.3 us
    ppermute x14, waiting for transfers between devices, send(): return lax.ppermute(value, AXES, pairs)  12.4 us
    unnamed x36, local copies, waits for them, and re-layouts  11.8 us
    pallas_call x1, Pallas kernels, statistics(): pl.pallas_call(stats_kernel, out_shape=[jax.ShapeDtypeStruct((1, ORDER, O...  4.69 us
    all_to_all x1, starting transfers between devices, local(): got = lax.all_to_all(rows, ('xh', 'z'), 0, 0, tiled=True)  3.57 us
  transfers between devices with their start and end apart: 15, of which 5 were waited for; matrix products, arithmetic and copies ran while one was open for 1% of the time, Pallas kernels for 19%

profile of v5, /device:TPU:1, one launch (start us, length us, event | category | flops | bytes accessed | tf_op | source)
XLA Modules:
  0.0 118.3 jit_solution(13931085415719486358)
XLA Ops:
  0.6 0.8 select_reduce_fusion
  1.5 3.4 %copy-done = bf16[1,16,512,512]{3,2,1,0:T(8,128)(2,1)S(1)} copy-done((bf16[1,16,512,512]{3,2,1,0:T(8,128)(2,1)S(1)}, bf16[1,16,512,512]{3,2,1,0:T(8,128)(2,1)}, u32[]{:S(2)}) %copy-start) | copy-done | bytes 8388632
  4.9 1.1 other0.1
  6.0 1.5 %collective-permute-start = (f32[32,11,8,128]{3,2,1,0:T(8,128)S(1)}, f32[32,11,8,128]{3,2,1,0:T(8,128)S(1)}, u32[]{:S(2)}, u32[]{:S(2)}) collective-permute-start(f32[32,11,8,128]{3,2,1,0:T(8,128)S(1)} %other0.1), channel_id=1, source_target_pairs={{0,8},{8,0},{16,24},{24,16},{32,40},{40,32},{48,56},{56,48},{2,10}... | collective-permute-start | bytes 4325384 | tf_op jit(solution)/shard_map/ppermute | solution.py:79
  7.5 1.1 other1.1
  8.8 1.1 other2.1
  9.9 0.6 collective-permute-start.2
  10.5 2.3 %own.1 = (f32[32,11,8,128]{3,2,1,0:T(8,128)S(1)}, f32[32,11,8,128]{3,2,1,0:T(8,128)S(1)}, f32[32,10,8,128]{3,2,1,0:T(8,128)S(1)}) custom-call(s32[21]{0:T(128)S(1)} %concatenate.3.table_ref, bf16[1,16,512,512]{3,2,1,0:T(8,128)(2,1)S(1)} %copy-done), custom_call_target="tpu_custom_call" | custom-call | tf_op jit(solution)/shard_map/own/pallas_call | solution.py:163
  12.8 2.2 %otherkeep.1 = f32[32,32,8,128]{3,2,1,0:T(8,128)S(1)} custom-call(s32[21]{0:T(128)S(1)} %concatenate.3.table_ref, bf16[1,16,512,512]{3,2,1,0:T(8,128)(2,1)S(1)} %copy-done), custom_call_target="tpu_custom_call" | custom-call | tf_op jit(solution)/shard_map/otherkeep/pallas_call | solution.py:163
  15.1 0.1 add.62
  15.4 0.1 add.63
  15.6 2.6 %collective-permute-start.4 = (f32[32,11,8,128]{3,2,1,0:T(8,128)S(1)}, f32[32,11,8,128]{3,2,1,0:T(8,128)S(1)}, u32[]{:S(2)}, u32[]{:S(2)}) collective-permute-start(f32[32,11,8,128]{3,2,1,0:T(8,128)S(1)} %add.62), channel_id=1, source_target_pairs={{0,1},{8,73},{16,17},{24,89},{32,33},{40,105},{48,49},{56,121},{2,... | collective-permute-start | bytes 4325384 | tf_op jit(solution)/shard_map/ppermute | solution.py:79
  18.2 2.7 %collective-permute-start.7 = (f32[32,11,8,128]{3,2,1,0:T(8,128)S(1)}, f32[32,11,8,128]{3,2,1,0:T(8,128)S(1)}, u32[]{:S(2)}, u32[]{:S(2)}) collective-permute-start(f32[32,11,8,128]{3,2,1,0:T(8,128)S(1)} %add.63), channel_id=1, source_target_pairs={{0,2},{8,14},{16,18},{24,30},{32,34},{40,46},{48,50},{56,62},{2,0}... | collective-permute-start | bytes 4325384 | tf_op jit(solution)/shard_map/ppermute | solution.py:79
  21.0 1.6 %collective-permute-start.10 = (f32[32,10,8,128]{3,2,1,0:T(8,128)S(1)}, f32[32,10,8,128]{3,2,1,0:T(8,128)S(1)}, u32[]{:S(2)}, u32[]{:S(2)}) collective-permute-start(f32[32,10,8,128]{3,2,1,0:T(8,128)S(1)} %add.64), channel_id=1, source_target_pairs={{0,48},{8,24},{16,32},{24,8},{32,16},{40,56},{48,0},{56,40},{2,50}... | collective-permute-start | bytes 3932168 | tf_op jit(solution)/shard_map/ppermute | solution.py:79
  22.6 9.6 %keep.1 = (f32[512,512]{1,0:T(8,128)S(1)}, bf16[512,512]{1,0:T(8,128)(2,1)S(1)}, bf16[512,512]{1,0:T(8,128)(2,1)S(1)}, f32[512,512]{1,0:T(8,128)S(1)}, bf16[512,...) custom-call(s32[21]{0:T(128)S(1)} %concatenate.3.table_ref, ...), custom_call_target="tpu_custom_call" | custom-call | tf_op jit(solution)/shard_map/keep/pallas_call | solution.py:163
  32.3 0.4 slice_add_fusion
  32.7 0.6 copy-done.16
  33.3 1.8 %collective-permute-done.4 = f32[32,11,8,128]{3,2,1,0:T(8,128)S(1)} collective-permute-done((f32[32,11,8,128]{3,2,1,0:T(8,128)S(1)}, f32[32,11,8,128]{3,2,1,0:T(8,128)S(1)}, u32[]{:S(2)}, u32[]{:S(2)}) %collective-permute-start.4) | collective-permute-done | bytes 1441824 | tf_op jit(solution)/shard_map/ppermute | solution.py:79
  35.0 0.1 slice_add_fusion.6
  35.2 2.9 %collective-permute-start.5 = (f32[16,11,8,128]{3,2,1,0:T(8,128)S(1)}, f32[16,11,8,128]{3,2,1,0:T(8,128)S(1)}, u32[]{:S(2)}, u32[]{:S(2)}) collective-permute-start(f32[16,11,8,128]{3,2,1,0:T(8,128)S(1)} %get-tuple-element.76), channel_id=1, source_target_pairs={{0,2},{8,14},{16,18},{24,30},{32,34},{40,46},{48,50},{56,62},{2,0}... | collective-permute-start | bytes 2162696 | tf_op jit(solution)/shard_map/ppermute | solution.py:79
  38.1 0.1 slice_add_fusion.4
  38.2 1.4 %collective-permute-start.8 = (f32[16,11,8,128]{3,2,1,0:T(8,128)S(1)}, f32[16,11,8,128]{3,2,1,0:T(8,128)S(1)}, u32[]{:S(2)}, u32[]{:S(2)}) collective-permute-start(f32[16,11,8,128]{3,2,1,0:T(8,128)S(1)} %get-tuple-element.74), channel_id=1, source_target_pairs={{0,48},{8,24},{16,32},{24,8},{32,16},{40,56},{48,0},{56,40},{2,50}... | collective-permute-start | bytes 2162696 | tf_op jit(solution)/shard_map/ppermute | solution.py:79
  39.7 0.2 slice_add_fusion.2
  39.9 0.1 slice_add_fusion.8
  40.0 2.6 %collective-permute-start.11 = (f32[16,10,8,128]{3,2,1,0:T(8,128)S(1)}, f32[16,10,8,128]{3,2,1,0:T(8,128)S(1)}, u32[]{:S(2)}, u32[]{:S(2)}) collective-permute-start(f32[16,10,8,128]{3,2,1,0:T(8,128)S(1)} %get-tuple-element.78), channel_id=1, source_target_pairs={{0,1},{8,73},{16,17},{24,89},{32,33},{40,105},{48,49},{56,121},{2,... | collective-permute-start | bytes 1966088 | tf_op jit(solution)/shard_map/ppermute | solution.py:79
  42.6 4.5 %collective-permute-done.5 = f32[16,11,8,128]{3,2,1,0:T(8,128)S(1)} collective-permute-done((f32[16,11,8,128]{3,2,1,0:T(8,128)S(1)}, f32[16,11,8,128]{3,2,1,0:T(8,128)S(1)}, u32[]{:S(2)}, u32[]{:S(2)}) %collective-permute-start.5) | collective-permute-done | bytes 720928 | tf_op jit(solution)/shard_map/ppermute | solution.py:79
  47.1 1.1 collective-permute-start.6
  48.3 0.5 collective-permute-done.8
  48.8 2.6 %collective-permute-start.9 = (f32[8,11,8,128]{3,2,1,0:T(8,128)S(1)}, f32[8,11,8,128]{3,2,1,0:T(8,128)S(1)}, u32[]{:S(2)}, u32[]{:S(2)}) collective-permute-start(f32[8,11,8,128]{3,2,1,0:T(8,128)S(1)} %get-tuple-element.79), channel_id=1, source_target_pairs={{0,1},{8,73},{16,17},{24,89},{32,33},{40,105},{48,49},{56,121},{2,... | collective-permute-start | bytes 1081352 | tf_op jit(solution)/shard_map/ppermute | solution.py:79
  51.5 2.3 %collective-permute-start.12 = (f32[8,10,8,128]{3,2,1,0:T(8,128)S(1)}, f32[8,10,8,128]{3,2,1,0:T(8,128)S(1)}, u32[]{:S(2)}, u32[]{:S(2)}) collective-permute-start(f32[8,10,8,128]{3,2,1,0:T(8,128)S(1)} %get-tuple-element.83), channel_id=1, source_target_pairs={{0,2},{8,14},{16,18},{24,30},{32,34},{40,46},{48,50},{56,62},{2,0}... | collective-permute-start | bytes 983048 | tf_op jit(solution)/shard_map/ppermute | solution.py:79
  53.7 5.0 %collective-permute-done.12.r2 = f32[8,10,8,128]{3,2,1,0:T(8,128)S(1)} collective-permute-done((f32[8,10,8,128]{3,2,1,0:T(8,128)S(1)}, f32[8,10,8,128]{3,2,1,0:T(8,128)S(1)}, u32[]{:S(2)}, u32[]{:S(2)}) %collective-permute-start.12) | collective-permute-done | bytes 327712 | tf_op jit(solution)/shard_map/ppermute | solution.py:79
  58.7 0.1 join.1
  58.8 14.3 %all_to_all.15.parts = f32[8,32,8,128]{3,2,1,0:T(8,128)S(1)} all-to-all(f32[8,32,8,128]{3,2,1,0:T(8,128)S(1)} %join.1), channel_id=1, replica_groups={{87,71,81,65,22,6,16,0},{119,103,113,97,54,38,48,32},{85,69,83,67,20,4,..., dimensions={0} | all-to-all | bytes 2097152 | tf_op jit(solution)/shard_map/all_to_all | solution.py:371
  73.2 16.2 %all_to_all.16 = f32[8,64,512]{2,1,0:T(8,128)S(1)} all-to-all(f32[8,64,512]{2,1,0:T(8,128)S(1)} %total.1), channel_id=1, replica_groups=mesh['xh'=2,'z'=4,'core'=2,'y'=4,'xl'=2] {'y','xl'}, dimensions={0} | all-to-all | bytes 2097152 | tf_op jit(solution)/shard_map/all_to_all | solution.py:372
  89.4 3.4 %rows.1 = f32[8,64,512]{2,1,0:T(8,128)} custom-call(s32[21]{0:T(128)S(1)} %concatenate.3.table_ref, f32[512,512]{1,0:T(8,128)S(1)} %bitcast.6, f32[512,512]{1,0:T(8,128)S(1)} %get-tuple-element.54.lc, bf16[512,512]{1,0:T(8,128)(2,1)S(1)} %get-tuple-element.55.lkh, bf16[512,512]{1,0:T(8,128)(2,1)S(1)} %get-tuple-element.56.lkl, ...), custom_call_target="tpu_custom_call" | custom-call | tf_op jit(solution)/shard_map/rows/pallas_call | solution.py:265
  92.9 3.6 %all-to-all-start.2 = ((f32[8,64,512]{2,1,0:T(8,128)}), f32[8,64,512]{2,1,0:T(8,128)S(1)}, u32[]{:S(2)}, u32[]{:S(2)}) async-start(f32[8,64,512]{2,1,0:T(8,128)} %rows.1), calls=%async_computation.2 | async-start | bytes 2097152 | tf_op jit(solution)/shard_map/all_to_all | solution.py:374
  96.5 1.2 %copy-done.5 = f32[1,512,512]{2,1,0:T(8,128)S(1)} copy-done((f32[1,512,512]{2,1,0:T(8,128)S(1)}, f32[1,512,512]{2,1,0:T(8,128)}, u32[]{:S(2)}) %copy-start.5) | copy-done | bytes 1048600
  97.7 1.2 %copy-done.7 = f32[512,512]{1,0:T(8,128)S(1)} copy-done((f32[512,512]{1,0:T(8,128)S(1)}, f32[512,512]{1,0:T(8,128)}, u32[]{:S(2)}) %copy-start.7) | copy-done | bytes 1048600
  98.9 1.0 copy-done.9
  99.9 1.0 copy-done.11
  101.0 1.0 copy-done.13
  102.0 1.0 copy-done.15
  103.1 1.2 %copy-done.17 = f32[512,512]{1,0:T(8,128)S(1)} copy-done((f32[512,512]{1,0:T(8,128)S(1)}, f32[512,512]{1,0:T(8,128)}, u32[]{:S(2)}) %copy-start.17) | copy-done | bytes 1048600
  104.3 4.7 %stats.1 = (f32[1,512,512]{2,1,0:T(8,128)}, f32[1,512,512]{2,1,0:T(8,128)}, f32[1,512,512]{2,1,0:T(8,128)}, f32[1,512,512]{2,1,0:T(8,128)}) custom-call(f32[512,512]{1,0:T(8,128)S(1)} %bitcast.7, f32[512,512]{1,0:T(8,128)S(1)} %copy-done.7, bf16[512,512]{1,0:T(8,128)(2,1)S(1)} %copy-done.9, bf16[512,512]{1,0:T(8,128)(2,1)S(1)} %copy-done.11, ...), custom_call_target="tpu_custom_call" | custom-call | flops 3221225472 | bytes 11534336 | tf_op jit(solution)/shard_map/stats/pallas_call | solution.py:288
  109.0 5.3 %collective-permute-start.13 = (f32[8,64,512]{2,1,0:T(8,128)S(1)}, f32[8,64,512]{2,1,0:T(8,128)S(1)}, u32[]{:S(2)}, u32[]{:S(2)}) collective-permute-start(f32[8,64,512]{2,1,0:T(8,128)S(1)} %all-to-all-done.2.refs_0_), channel_id=1, source_target_pairs={{0,8},{8,0},{16,24},{24,16},{32,40},{40,32},{48,56},{56,48},{2,10}... | collective-permute-start | bytes 3145736 | tf_op jit(solution)/shard_map/ppermute | solution.py:79
  114.3 1.6 %spread.1.refs_1_ = f32[16,64,512]{2,1,0:T(8,128)} custom-call(s32[21]{0:T(128)S(1)} %concatenate.3.table_ref, f32[8,64,512]{2,1,0:T(8,128)S(1)} %all-to-all-done.2.refs_0_), custom_call_target="tpu_custom_call" | custom-call | tf_op jit(solution)/shard_map/spread/pallas_call | solution.py:315
  115.8 0.7 collective-permute-done.13.refs_0_
  116.6 1.6 %spread_late.1 = f32[16,64,512]{2,1,0:T(8,128)} custom-call(s32[21]{0:T(128)S(1)} %concatenate.3.table_ref, f32[8,64,512]{2,1,0:T(8,128)S(1)} %collective-permute-done.13.refs_0_, f32[16,64,512]{2,1,0:T(8,128)} %spread.1.refs_1_), custom_call_target="tpu_custom_call", output_to_operand_aliasing={{}: (2, {})} | custom-call | tf_op jit(solution)/shard_map/spread_late/pallas_call | solution.py:315
  (45 shorter events, 0.8 us)
Async XLA Ops:
  1.5 3.4 %copy-start = (bf16[1,16,512,512]{3,2,1,0:T(8,128)(2,1)S(1)}, bf16[1,16,512,512]{3,2,1,0:T(8,128)(2,1)}, u32[]{:S(2)}) copy-start(bf16[1,16,512,512]{3,2,1,0:T(8,128)(2,1)} %blocks.11) | copy-start | bytes 25165828
  6.0 9.1 %collective-permute-start = (f32[32,11,8,128]{3,2,1,0:T(8,128)S(1)}, f32[32,11,8,128]{3,2,1,0:T(8,128)S(1)}, u32[]{:S(2)}, u32[]{:S(2)}) collective-permute-start(f32[32,11,8,128]{3,2,1,0:T(8,128)S(1)} %other0.1), channel_id=1, source_target_pairs={{0,8},{8,0},{16,24},{24,16},{32,40},{40,32},{48,56},{56,48},{2,10}... | collective-permute-start | bytes 4325384 | tf_op jit(solution)/shard_map/ppermute | solution.py:79
  8.7 6.7 %collective-permute-start.1 = (f32[32,11,8,128]{3,2,1,0:T(8,128)S(1)}, f32[32,11,8,128]{3,2,1,0:T(8,128)S(1)}, u32[]{:S(2)}, u32[]{:S(2)}) collective-permute-start(f32[32,11,8,128]{3,2,1,0:T(8,128)S(1)} %other1.1), channel_id=1, source_target_pairs={{0,8},{8,0},{16,24},{24,16},{32,40},{40,32},{48,56},{56,48},{2,10}... | collective-permute-start | bytes 4325384 | tf_op jit(solution)/shard_map/ppermute | solution.py:79
  9.9 5.0 %collective-permute-start.2 = (f32[32,10,8,128]{3,2,1,0:T(8,128)S(1)}, f32[32,10,8,128]{3,2,1,0:T(8,128)S(1)}, u32[]{:S(2)}, u32[]{:S(2)}) collective-permute-start(f32[32,10,8,128]{3,2,1,0:T(8,128)S(1)} %other2.1), channel_id=1, source_target_pairs={{0,8},{8,0},{16,24},{24,16},{32,40},{40,32},{48,56},{56,48},{2,10}... | collective-permute-start | bytes 3932168 | tf_op jit(solution)/shard_map/ppermute | solution.py:79
  15.3 7.3 %copy-start.1 = (f32[1,512,512]{2,1,0:T(8,128)S(1)}, f32[1,512,512]{2,1,0:T(8,128)}, u32[]{:S(2)}) copy-start(f32[1,512,512]{2,1,0:T(8,128)} %rest_2_.1) | copy-start | bytes 3145732
  15.3 7.3 %copy-start.2 = (f32[1,512,512]{2,1,0:T(8,128)S(1)}, f32[1,512,512]{2,1,0:T(8,128)}, u32[]{:S(2)}) copy-start(f32[1,512,512]{2,1,0:T(8,128)} %rest_3_.1) | copy-start | bytes 3145732
  15.3 7.3 %copy-start.3 = (f32[1,512,512]{2,1,0:T(8,128)S(1)}, f32[1,512,512]{2,1,0:T(8,128)}, u32[]{:S(2)}) copy-start(f32[1,512,512]{2,1,0:T(8,128)} %ls.1) | copy-start | bytes 3145732
  15.3 7.3 %copy-start.4 = (f32[1,512,512]{2,1,0:T(8,128)S(1)}, f32[1,512,512]{2,1,0:T(8,128)}, u32[]{:S(2)}) copy-start(f32[1,512,512]{2,1,0:T(8,128)} %rs.1) | copy-start | bytes 3145732
  15.5 16.8 %collective-permute-start.3 = (f32[32,32,8,128]{3,2,1,0:T(8,128)S(1)}, f32[32,32,8,128]{3,2,1,0:T(8,128)S(1)}, u32[]{:S(2)}, u32[]{:S(2)}) collective-permute-start(f32[32,32,8,128]{3,2,1,0:T(8,128)S(1)} %otherkeep.1), channel_id=1, source_target_pairs={{0,8},{8,0},{16,24},{24,16},{32,40},{40,32},{48,56},{56,48},{2,10}... | collective-permute-start | bytes 12582920 | tf_op jit(solution)/shard_map/ppermute | solution.py:79
  15.6 19.4 %collective-permute-start.4 = (f32[32,11,8,128]{3,2,1,0:T(8,128)S(1)}, f32[32,11,8,128]{3,2,1,0:T(8,128)S(1)}, u32[]{:S(2)}, u32[]{:S(2)}) collective-permute-start(f32[32,11,8,128]{3,2,1,0:T(8,128)S(1)} %add.62), channel_id=1, source_target_pairs={{0,1},{8,73},{16,17},{24,89},{32,33},{40,105},{48,49},{56,121},{2,... | collective-permute-start | bytes 4325384 | tf_op jit(solution)/shard_map/ppermute | solution.py:79
  18.2 19.9 %collective-permute-start.7 = (f32[32,11,8,128]{3,2,1,0:T(8,128)S(1)}, f32[32,11,8,128]{3,2,1,0:T(8,128)S(1)}, u32[]{:S(2)}, u32[]{:S(2)}) collective-permute-start(f32[32,11,8,128]{3,2,1,0:T(8,128)S(1)} %add.63), channel_id=1, source_target_pairs={{0,2},{8,14},{16,18},{24,30},{32,34},{40,46},{48,50},{56,62},{2,0}... | collective-permute-start | bytes 4325384 | tf_op jit(solution)/shard_map/ppermute | solution.py:79
  21.0 18.9 %collective-permute-start.10 = (f32[32,10,8,128]{3,2,1,0:T(8,128)S(1)}, f32[32,10,8,128]{3,2,1,0:T(8,128)S(1)}, u32[]{:S(2)}, u32[]{:S(2)}) collective-permute-start(f32[32,10,8,128]{3,2,1,0:T(8,128)S(1)} %add.64), channel_id=1, source_target_pairs={{0,48},{8,24},{16,32},{24,8},{32,16},{40,56},{48,0},{56,40},{2,50}... | collective-permute-start | bytes 3932168 | tf_op jit(solution)/shard_map/ppermute | solution.py:79
  32.3 1.0 copy-start.16
  32.3 57.1 %copy-start.6 = (f32[512,512]{1,0:T(8,128)}, f32[512,512]{1,0:T(8,128)S(1)}, u32[]{:S(2)}) copy-start(f32[512,512]{1,0:T(8,128)S(1)} %get-tuple-element.54.lc) | copy-start | bytes 3145732
  32.3 57.1 %copy-start.8 = (bf16[512,512]{1,0:T(8,128)(2,1)}, bf16[512,512]{1,0:T(8,128)(2,1)S(1)}, u32[]{:S(2)}) copy-start(bf16[512,512]{1,0:T(8,128)(2,1)S(1)} %get-tuple-element.55.lkh) | copy-start | bytes 1572868
  32.3 57.1 %copy-start.10 = (bf16[512,512]{1,0:T(8,128)(2,1)}, bf16[512,512]{1,0:T(8,128)(2,1)S(1)}, u32[]{:S(2)}) copy-start(bf16[512,512]{1,0:T(8,128)(2,1)S(1)} %get-tuple-element.56.lkl) | copy-start | bytes 1572868
  32.3 57.1 %copy-start.12 = (bf16[512,512]{1,0:T(8,128)(2,1)}, bf16[512,512]{1,0:T(8,128)(2,1)S(1)}, u32[]{:S(2)}) copy-start(bf16[512,512]{1,0:T(8,128)(2,1)S(1)} %get-tuple-element.57.rkh) | copy-start | bytes 1572868
  32.3 57.1 %copy-start.14 = (bf16[512,512]{1,0:T(8,128)(2,1)}, bf16[512,512]{1,0:T(8,128)(2,1)S(1)}, u32[]{:S(2)}) copy-start(bf16[512,512]{1,0:T(8,128)(2,1)S(1)} %get-tuple-element.58.rkl) | copy-start | bytes 1572868
  35.2 11.9 %collective-permute-start.5 = (f32[16,11,8,128]{3,2,1,0:T(8,128)S(1)}, f32[16,11,8,128]{3,2,1,0:T(8,128)S(1)}, u32[]{:S(2)}, u32[]{:S(2)}) collective-permute-start(f32[16,11,8,128]{3,2,1,0:T(8,128)S(1)} %get-tuple-element.76), channel_id=1, source_target_pairs={{0,2},{8,14},{16,18},{24,30},{32,34},{40,46},{48,50},{56,62},{2,0}... | collective-permute-start | bytes 2162696 | tf_op jit(solution)/shard_map/ppermute | solution.py:79
  38.2 10.5 %collective-permute-start.8 = (f32[16,11,8,128]{3,2,1,0:T(8,128)S(1)}, f32[16,11,8,128]{3,2,1,0:T(8,128)S(1)}, u32[]{:S(2)}, u32[]{:S(2)}) collective-permute-start(f32[16,11,8,128]{3,2,1,0:T(8,128)S(1)} %get-tuple-element.74), channel_id=1, source_target_pairs={{0,48},{8,24},{16,32},{24,8},{32,16},{40,56},{48,0},{56,40},{2,50}... | collective-permute-start | bytes 2162696 | tf_op jit(solution)/shard_map/ppermute | solution.py:79
  40.0 11.4 %collective-permute-start.11 = (f32[16,10,8,128]{3,2,1,0:T(8,128)S(1)}, f32[16,10,8,128]{3,2,1,0:T(8,128)S(1)}, u32[]{:S(2)}, u32[]{:S(2)}) collective-permute-start(f32[16,10,8,128]{3,2,1,0:T(8,128)S(1)} %get-tuple-element.78), channel_id=1, source_target_pairs={{0,1},{8,73},{16,17},{24,89},{32,33},{40,105},{48,49},{56,121},{2,... | collective-permute-start | bytes 1966088 | tf_op jit(solution)/shard_map/ppermute | solution.py:79
  47.1 11.5 %collective-permute-start.6 = (f32[8,11,8,128]{3,2,1,0:T(8,128)S(1)}, f32[8,11,8,128]{3,2,1,0:T(8,128)S(1)}, u32[]{:S(2)}, u32[]{:S(2)}) collective-permute-start(f32[8,11,8,128]{3,2,1,0:T(8,128)S(1)} %get-tuple-element.81), channel_id=1, source_target_pairs={{0,48},{8,24},{16,32},{24,8},{32,16},{40,56},{48,0},{56,40},{2,50}... | collective-permute-start | bytes 1081352 | tf_op jit(solution)/shard_map/ppermute | solution.py:79
  48.8 9.9 %collective-permute-start.9 = (f32[8,11,8,128]{3,2,1,0:T(8,128)S(1)}, f32[8,11,8,128]{3,2,1,0:T(8,128)S(1)}, u32[]{:S(2)}, u32[]{:S(2)}) collective-permute-start(f32[8,11,8,128]{3,2,1,0:T(8,128)S(1)} %get-tuple-element.79), channel_id=1, source_target_pairs={{0,1},{8,73},{16,17},{24,89},{32,33},{40,105},{48,49},{56,121},{2,... | collective-permute-start | bytes 1081352 | tf_op jit(solution)/shard_map/ppermute | solution.py:79
  51.5 7.2 %collective-permute-start.12 = (f32[8,10,8,128]{3,2,1,0:T(8,128)S(1)}, f32[8,10,8,128]{3,2,1,0:T(8,128)S(1)}, u32[]{:S(2)}, u32[]{:S(2)}) collective-permute-start(f32[8,10,8,128]{3,2,1,0:T(8,128)S(1)} %get-tuple-element.83), channel_id=1, source_target_pairs={{0,2},{8,14},{16,18},{24,30},{32,34},{40,46},{48,50},{56,62},{2,0}... | collective-permute-start | bytes 983048 | tf_op jit(solution)/shard_map/ppermute | solution.py:79
  92.9 16.1 %all-to-all-start.2 = ((f32[8,64,512]{2,1,0:T(8,128)}), f32[8,64,512]{2,1,0:T(8,128)S(1)}, u32[]{:S(2)}, u32[]{:S(2)}) async-start(f32[8,64,512]{2,1,0:T(8,128)} %rows.1), calls=%async_computation.2 | async-start | bytes 2097152 | tf_op jit(solution)/shard_map/all_to_all | solution.py:374
  96.4 1.2 %copy-start.5 = (f32[1,512,512]{2,1,0:T(8,128)S(1)}, f32[1,512,512]{2,1,0:T(8,128)}, u32[]{:S(2)}) copy-start(f32[1,512,512]{2,1,0:T(8,128)} %rs.1) | copy-start | bytes 3145732
  97.7 1.2 %copy-start.7 = (f32[512,512]{1,0:T(8,128)S(1)}, f32[512,512]{1,0:T(8,128)}, u32[]{:S(2)}) copy-start(f32[512,512]{1,0:T(8,128)} %copy-done.6) | copy-start | bytes 3145732
  98.9 1.0 copy-start.9
  99.9 1.0 copy-start.11
  101.0 1.0 copy-start.13
  102.0 1.0 copy-start.15
  103.1 1.2 %copy-start.17 = (f32[512,512]{1,0:T(8,128)S(1)}, f32[512,512]{1,0:T(8,128)}, u32[]{:S(2)}) copy-start(f32[512,512]{1,0:T(8,128)} %copy-done.16) | copy-start | bytes 3145732
  109.0 7.6 %collective-permute-start.13 = (f32[8,64,512]{2,1,0:T(8,128)S(1)}, f32[8,64,512]{2,1,0:T(8,128)S(1)}, u32[]{:S(2)}, u32[]{:S(2)}) collective-permute-start(f32[8,64,512]{2,1,0:T(8,128)S(1)} %all-to-all-done.2.refs_0_), channel_id=1, source_target_pairs={{0,8},{8,0},{16,24},{24,16},{32,40},{40,32},{48,56},{56,48},{2,10}... | collective-permute-start | bytes 3145736 | tf_op jit(solution)/shard_map/ppermute | solution.py:79

commit v6 on v4

--- a/solution.py
+++ b/solution.py
@@ -99,6 +99,18 @@
         return lax.dot_general(a, b, (dims, ((), ())), preferred_element_type=jnp.float32)
 
     return dot(fh, sh) + (dot(fh, sl) + dot(fl, sh))
+
+
+NARROW = [
+    [index_of(2 * xh + xl, y, z, c) for y in range(4)[::-1] for xl in BITS[::-1]]
+    for xh in BITS
+    for z in range(4)
+    for c in BITS
+]
+
+
+def gradient(pieces_ref):
+    return jnp.concatenate([pieces_ref[7 - n] for n in range(8)], axis=0)
 
 
 def thin_product(first, second, dims=((1,), (0,))):
@@ -236,7 +248,7 @@
 
 
 def rows_kernel(table_ref, grad, lc, lkh, lkl, rkh, rkl, rch, rcl, out):
-    g = split(grad[...])
+    g = split(gradient(grad))
     rows = pl.ds(pl.multiple_of(table_ref[20] * ROWS, ROWS), ROWS)
     inner = thin_product((lkh[rows, :], lkl[rows, :]), g)
     left = lc[rows, :] - thin_product(split(inner), g, NT)
@@ -260,7 +272,7 @@
 
 
 def stats_kernel(grad, lc, lkh, lkl, rc, rkh, rkl, ls, rs, ln, rn, li, ri):
-    g = split(grad[...])
+    g = split(gradient(grad))
     for dims, stat_ref, c_ref, kh, kl, new_ref, inv_ref in (
         (NT, ls, lc, lkh, lkl, ln, li),
         (TN, rs, rc, rkh, rkl, rn, ri),
@@ -355,7 +367,7 @@
             kept[s] = kept[s][:half] + got[:half]
     joined = join([value for pair in tails for value in pair])
     parts = lax.all_to_all(joined, AXES, 0, 0, axis_index_groups=CUBES, tiled=True)
-    grad = lax.all_to_all(total(parts), ("y", "xl"), 0, 0, tiled=True).reshape(ORDER, ORDER)
+    grad = lax.all_to_all(total(parts), AXES, 0, 0, axis_index_groups=NARROW, tiled=True)
     rows = precondition_rows(table, grad, constants)
     got = lax.all_to_all(rows, ("xh", "z"), 0, 0, tiled=True)
     stats = statistics(grad, constants, left_stat, right_stat)

time: 119 us -> 119 us (level)
  no operation moved by 1% of the time
where the time goes in v6:
time: 119 us
  blocking collectives  31 us (26%)
  starting transfers between devices  30.8 us (26%)
  Pallas kernels  29.1 us (24%)
  waiting for transfers between devices  12.4 us (10%)
  local copies, waits for them, and re-layouts  11.9 us (10%)
  other arithmetic  2.39 us (2%)
    ppermute x14, starting transfers between devices, send(): return lax.ppermute(value, AXES, pairs)  26.6 us
    pallas_call x6, Pallas kernels, pack(): pl.pallas_call(functools.partial(pack_kernel, parts), out_shape=extra + p...  17.5 us
    all_to_all x1, blocking collectives, local(): lax.all_to_all(total(parts), AXES, 0, 0, axis_index_groups=NARROW, tiled=...  16.7 us
    all_to_all x1, blocking collectives, local(): lax.all_to_all(joined, AXES, 0, 0, axis_index_groups=CUBES, tiled=True)  14.3 us
    ppermute x14, waiting for transfers between devices, send(): return lax.ppermute(value, AXES, pairs)  12.4 us
    unnamed x36, local copies, waits for them, and re-layouts  11.8 us
    pallas_call x1, Pallas kernels, statistics(): pl.pallas_call(stats_kernel, out_shape=[jax.ShapeDtypeStruct((1, ORDER, O...  4.7 us
    all_to_all x1, starting transfers between devices, local(): got = lax.all_to_all(rows, ('xh', 'z'), 0, 0, tiled=True)  4.16 us
  transfers between devices with their start and end apart: 15, of which 5 were waited for; matrix products, arithmetic and copies ran while one was open for 1% of the time, Pallas kernels for 19%

profile of v6, /device:TPU:1, one launch (start us, length us, event | category | flops | bytes accessed | tf_op | source)
XLA Modules:
  0.0 118.7 jit_solution(2699551502758164881)
XLA Ops:
  0.6 0.8 select_reduce_fusion
  1.5 3.4 %copy-done = bf16[1,16,512,512]{3,2,1,0:T(8,128)(2,1)S(1)} copy-done((bf16[1,16,512,512]{3,2,1,0:T(8,128)(2,1)S(1)}, bf16[1,16,512,512]{3,2,1,0:T(8,128)(2,1)}, u32[]{:S(2)}) %copy-start) | copy-done | bytes 8388632
  4.9 1.1 other0.1
  6.0 1.5 %collective-permute-start = (f32[32,11,8,128]{3,2,1,0:T(8,128)S(1)}, f32[32,11,8,128]{3,2,1,0:T(8,128)S(1)}, u32[]{:S(2)}, u32[]{:S(2)}) collective-permute-start(f32[32,11,8,128]{3,2,1,0:T(8,128)S(1)} %other0.1), channel_id=1, source_target_pairs={{0,8},{8,0},{16,24},{24,16},{32,40},{40,32},{48,56},{56,48},{2,10}... | collective-permute-start | bytes 4325384 | tf_op jit(solution)/shard_map/ppermute | solution.py:79
  7.5 1.1 other1.1
  8.8 1.1 other2.1
  9.9 0.6 collective-permute-start.2
  10.5 2.3 %own.1 = (f32[32,11,8,128]{3,2,1,0:T(8,128)S(1)}, f32[32,11,8,128]{3,2,1,0:T(8,128)S(1)}, f32[32,10,8,128]{3,2,1,0:T(8,128)S(1)}) custom-call(s32[21]{0:T(128)S(1)} %concatenate.3.table_ref, bf16[1,16,512,512]{3,2,1,0:T(8,128)(2,1)S(1)} %copy-done), custom_call_target="tpu_custom_call" | custom-call | tf_op jit(solution)/shard_map/own/pallas_call | solution.py:175
  12.8 2.2 %otherkeep.1 = f32[32,32,8,128]{3,2,1,0:T(8,128)S(1)} custom-call(s32[21]{0:T(128)S(1)} %concatenate.3.table_ref, bf16[1,16,512,512]{3,2,1,0:T(8,128)(2,1)S(1)} %copy-done), custom_call_target="tpu_custom_call" | custom-call | tf_op jit(solution)/shard_map/otherkeep/pallas_call | solution.py:175
  15.1 0.1 add.62
  15.4 0.1 add.63
  15.6 2.6 %collective-permute-start.4 = (f32[32,11,8,128]{3,2,1,0:T(8,128)S(1)}, f32[32,11,8,128]{3,2,1,0:T(8,128)S(1)}, u32[]{:S(2)}, u32[]{:S(2)}) collective-permute-start(f32[32,11,8,128]{3,2,1,0:T(8,128)S(1)} %add.62), channel_id=1, source_target_pairs={{0,1},{8,73},{16,17},{24,89},{32,33},{40,105},{48,49},{56,121},{2,... | collective-permute-start | bytes 4325384 | tf_op jit(solution)/shard_map/ppermute | solution.py:79
  18.2 2.7 %collective-permute-start.7 = (f32[32,11,8,128]{3,2,1,0:T(8,128)S(1)}, f32[32,11,8,128]{3,2,1,0:T(8,128)S(1)}, u32[]{:S(2)}, u32[]{:S(2)}) collective-permute-start(f32[32,11,8,128]{3,2,1,0:T(8,128)S(1)} %add.63), channel_id=1, source_target_pairs={{0,2},{8,14},{16,18},{24,30},{32,34},{40,46},{48,50},{56,62},{2,0}... | collective-permute-start | bytes 4325384 | tf_op jit(solution)/shard_map/ppermute | solution.py:79
  21.0 1.6 %collective-permute-start.10 = (f32[32,10,8,128]{3,2,1,0:T(8,128)S(1)}, f32[32,10,8,128]{3,2,1,0:T(8,128)S(1)}, u32[]{:S(2)}, u32[]{:S(2)}) collective-permute-start(f32[32,10,8,128]{3,2,1,0:T(8,128)S(1)} %add.64), channel_id=1, source_target_pairs={{0,48},{8,24},{16,32},{24,8},{32,16},{40,56},{48,0},{56,40},{2,50}... | collective-permute-start | bytes 3932168 | tf_op jit(solution)/shard_map/ppermute | solution.py:79
  22.6 9.6 %keep.1 = (f32[512,512]{1,0:T(8,128)S(1)}, bf16[512,512]{1,0:T(8,128)(2,1)S(1)}, bf16[512,512]{1,0:T(8,128)(2,1)S(1)}, f32[512,512]{1,0:T(8,128)S(1)}, bf16[512,...) custom-call(s32[21]{0:T(128)S(1)} %concatenate.3.table_ref, ...), custom_call_target="tpu_custom_call" | custom-call | tf_op jit(solution)/shard_map/keep/pallas_call | solution.py:175
  32.3 0.4 slice_add_fusion
  32.7 0.6 copy-done.16
  33.3 1.8 %collective-permute-done.4 = f32[32,11,8,128]{3,2,1,0:T(8,128)S(1)} collective-permute-done((f32[32,11,8,128]{3,2,1,0:T(8,128)S(1)}, f32[32,11,8,128]{3,2,1,0:T(8,128)S(1)}, u32[]{:S(2)}, u32[]{:S(2)}) %collective-permute-start.4) | collective-permute-done | bytes 1441824 | tf_op jit(solution)/shard_map/ppermute | solution.py:79
  35.0 0.1 slice_add_fusion.6
  35.2 2.9 %collective-permute-start.5 = (f32[16,11,8,128]{3,2,1,0:T(8,128)S(1)}, f32[16,11,8,128]{3,2,1,0:T(8,128)S(1)}, u32[]{:S(2)}, u32[]{:S(2)}) collective-permute-start(f32[16,11,8,128]{3,2,1,0:T(8,128)S(1)} %get-tuple-element.76), channel_id=1, source_target_pairs={{0,2},{8,14},{16,18},{24,30},{32,34},{40,46},{48,50},{56,62},{2,0}... | collective-permute-start | bytes 2162696 | tf_op jit(solution)/shard_map/ppermute | solution.py:79
  38.1 0.1 slice_add_fusion.4
  38.2 1.4 %collective-permute-start.8 = (f32[16,11,8,128]{3,2,1,0:T(8,128)S(1)}, f32[16,11,8,128]{3,2,1,0:T(8,128)S(1)}, u32[]{:S(2)}, u32[]{:S(2)}) collective-permute-start(f32[16,11,8,128]{3,2,1,0:T(8,128)S(1)} %get-tuple-element.74), channel_id=1, source_target_pairs={{0,48},{8,24},{16,32},{24,8},{32,16},{40,56},{48,0},{56,40},{2,50}... | collective-permute-start | bytes 2162696 | tf_op jit(solution)/shard_map/ppermute | solution.py:79
  39.7 0.2 slice_add_fusion.2
  39.9 0.1 slice_add_fusion.8
  40.0 2.6 %collective-permute-start.11 = (f32[16,10,8,128]{3,2,1,0:T(8,128)S(1)}, f32[16,10,8,128]{3,2,1,0:T(8,128)S(1)}, u32[]{:S(2)}, u32[]{:S(2)}) collective-permute-start(f32[16,10,8,128]{3,2,1,0:T(8,128)S(1)} %get-tuple-element.78), channel_id=1, source_target_pairs={{0,1},{8,73},{16,17},{24,89},{32,33},{40,105},{48,49},{56,121},{2,... | collective-permute-start | bytes 1966088 | tf_op jit(solution)/shard_map/ppermute | solution.py:79
  42.6 4.5 %collective-permute-done.5 = f32[16,11,8,128]{3,2,1,0:T(8,128)S(1)} collective-permute-done((f32[16,11,8,128]{3,2,1,0:T(8,128)S(1)}, f32[16,11,8,128]{3,2,1,0:T(8,128)S(1)}, u32[]{:S(2)}, u32[]{:S(2)}) %collective-permute-start.5) | collective-permute-done | bytes 720928 | tf_op jit(solution)/shard_map/ppermute | solution.py:79
  47.1 1.1 collective-permute-start.6
  48.3 0.5 collective-permute-done.8
  48.8 2.6 %collective-permute-start.9 = (f32[8,11,8,128]{3,2,1,0:T(8,128)S(1)}, f32[8,11,8,128]{3,2,1,0:T(8,128)S(1)}, u32[]{:S(2)}, u32[]{:S(2)}) collective-permute-start(f32[8,11,8,128]{3,2,1,0:T(8,128)S(1)} %get-tuple-element.79), channel_id=1, source_target_pairs={{0,1},{8,73},{16,17},{24,89},{32,33},{40,105},{48,49},{56,121},{2,... | collective-permute-start | bytes 1081352 | tf_op jit(solution)/shard_map/ppermute | solution.py:79
  51.5 2.3 %collective-permute-start.12 = (f32[8,10,8,128]{3,2,1,0:T(8,128)S(1)}, f32[8,10,8,128]{3,2,1,0:T(8,128)S(1)}, u32[]{:S(2)}, u32[]{:S(2)}) collective-permute-start(f32[8,10,8,128]{3,2,1,0:T(8,128)S(1)} %get-tuple-element.83), channel_id=1, source_target_pairs={{0,2},{8,14},{16,18},{24,30},{32,34},{40,46},{48,50},{56,62},{2,0}... | collective-permute-start | bytes 983048 | tf_op jit(solution)/shard_map/ppermute | solution.py:79
  53.7 5.0 %collective-permute-done.12.r2 = f32[8,10,8,128]{3,2,1,0:T(8,128)S(1)} collective-permute-done((f32[8,10,8,128]{3,2,1,0:T(8,128)S(1)}, f32[8,10,8,128]{3,2,1,0:T(8,128)S(1)}, u32[]{:S(2)}, u32[]{:S(2)}) %collective-permute-start.12) | collective-permute-done | bytes 327712 | tf_op jit(solution)/shard_map/ppermute | solution.py:79
  58.7 0.1 join.1
  58.8 14.3 %all_to_all.15.parts = f32[8,32,8,128]{3,2,1,0:T(8,128)S(1)} all-to-all(f32[8,32,8,128]{3,2,1,0:T(8,128)S(1)} %join.1), channel_id=1, replica_groups={{87,71,81,65,22,6,16,0},{119,103,113,97,54,38,48,32},{85,69,83,67,20,4,..., dimensions={0} | all-to-all | bytes 2097152 | tf_op jit(solution)/shard_map/all_to_all | solution.py:369
  73.2 16.7 %all_to_all.16.grad = f32[8,64,512]{2,1,0:T(8,128)S(1)} all-to-all(f32[8,64,512]{2,1,0:T(8,128)S(1)} %total.1), channel_id=1, replica_groups={{7,6,5,4,3,2,1,0},{15,14,13,12,11,10,9,8},{23,22,21,20,19,18,17,16},{31..., dimensions={0} | all-to-all | bytes 2097152 | tf_op jit(solution)/shard_map/all_to_all | solution.py:370
  90.0 3.5 %rows.1 = f32[8,64,512]{2,1,0:T(8,128)} custom-call(s32[21]{0:T(128)S(1)} %concatenate.3.table_ref, f32[8,64,512]{2,1,0:T(8,128)S(1)} %all_to_all.16.grad, f32[512,512]{1,0:T(8,128)S(1)} %get-tuple-element.54.lc, bf16[512,512]{1,0:T(8,128)(2,1)S(1)} %get-tuple-element.55.lkh, bf16[512,512]{1,0:T(8,128)(2,1)S(1)} %get-tuple-element.56.lkl, ...), custom_call_target="tpu_custom_call" | custom-call | tf_op jit(solution)/shard_map/rows/pallas_call | solution.py:264
  93.5 4.2 %all-to-all-start.2 = ((f32[8,64,512]{2,1,0:T(8,128)}), f32[8,64,512]{2,1,0:T(8,128)S(1)}, u32[]{:S(2)}, u32[]{:S(2)}) async-start(f32[8,64,512]{2,1,0:T(8,128)} %rows.1), calls=%async_computation.2 | async-start | bytes 2097152 | tf_op jit(solution)/shard_map/all_to_all | solution.py:372
  97.6 1.2 %copy-done.5 = f32[1,512,512]{2,1,0:T(8,128)S(1)} copy-done((f32[1,512,512]{2,1,0:T(8,128)S(1)}, f32[1,512,512]{2,1,0:T(8,128)}, u32[]{:S(2)}) %copy-start.5) | copy-done | bytes 1048600
  98.8 1.2 %copy-done.7 = f32[512,512]{1,0:T(8,128)S(1)} copy-done((f32[512,512]{1,0:T(8,128)S(1)}, f32[512,512]{1,0:T(8,128)}, u32[]{:S(2)}) %copy-start.7) | copy-done | bytes 1048600
  100.1 1.0 copy-done.9
  101.1 1.0 copy-done.11
  102.2 1.0 copy-done.13
  103.2 1.0 copy-done.15
  104.2 1.2 %copy-done.17 = f32[512,512]{1,0:T(8,128)S(1)} copy-done((f32[512,512]{1,0:T(8,128)S(1)}, f32[512,512]{1,0:T(8,128)}, u32[]{:S(2)}) %copy-start.17) | copy-done | bytes 1048600
  105.5 4.7 %stats.1 = (f32[1,512,512]{2,1,0:T(8,128)}, f32[1,512,512]{2,1,0:T(8,128)}, f32[1,512,512]{2,1,0:T(8,128)}, f32[1,512,512]{2,1,0:T(8,128)}) custom-call(f32[8,64,512]{2,1,0:T(8,128)S(1)} %all_to_all.16.grad, f32[512,512]{1,0:T(8,128)S(1)} %copy-done.7, bf16[512,512]{1,0:T(8,128)(2,1)S(1)} %copy-done.9, bf16[512,512]{1,0:T(8,128)(2,1)S(1)} %copy-done.11, ...), custom_call_target="tpu_custom_call" | custom-call | flops 3221225472 | bytes 11534336 | tf_op jit(solution)/shard_map/stats/pallas_call | solution.py:286
  110.2 4.5 %collective-permute-start.13 = (f32[8,64,512]{2,1,0:T(8,128)S(1)}, f32[8,64,512]{2,1,0:T(8,128)S(1)}, u32[]{:S(2)}, u32[]{:S(2)}) collective-permute-start(f32[8,64,512]{2,1,0:T(8,128)S(1)} %all-to-all-done.2.refs_0_), channel_id=1, source_target_pairs={{0,8},{8,0},{16,24},{24,16},{32,40},{40,32},{48,56},{56,48},{2,10}... | collective-permute-start | bytes 3145736 | tf_op jit(solution)/shard_map/ppermute | solution.py:79
  114.7 1.6 %spread.1.refs_1_ = f32[16,64,512]{2,1,0:T(8,128)} custom-call(s32[21]{0:T(128)S(1)} %concatenate.3.table_ref, f32[8,64,512]{2,1,0:T(8,128)S(1)} %all-to-all-done.2.refs_0_), custom_call_target="tpu_custom_call" | custom-call | tf_op jit(solution)/shard_map/spread/pallas_call | solution.py:313
  116.3 0.7 collective-permute-done.13.refs_0_
  117.0 1.6 %spread_late.1 = f32[16,64,512]{2,1,0:T(8,128)} custom-call(s32[21]{0:T(128)S(1)} %concatenate.3.table_ref, f32[8,64,512]{2,1,0:T(8,128)S(1)} %collective-permute-done.13.refs_0_, f32[16,64,512]{2,1,0:T(8,128)} %spread.1.refs_1_), custom_call_target="tpu_custom_call", output_to_operand_aliasing={{}: (2, {})} | custom-call | tf_op jit(solution)/shard_map/spread_late/pallas_call | solution.py:313
  (45 shorter events, 0.8 us)
Async XLA Ops:
  1.5 3.4 %copy-start = (bf16[1,16,512,512]{3,2,1,0:T(8,128)(2,1)S(1)}, bf16[1,16,512,512]{3,2,1,0:T(8,128)(2,1)}, u32[]{:S(2)}) copy-start(bf16[1,16,512,512]{3,2,1,0:T(8,128)(2,1)} %blocks.11) | copy-start | bytes 25165828
  6.0 9.1 %collective-permute-start = (f32[32,11,8,128]{3,2,1,0:T(8,128)S(1)}, f32[32,11,8,128]{3,2,1,0:T(8,128)S(1)}, u32[]{:S(2)}, u32[]{:S(2)}) collective-permute-start(f32[32,11,8,128]{3,2,1,0:T(8,128)S(1)} %other0.1), channel_id=1, source_target_pairs={{0,8},{8,0},{16,24},{24,16},{32,40},{40,32},{48,56},{56,48},{2,10}... | collective-permute-start | bytes 4325384 | tf_op jit(solution)/shard_map/ppermute | solution.py:79
  8.7 6.7 %collective-permute-start.1 = (f32[32,11,8,128]{3,2,1,0:T(8,128)S(1)}, f32[32,11,8,128]{3,2,1,0:T(8,128)S(1)}, u32[]{:S(2)}, u32[]{:S(2)}) collective-permute-start(f32[32,11,8,128]{3,2,1,0:T(8,128)S(1)} %other1.1), channel_id=1, source_target_pairs={{0,8},{8,0},{16,24},{24,16},{32,40},{40,32},{48,56},{56,48},{2,10}... | collective-permute-start | bytes 4325384 | tf_op jit(solution)/shard_map/ppermute | solution.py:79
  9.9 5.0 %collective-permute-start.2 = (f32[32,10,8,128]{3,2,1,0:T(8,128)S(1)}, f32[32,10,8,128]{3,2,1,0:T(8,128)S(1)}, u32[]{:S(2)}, u32[]{:S(2)}) collective-permute-start(f32[32,10,8,128]{3,2,1,0:T(8,128)S(1)} %other2.1), channel_id=1, source_target_pairs={{0,8},{8,0},{16,24},{24,16},{32,40},{40,32},{48,56},{56,48},{2,10}... | collective-permute-start | bytes 3932168 | tf_op jit(solution)/shard_map/ppermute | solution.py:79
  15.3 7.3 %copy-start.1 = (f32[1,512,512]{2,1,0:T(8,128)S(1)}, f32[1,512,512]{2,1,0:T(8,128)}, u32[]{:S(2)}) copy-start(f32[1,512,512]{2,1,0:T(8,128)} %rest_2_.1) | copy-start | bytes 3145732
  15.3 7.3 %copy-start.2 = (f32[1,512,512]{2,1,0:T(8,128)S(1)}, f32[1,512,512]{2,1,0:T(8,128)}, u32[]{:S(2)}) copy-start(f32[1,512,512]{2,1,0:T(8,128)} %rest_3_.1) | copy-start | bytes 3145732
  15.3 7.3 %copy-start.3 = (f32[1,512,512]{2,1,0:T(8,128)S(1)}, f32[1,512,512]{2,1,0:T(8,128)}, u32[]{:S(2)}) copy-start(f32[1,512,512]{2,1,0:T(8,128)} %ls.1) | copy-start | bytes 3145732
  15.3 7.3 %copy-start.4 = (f32[1,512,512]{2,1,0:T(8,128)S(1)}, f32[1,512,512]{2,1,0:T(8,128)}, u32[]{:S(2)}) copy-start(f32[1,512,512]{2,1,0:T(8,128)} %rs.1) | copy-start | bytes 3145732
  15.5 16.8 %collective-permute-start.3 = (f32[32,32,8,128]{3,2,1,0:T(8,128)S(1)}, f32[32,32,8,128]{3,2,1,0:T(8,128)S(1)}, u32[]{:S(2)}, u32[]{:S(2)}) collective-permute-start(f32[32,32,8,128]{3,2,1,0:T(8,128)S(1)} %otherkeep.1), channel_id=1, source_target_pairs={{0,8},{8,0},{16,24},{24,16},{32,40},{40,32},{48,56},{56,48},{2,10}... | collective-permute-start | bytes 12582920 | tf_op jit(solution)/shard_map/ppermute | solution.py:79
  15.6 19.4 %collective-permute-start.4 = (f32[32,11,8,128]{3,2,1,0:T(8,128)S(1)}, f32[32,11,8,128]{3,2,1,0:T(8,128)S(1)}, u32[]{:S(2)}, u32[]{:S(2)}) collective-permute-start(f32[32,11,8,128]{3,2,1,0:T(8,128)S(1)} %add.62), channel_id=1, source_target_pairs={{0,1},{8,73},{16,17},{24,89},{32,33},{40,105},{48,49},{56,121},{2,... | collective-permute-start | bytes 4325384 | tf_op jit(solution)/shard_map/ppermute | solution.py:79
  18.2 19.9 %collective-permute-start.7 = (f32[32,11,8,128]{3,2,1,0:T(8,128)S(1)}, f32[32,11,8,128]{3,2,1,0:T(8,128)S(1)}, u32[]{:S(2)}, u32[]{:S(2)}) collective-permute-start(f32[32,11,8,128]{3,2,1,0:T(8,128)S(1)} %add.63), channel_id=1, source_target_pairs={{0,2},{8,14},{16,18},{24,30},{32,34},{40,46},{48,50},{56,62},{2,0}... | collective-permute-start | bytes 4325384 | tf_op jit(solution)/shard_map/ppermute | solution.py:79
  21.0 18.9 %collective-permute-start.10 = (f32[32,10,8,128]{3,2,1,0:T(8,128)S(1)}, f32[32,10,8,128]{3,2,1,0:T(8,128)S(1)}, u32[]{:S(2)}, u32[]{:S(2)}) collective-permute-start(f32[32,10,8,128]{3,2,1,0:T(8,128)S(1)} %add.64), channel_id=1, source_target_pairs={{0,48},{8,24},{16,32},{24,8},{32,16},{40,56},{48,0},{56,40},{2,50}... | collective-permute-start | bytes 3932168 | tf_op jit(solution)/shard_map/ppermute | solution.py:79
  32.3 1.0 copy-start.16
  32.3 57.7 %copy-start.6 = (f32[512,512]{1,0:T(8,128)}, f32[512,512]{1,0:T(8,128)S(1)}, u32[]{:S(2)}) copy-start(f32[512,512]{1,0:T(8,128)S(1)} %get-tuple-element.54.lc) | copy-start | bytes 3145732
  32.3 57.7 %copy-start.8 = (bf16[512,512]{1,0:T(8,128)(2,1)}, bf16[512,512]{1,0:T(8,128)(2,1)S(1)}, u32[]{:S(2)}) copy-start(bf16[512,512]{1,0:T(8,128)(2,1)S(1)} %get-tuple-element.55.lkh) | copy-start | bytes 1572868
  32.3 57.7 %copy-start.10 = (bf16[512,512]{1,0:T(8,128)(2,1)}, bf16[512,512]{1,0:T(8,128)(2,1)S(1)}, u32[]{:S(2)}) copy-start(bf16[512,512]{1,0:T(8,128)(2,1)S(1)} %get-tuple-element.56.lkl) | copy-start | bytes 1572868
  32.3 57.7 %copy-start.12 = (bf16[512,512]{1,0:T(8,128)(2,1)}, bf16[512,512]{1,0:T(8,128)(2,1)S(1)}, u32[]{:S(2)}) copy-start(bf16[512,512]{1,0:T(8,128)(2,1)S(1)} %get-tuple-element.57.rkh) | copy-start | bytes 1572868
  32.3 57.7 %copy-start.14 = (bf16[512,512]{1,0:T(8,128)(2,1)}, bf16[512,512]{1,0:T(8,128)(2,1)S(1)}, u32[]{:S(2)}) copy-start(bf16[512,512]{1,0:T(8,128)(2,1)S(1)} %get-tuple-element.58.rkl) | copy-start | bytes 1572868
  35.2 11.9 %collective-permute-start.5 = (f32[16,11,8,128]{3,2,1,0:T(8,128)S(1)}, f32[16,11,8,128]{3,2,1,0:T(8,128)S(1)}, u32[]{:S(2)}, u32[]{:S(2)}) collective-permute-start(f32[16,11,8,128]{3,2,1,0:T(8,128)S(1)} %get-tuple-element.76), channel_id=1, source_target_pairs={{0,2},{8,14},{16,18},{24,30},{32,34},{40,46},{48,50},{56,62},{2,0}... | collective-permute-start | bytes 2162696 | tf_op jit(solution)/shard_map/ppermute | solution.py:79
  38.2 10.5 %collective-permute-start.8 = (f32[16,11,8,128]{3,2,1,0:T(8,128)S(1)}, f32[16,11,8,128]{3,2,1,0:T(8,128)S(1)}, u32[]{:S(2)}, u32[]{:S(2)}) collective-permute-start(f32[16,11,8,128]{3,2,1,0:T(8,128)S(1)} %get-tuple-element.74), channel_id=1, source_target_pairs={{0,48},{8,24},{16,32},{24,8},{32,16},{40,56},{48,0},{56,40},{2,50}... | collective-permute-start | bytes 2162696 | tf_op jit(solution)/shard_map/ppermute | solution.py:79
  40.0 11.4 %collective-permute-start.11 = (f32[16,10,8,128]{3,2,1,0:T(8,128)S(1)}, f32[16,10,8,128]{3,2,1,0:T(8,128)S(1)}, u32[]{:S(2)}, u32[]{:S(2)}) collective-permute-start(f32[16,10,8,128]{3,2,1,0:T(8,128)S(1)} %get-tuple-element.78), channel_id=1, source_target_pairs={{0,1},{8,73},{16,17},{24,89},{32,33},{40,105},{48,49},{56,121},{2,... | collective-permute-start | bytes 1966088 | tf_op jit(solution)/shard_map/ppermute | solution.py:79
  47.1 11.5 %collective-permute-start.6 = (f32[8,11,8,128]{3,2,1,0:T(8,128)S(1)}, f32[8,11,8,128]{3,2,1,0:T(8,128)S(1)}, u32[]{:S(2)}, u32[]{:S(2)}) collective-permute-start(f32[8,11,8,128]{3,2,1,0:T(8,128)S(1)} %get-tuple-element.81), channel_id=1, source_target_pairs={{0,48},{8,24},{16,32},{24,8},{32,16},{40,56},{48,0},{56,40},{2,50}... | collective-permute-start | bytes 1081352 | tf_op jit(solution)/shard_map/ppermute | solution.py:79
  48.8 9.9 %collective-permute-start.9 = (f32[8,11,8,128]{3,2,1,0:T(8,128)S(1)}, f32[8,11,8,128]{3,2,1,0:T(8,128)S(1)}, u32[]{:S(2)}, u32[]{:S(2)}) collective-permute-start(f32[8,11,8,128]{3,2,1,0:T(8,128)S(1)} %get-tuple-element.79), channel_id=1, source_target_pairs={{0,1},{8,73},{16,17},{24,89},{32,33},{40,105},{48,49},{56,121},{2,... | collective-permute-start | bytes 1081352 | tf_op jit(solution)/shard_map/ppermute | solution.py:79
  51.5 7.2 %collective-permute-start.12 = (f32[8,10,8,128]{3,2,1,0:T(8,128)S(1)}, f32[8,10,8,128]{3,2,1,0:T(8,128)S(1)}, u32[]{:S(2)}, u32[]{:S(2)}) collective-permute-start(f32[8,10,8,128]{3,2,1,0:T(8,128)S(1)} %get-tuple-element.83), channel_id=1, source_target_pairs={{0,2},{8,14},{16,18},{24,30},{32,34},{40,46},{48,50},{56,62},{2,0}... | collective-permute-start | bytes 983048 | tf_op jit(solution)/shard_map/ppermute | solution.py:79
  93.5 16.7 %all-to-all-start.2 = ((f32[8,64,512]{2,1,0:T(8,128)}), f32[8,64,512]{2,1,0:T(8,128)S(1)}, u32[]{:S(2)}, u32[]{:S(2)}) async-start(f32[8,64,512]{2,1,0:T(8,128)} %rows.1), calls=%async_computation.2 | async-start | bytes 2097152 | tf_op jit(solution)/shard_map/all_to_all | solution.py:372
  97.6 1.2 %copy-start.5 = (f32[1,512,512]{2,1,0:T(8,128)S(1)}, f32[1,512,512]{2,1,0:T(8,128)}, u32[]{:S(2)}) copy-start(f32[1,512,512]{2,1,0:T(8,128)} %rs.1) | copy-start | bytes 3145732
  98.8 1.2 %copy-start.7 = (f32[512,512]{1,0:T(8,128)S(1)}, f32[512,512]{1,0:T(8,128)}, u32[]{:S(2)}) copy-start(f32[512,512]{1,0:T(8,128)} %copy-done.6) | copy-start | bytes 3145732
  100.1 1.0 copy-start.9
  101.1 1.0 copy-start.11
  102.2 1.0 copy-start.13
  103.2 1.0 copy-start.15
  104.2 1.2 %copy-start.17 = (f32[512,512]{1,0:T(8,128)S(1)}, f32[512,512]{1,0:T(8,128)}, u32[]{:S(2)}) copy-start(f32[512,512]{1,0:T(8,128)} %copy-done.16) | copy-start | bytes 3145732
  110.2 6.8 %collective-permute-start.13 = (f32[8,64,512]{2,1,0:T(8,128)S(1)}, f32[8,64,512]{2,1,0:T(8,128)S(1)}, u32[]{:S(2)}, u32[]{:S(2)}) collective-permute-start(f32[8,64,512]{2,1,0:T(8,128)S(1)} %all-to-all-done.2.refs_0_), channel_id=1, source_target_pairs={{0,8},{8,0},{16,24},{24,16},{32,40},{40,32},{48,56},{56,48},{2,10}... | collective-permute-start | bytes 3145736 | tf_op jit(solution)/shard_map/ppermute | solution.py:79
